TPU v7x, 32 devices: a whole 2x2x4 slice. The times are simulated.
32 devices in a mesh: ctx: 8 (over y, x, core), head: 4 (over z).
Axes of the slice: x: 2, y: 2, z: 4, core: 2. Of those that a mesh axis runs over, the one named last changes fastest.
Arguments:
- light_query: bfloat16 [16384, 2048], P(('ctx', 'head')), may hold values from -6 to 6
- light_key: bfloat16 [16384, 2048], P(('ctx', 'head')), may hold values from -6 to 6
- light_value: bfloat16 [16384, 2048], P(('ctx', 'head')), may hold values from -6 to 6
- soft_query: bfloat16 [16384, 2048], P(('ctx', 'head')), may hold values from -52 to 52
- soft_key: bfloat16 [16384, 2048], P(('ctx', 'head')), may hold values from -6 to 6
- upstream: bfloat16 [16384, 2048], P(('ctx', 'head')), may hold values from -6 to 6
- decays: bfloat16 [16384, 32], P(('ctx', 'head')), may hold values from 0 to 1
- block_mask: int32 [128, 16], P('ctx'), may hold values from 0 to 1, as said below
Outputs:
- grad_light_query: bfloat16 [16384, 2048], P(('ctx', 'head'))
- grad_light_key: bfloat16 [16384, 2048], P(('ctx', 'head'))
- grad_light_value: bfloat16 [16384, 2048], P(('ctx', 'head'))
Inputs may be any that keep to these rules, and one draw needn't show every extreme that they name: `block_mask`: in each query block, the flag of its own block within the span is 1 and flags of later blocks are 0; earlier blocks are 0 or 1.
All inputs are finite; a program needn't handle non-finite values.
Results may differ from a plain program's by a relative error of at most 0.0057.
Values may be sent and summed in bfloat16 or wider, within the bound.
No kernel may reach another device: no remote copies, remote signals or barrier semaphores. Data moves between devices by JAX's collectives and lax.ppermute only.
A program may use at most 128 MiB of HBM per device.

v0:
```python
import functools
import math

import jax
import jax.numpy as jnp
from jax import lax
from jax.experimental import pallas as pl
from jax.experimental.pallas import tpu as pltpu
from jax.sharding import PartitionSpec as P


BLOCK = 128
BF = jnp.bfloat16
F32 = jnp.float32
NEG = -1e30
AXES = ("ctx", "head")


def mm(a, b, ca, cb):
    return lax.dot_general(a, b, (((ca,), (cb,)), ((), ())), preferred_element_type=F32)


def params(megabytes=48):
    return pltpu.CompilerParams(vmem_limit_bytes=megabytes * 2**20)


def lane_masks(width):
    lane = lax.broadcasted_iota(jnp.int32, (1, width), 1)
    left = (lane < width // 2).astype(F32).astype(BF)
    right = (lane >= width // 2).astype(F32).astype(BF)
    return left, right


def split_pair(x):
    left, right = lane_masks(x.shape[1])
    return jnp.concatenate([x * left, x * right], axis=0)


def pack_kernel(count, _, *refs):
    ins, outs = refs[: 3 * count], refs[3 * count :]
    for k in range(count):
        for n in range(3):
            outs[k][n] = ins[3 * k + n][...]


def pack(here, arrays, chunk, count, width):
    rows = arrays[0].shape[0]

    def spec(k):
        return pl.BlockSpec(
            (rows, width), lambda i, z: (0, chunk * count + lax.rem(z[0] + k, count))
        )

    return pl.pallas_call(
        functools.partial(pack_kernel, count),
        out_shape=[jax.ShapeDtypeStruct((3, rows, width), BF)] * count,
        grid_spec=pltpu.PrefetchScalarGridSpec(
            num_scalar_prefetch=1,
            grid=(1,),
            in_specs=[spec(k) for k in range(count) for _ in range(3)],
            out_specs=[pl.BlockSpec((3, rows, width), lambda i, z: (0, 0, 0))] * count,
        ),
        compiler_params=params(),
        cost_estimate=pl.CostEstimate(
            flops=0, transcendentals=0, bytes_accessed=12 * count * rows * width
        ),
        name="pack",
    )(here, *(array for _ in range(count) for array in arrays))


def soft_kernel(count, root, z_ref, flags, *refs):
    ins = refs[:count]
    outs = refs[count : 2 * count]
    queries, keys, cotans, scores, tops, summed, listed = refs[2 * count :]
    rows, width = ins[0].shape[1:]
    z = z_ref[0]
    pairs = width // BLOCK
    groups = BLOCK // 8
    wide = 2 * BLOCK
    for k in range(count):
        owner = lax.rem(z - k + count, count)
        at = pl.ds(pl.multiple_of(owner * rows, rows), rows)
        queries[at, :] = ins[k][0] * jnp.asarray(root, BF)
        keys[at, :] = ins[k][1]
        cotans[at, :] = ins[k][2]
    summed[...] = jnp.zeros_like(summed)

    def rows_of(j):
        return pl.ds(pl.multiple_of(j * BLOCK, BLOCK), BLOCK)

    def lanes_of(p):
        return slice(p * BLOCK, (p + 1) * BLOCK)

    def query_block(i, _):
        query = [split_pair(queries[rows_of(i), lanes_of(p)]) for p in range(pairs)]
        cotan = [split_pair(cotans[rows_of(i), lanes_of(p)]) for p in range(pairs)]

        def collect(j, found):
            listed[found] = j
            return found + flags[i, j]

        listed[0] = i
        found = lax.fori_loop(0, i, collect, 1)
        key_at = lax.broadcasted_iota(jnp.int32, (BLOCK, wide), 0)
        query_at = lax.rem(lax.broadcasted_iota(jnp.int32, (BLOCK, wide), 1), BLOCK)

        def absorb(slots, p, blocks, top, total):
            newer = top
            for block in blocks:
                newer = jnp.maximum(newer, jnp.max(block, axis=0))
            total = total * jnp.exp(top - newer)
            for n, block in zip(slots, blocks):
                block = jnp.exp(block - newer[None])
                scores[p, n] = block
                tops[p, n] = newer
                total = total + jnp.sum(block, axis=0)
            return newer, total

        def raw(n, p):
            block = mm(keys[rows_of(listed[n]), lanes_of(p)], query[p], 1, 1)
            return block.reshape(groups, 8, wide)

        held = []
        for p in range(pairs):
            own = mm(keys[rows_of(i), lanes_of(p)], query[p], 1, 1)
            own = jnp.where(key_at <= query_at, own, NEG).reshape(groups, 8, wide)
            floor = jnp.full((8, wide), NEG, F32)
            held.append(absorb((0,), p, (own,), floor, jnp.zeros((8, wide), F32)))

        def first(unroll, start):
            def step(n, held):
                slots = [start + unroll * n + m for m in range(unroll)]
                blocks = [[raw(n, p) for n in slots] for p in range(pairs)]
                return tuple(absorb(slots, p, blocks[p], *held[p]) for p in range(pairs))

            return step

        twice = (found - 1) // 2
        held = lax.fori_loop(0, twice, first(2, 1), tuple(held))
        held = lax.fori_loop(2 * twice, found - 1, first(1, 1), held)
        highest, share = [], []
        for top, total in held:
            most = jnp.max(top, axis=0, keepdims=True)
            total = jnp.sum(total * jnp.exp(top - most), axis=0, keepdims=True)
            highest.append(most)
            share.append(1.0 / total)

        def second(unroll):
            def step(n, _):
                slots = [unroll * n + m for m in range(unroll)]
                parts = []
                for n in slots:
                    for p in range(pairs):
                        factor = jnp.exp(tops[p, n] - highest[p]) * share[p]
                        block = (scores[p, n] * factor[None]).reshape(BLOCK, wide).astype(BF)
                        parts.append((n, p, mm(block, cotan[p], 1, 0)))
                for n, p, part in parts:
                    summed[rows_of(listed[n]), lanes_of(p)] += part
                return 0

            return step

        twice = found // 2
        lax.fori_loop(0, twice, second(2), 0)
        lax.fori_loop(2 * twice, found, second(1), 0)
        return 0

    lax.fori_loop(0, count * (rows // BLOCK), query_block, 0)
    for k in range(count):
        owner = lax.rem(z + k, count)
        at = pl.ds(pl.multiple_of(owner * rows, rows), rows)
        outs[k][...] = summed[at, :].astype(BF)


def soft(here, flags, pieces, root):
    count = len(pieces)
    rows, width = pieces[0].shape[1:]
    span = count * rows
    vmem = pl.BlockSpec(memory_space=pltpu.VMEM)
    smem = pl.BlockSpec(memory_space=pltpu.SMEM)
    return pl.pallas_call(
        functools.partial(soft_kernel, count, root),
        out_shape=[jax.ShapeDtypeStruct((rows, width), BF)] * count,
        in_specs=[smem, smem] + [vmem] * count,
        out_specs=[vmem] * count,
        scratch_shapes=[
            pltpu.VMEM((span, width), BF),
            pltpu.VMEM((span, width), BF),
            pltpu.VMEM((span, width), BF),
            pltpu.VMEM((width // BLOCK, span // BLOCK, BLOCK // 8, 8, 2 * BLOCK), F32),
            pltpu.VMEM((width // BLOCK, span // BLOCK, 8, 2 * BLOCK), F32),
            pltpu.VMEM((span, width), F32),
            pltpu.SMEM((span // BLOCK + 1,), jnp.int32),
        ],
        compiler_params=params(),
        cost_estimate=pl.CostEstimate(
            flops=4 * span * span * width, transcendentals=span * span, bytes_accessed=8 * span * width
        ),
        name="soft",
    )(here, flags, *pieces)


def triangle():
    row = lax.broadcasted_iota(jnp.int32, (BLOCK, BLOCK), 0)
    column = lax.broadcasted_iota(jnp.int32, (BLOCK, BLOCK), 1)
    return row >= column


def spread_decays(decays, first, width, each):
    heads = decays.shape[1]
    head = lax.broadcasted_iota(jnp.int32, (heads, width), 0)
    lane = lax.broadcasted_iota(jnp.int32, (heads, width), 1)
    spread = (head == first + lane // each).astype(F32).astype(BF)
    return mm(decays, spread, 1, 0).astype(BF)


def device_levels(decays, first, width):
    wide = spread_decays(decays, first, width, BLOCK // 2)
    lower = triangle().astype(F32).astype(BF)
    before = jnp.zeros((1, width), F32)
    levels = []
    for b in range(decays.shape[0] // BLOCK):
        level = mm(lower, wide[b * BLOCK : (b + 1) * BLOCK], 1, 0)
        levels.append(level + before)
        before = before + level[BLOCK - 1 :]
    return jnp.concatenate(levels, axis=0), before


def by_lane(first, second):
    lane = lax.broadcasted_iota(jnp.int32, first.shape, 1)
    return jnp.where(lane < BLOCK // 2, first, second)


def on_diagonal(x):
    row = lax.broadcasted_iota(jnp.int32, x.shape, 0)
    lane = lax.broadcasted_iota(jnp.int32, x.shape, 1)
    half = BLOCK // 2
    return jnp.where((row < half) == (lane < half), x, 0.0)


def fold(x):
    return x[: BLOCK // 2] + x[BLOCK // 2 :]


def state_kernel(q_ref, k_ref, v_ref, d_ref, sum_ref, total_ref, scaled_ref):
    level, last = device_levels(d_ref[...], 2 * pl.program_id(0), BLOCK)
    key = (k_ref[...].astype(F32) * jnp.exp(level - last)).astype(BF)
    sum_ref[0] = fold(on_diagonal(mm(key, v_ref[...], 0, 0))).astype(BF)
    total_ref[0] = jnp.broadcast_to(last, total_ref.shape[1:])
    scaled_ref[...] = (q_ref[...].astype(F32) * jnp.exp(-level)).astype(BF)


def device_state(light_query, light_key, light_value, decays, pairs):
    rows = light_key.shape[0]
    block = pl.BlockSpec((rows, BLOCK), lambda p: (0, p))
    return pl.pallas_call(
        state_kernel,
        out_shape=[
            jax.ShapeDtypeStruct((pairs, BLOCK // 2, BLOCK), BF),
            jax.ShapeDtypeStruct((pairs, 8, BLOCK), F32),
            jax.ShapeDtypeStruct(light_query.shape, BF),
        ],
        grid=(pairs,),
        in_specs=[block, block, block, pl.BlockSpec(decays.shape, lambda p: (0, 0))],
        out_specs=[
            pl.BlockSpec((1, BLOCK // 2, BLOCK), lambda p: (p, 0, 0)),
            pl.BlockSpec((1, 8, BLOCK), lambda p: (p, 0, 0)),
            block,
        ],
        compiler_params=params(),
        cost_estimate=pl.CostEstimate(
            flops=8 * rows * pairs * BLOCK * BLOCK, transcendentals=rows * pairs * BLOCK, bytes_accessed=8 * rows * pairs * BLOCK
        ),
        name="state",
    )(light_query, light_key, light_value, decays)


def take_lit(count, z, lits, held):
    @pl.when(pl.program_id(0) == 0)
    def _():
        per = lits[0].shape[1] // BLOCK
        for k in range(count):
            owner = lax.rem(z - k + count, count)
            for p in range(per):
                held[owner * per + p] = lits[k][:, p * BLOCK : (p + 1) * BLOCK]


def reach_kernel(count, z_ref, q_ref, *refs):
    lits, sum_ref = refs[:count], refs[count]
    _, width = lits[0].shape
    per = width // BLOCK
    for k in range(count):
        owner = lax.rem(z_ref[0] - k + count, count)
        for p in range(per):
            at = pl.ds(pl.multiple_of((owner * per + p) * BLOCK, BLOCK), BLOCK)
            product = mm(q_ref[:, at], lits[k][:, p * BLOCK : (p + 1) * BLOCK], 0, 0)
            sum_ref[owner * per + p] = fold(on_diagonal(product)).astype(BF)


def device_reach(here, scaled, lits, chunk):
    count = len(lits)
    rows, width = lits[0].shape
    pairs = count * width // BLOCK
    return pl.pallas_call(
        functools.partial(reach_kernel, count),
        out_shape=jax.ShapeDtypeStruct((pairs, BLOCK // 2, BLOCK), BF),
        grid_spec=pltpu.PrefetchScalarGridSpec(
            num_scalar_prefetch=1,
            grid=(1,),
            in_specs=[pl.BlockSpec((rows, count * width), lambda p, z: (0, chunk))]
            + [pl.BlockSpec((rows, width), lambda p, z: (0, 0))] * count,
            out_specs=pl.BlockSpec((pairs, BLOCK // 2, BLOCK), lambda p, z: (0, 0, 0)),
        ),
        compiler_params=params(),
        cost_estimate=pl.CostEstimate(
            flops=2 * rows * pairs * BLOCK * BLOCK, transcendentals=0, bytes_accessed=4 * rows * pairs * BLOCK
        ),
        name="reach",
    )(here, scaled, *lits)


def chain_kernel(x_ref, a_ref, o_ref):
    count, half = x_ref.shape[0], x_ref.shape[1] // 2
    zero = jnp.zeros((half, x_ref.shape[2]), F32)

    def step(n, carried):
        early, late = carried
        m = count - 1 - n
        o_ref[n, :half, :] = early.astype(BF)
        o_ref[m, half:, :] = late.astype(BF)
        early = a_ref[n] * early + x_ref[n, :half, :].astype(F32)
        late = a_ref[m] * late + x_ref[m, half:, :].astype(F32)
        return early, late

    lax.fori_loop(0, count, step, (zero, zero))


def chain(items, totals):
    vmem = pl.BlockSpec(memory_space=pltpu.VMEM)
    return pl.pallas_call(
        chain_kernel,
        out_shape=jax.ShapeDtypeStruct(items.shape, BF),
        in_specs=[vmem, vmem],
        out_specs=vmem,
        compiler_params=params(),
        cost_estimate=pl.CostEstimate(flops=2 * items.size, transcendentals=0, bytes_accessed=8 * items.size),
        name="chain",
    )(items, totals)


def local_kernel(count, first_pair, skip, olds, z_ref, q_ref, k_ref, v_ref, d_ref, t_ref, *refs):
    lits = refs[:count]
    gq_ref, gk_ref, gv_ref, lit_ref, held = refs[count + olds :]
    take_lit(count, z_ref[0], lits, held)
    here = pl.program_id(0)
    blocks = q_ref.shape[0] // BLOCK
    shape = (BLOCK, BLOCK)
    row_at = lax.broadcasted_iota(jnp.int32, shape, 0)
    lane_at = lax.broadcasted_iota(jnp.int32, shape, 1)
    lower, upper = row_at >= lane_at, row_at <= lane_at
    ones_lower, ones_upper = (side.astype(F32).astype(BF) for side in (lower, upper))
    slot = skip + here
    spread = spread_decays(d_ref[...], 2 * (first_pair + slot), 2 * BLOCK, BLOCK)
    lines = t_ref[0].astype(BF)
    lit_ref[...] = held[slot]
    state = None
    kept = []
    for b in range(blocks):
        at = slice(b * BLOCK, (b + 1) * BLOCK)
        query, key, value, lit = (q_ref[at, :], k_ref[at, :], v_ref[at, :], held[slot, at, :])
        levels = mm(ones_lower, spread[at], 1, 0)
        lined = mm(lines[:, at], ones_upper, 1, 0)
        columns = (levels[:, :BLOCK], levels[:, BLOCK:])
        level = by_lane(*columns)
        last = level[BLOCK - 1 :]
        entries = jnp.exp(-level)
        leaving = jnp.exp(level - last)
        decay = jnp.exp(-last)
        spans = [lined[4 * n : 4 * n + 1] - columns[n] for n in range(2)]
        weights = jnp.concatenate(
            [jnp.where(lower, jnp.exp(jnp.minimum(span, 0.0)), 0.0) for span in spans], axis=1
        )
        turned = jnp.concatenate(
            [jnp.where(upper, jnp.exp(jnp.minimum(-span, 0.0)), 0.0) for span in spans], axis=1
        )
        queries, keys, values, twice = (split_pair(query), split_pair(key), split_pair(value), split_pair(lit))
        back = (mm(lit, values, 1, 1) * weights).astype(BF)
        back_turned = (mm(value, twice, 1, 1) * turned).astype(BF)
        mixed_turned = (mm(key, queries, 1, 1) * turned).astype(BF)
        grad_query = mm(back, keys, 1, 0)
        if state is not None:
            grad_query = grad_query + entries * mm(lit, state.astype(BF), 1, 1)
        gq_ref[at, :] = grad_query
        grad_key = mm(back_turned, queries, 1, 0)
        grad_value = mm(mixed_turned, twice, 1, 0)
        kept.append((grad_key, grad_value, entries, leaving, decay))
        if b < blocks - 1:
            left = (key.astype(F32) * leaving).astype(BF)
            left = on_diagonal(mm(left, value, 0, 0))
            state = left if state is None else decay * state + left
    state = None
    for b in reversed(range(blocks)):
        at = slice(b * BLOCK, (b + 1) * BLOCK)
        grad_key, grad_value, entries, leaving, decay = kept[b]
        if state is not None:
            low = state.astype(BF)
            grad_key = grad_key + leaving * mm(v_ref[at, :], low, 1, 1)
            grad_value = grad_value + leaving * mm(k_ref[at, :], low, 1, 0)
        gk_ref[at, :] = grad_key
        gv_ref[at, :] = grad_value
        if b > 0:
            query = (q_ref[at, :].astype(F32) * entries).astype(BF)
            query = on_diagonal(mm(query, held[slot, at, :], 0, 0))
            state = query if state is None else decay * state + query


def local(here, light_query, light_key, light_value, decays, lines, lits, first, skip, many, olds):
    count = len(lits)
    rows, columns = light_query.shape
    width = lits[0].shape[1]
    pairs = count * width // BLOCK
    block = pl.BlockSpec((rows, BLOCK), lambda p, z: (0, first + skip + p))
    base = 6 + count
    return pl.pallas_call(
        functools.partial(local_kernel, count, first, skip, len(olds)),
        out_shape=[jax.ShapeDtypeStruct((rows, columns), F32)] * 3 + [jax.ShapeDtypeStruct((rows, columns), BF)],
        grid_spec=pltpu.PrefetchScalarGridSpec(
            num_scalar_prefetch=1,
            grid=(many,),
            in_specs=[
                block,
                block,
                block,
                pl.BlockSpec(decays.shape, lambda p, z: (0, 0)),
                pl.BlockSpec((1, 8, rows), lambda p, z: (first + skip + p, 0, 0)),
            ]
            + [pl.BlockSpec((rows, width), lambda p, z: (0, 0))] * count
            + [pl.BlockSpec(memory_space=pl.ANY)] * len(olds),
            out_specs=[block] * 4,
            scratch_shapes=[pltpu.VMEM((pairs, rows, BLOCK), BF)],
        ),
        input_output_aliases={base + n: n for n in range(len(olds))},
        compiler_params=params(),
        cost_estimate=pl.CostEstimate(
            flops=40 * rows * many * BLOCK * BLOCK, transcendentals=4 * rows * many * BLOCK, bytes_accessed=22 * rows * many * BLOCK
        ),
        name="local",
    )(here, light_query, light_key, light_value, decays, lines, *lits, *olds)


def wide_state(x):
    pairs = x.shape[0]
    width = pairs * BLOCK
    x = jnp.concatenate([x[p] for p in range(pairs)], axis=1)
    x = jnp.concatenate([x] * (2 * pairs), axis=0)
    half = BLOCK // 2
    row = lax.broadcasted_iota(jnp.int32, (width, width), 0) // half
    lane = lax.broadcasted_iota(jnp.int32, (width, width), 1) // half
    return x * (row == lane).astype(F32).astype(BF)


def final_kernel(scale, pq_ref, pk_ref, pv_ref, lit_ref, k_ref, v_ref, d_ref, s_ref, r_ref, gq_ref, gk_ref, gv_ref):
    pairs = s_ref.shape[0]
    width = pairs * BLOCK
    level, last = device_levels(d_ref[...], 2 * pairs * pl.program_id(0), width)
    entries = scale * jnp.exp(-level)
    leaving = scale * jnp.exp(level - last)
    state, reach = wide_state(s_ref[...]), wide_state(r_ref[...])
    gq_ref[...] = (scale * pq_ref[...] + entries * mm(lit_ref[...], state, 1, 1)).astype(BF)
    gk_ref[...] = (scale * pk_ref[...] + leaving * mm(v_ref[...], reach, 1, 1)).astype(BF)
    gv_ref[...] = (scale * pv_ref[...] + leaving * mm(k_ref[...], reach, 1, 0)).astype(BF)


def final(parts, light_key, light_value, decays, state_in, reach_in, scale):
    rows, columns = light_key.shape
    pairs = columns // BLOCK
    step = 2 if pairs % 2 == 0 else 1
    block = pl.BlockSpec((rows, step * BLOCK), lambda p: (0, p))
    small = pl.BlockSpec((step, BLOCK // 2, BLOCK), lambda p: (p, 0, 0))
    return pl.pallas_call(
        functools.partial(final_kernel, scale),
        out_shape=[jax.ShapeDtypeStruct((rows, columns), BF)] * 3,
        grid=(pairs // step,),
        in_specs=[block] * 6 + [pl.BlockSpec(decays.shape, lambda p: (0, 0)), small, small],
        out_specs=[block] * 3,
        compiler_params=params(),
        cost_estimate=pl.CostEstimate(
            flops=6 * rows * columns * BLOCK, transcendentals=2 * rows * columns, bytes_accessed=24 * rows * columns
        ),
        name="final",
    )(*parts, light_key, light_value, decays, state_in, reach_in)


def turn(pieces, count):
    return [pieces[0]] + [
        lax.ppermute(pieces[k], "head", [(i, (i + k) % count) for i in range(count)])
        for k in range(1, count)
    ]


def program(light_query, light_key, light_value, soft_query, soft_key, upstream, decays, block_mask):
    count, spans = lax.axis_size("head"), lax.axis_size("ctx")
    devices = count * spans
    rows, columns = light_query.shape
    heads = decays.shape[1]
    head_width = columns // heads
    pairs = heads // 2
    share = pairs // count
    chunks = 2 if share % 2 == 0 else 1
    per = share // chunks
    assert 2 * head_width == BLOCK and share * count == pairs
    part = count * per * head_width // devices
    again = head_width // part
    assert part * again == head_width
    scale = 1.0 / (head_width * math.sqrt(head_width))
    root = 1.0 / math.sqrt(head_width)
    here = lax.axis_index("head").astype(jnp.int32).reshape(1)

    packed = []
    for c in range(chunks):
        pieces = pack(here, (soft_query, soft_key, upstream), c, count, per * BLOCK)
        packed.append(turn(pieces, count))
    sums, totals, scaled = device_state(light_query, light_key, light_value, decays, pairs)
    lines = jnp.repeat(decays.T.astype(F32).reshape(pairs, 2, rows), 4, axis=1)

    parts, reaches = (), []
    for c in range(chunks):
        lits = soft(here, block_mask, packed[c], root)
        lits = turn(lits, count)
        reaches.append(device_reach(here, scaled, lits, c))
        first, many = c * count * per, count * per
        cuts = (0, many // 2, many) if c == chunks - 1 else (0, many)
        for n in range(len(cuts) - 1):
            parts = local(
                here, light_query, light_key, light_value, decays, lines, lits, first,
                cuts[n], cuts[n + 1] - cuts[n], tuple(parts),
            )

    def exchange(x):
        return lax.all_to_all(x, AXES, split_axis=0, concat_axis=0, tiled=True)

    def spread(x):
        x = x.reshape(chunks, devices, part, BLOCK)
        return jnp.swapaxes(x, 0, 1).reshape(devices, chunks * part, BLOCK)

    def gather(x):
        x = x.reshape(devices, chunks, part, BLOCK)
        return jnp.swapaxes(x, 0, 1).reshape(pairs, head_width, BLOCK)

    rates = jnp.swapaxes(totals[:, 0].reshape(chunks, count * per, BLOCK), 0, 1)
    rates = jnp.repeat(rates, again, axis=0)
    thirds = []
    for _ in range(3):
        thirds.append(lax.reduce_precision(rates, 8, 7))
        rates = rates - thirds[-1]
    thirds = jnp.stack(thirds, axis=1).reshape(devices, 3 * chunks, BLOCK).astype(BF)
    half = chunks * part
    fill = jnp.zeros((devices, -(2 * half + 3 * chunks) % 8, BLOCK), BF)
    sends = [spread(sums), spread(jnp.concatenate(reaches, axis=0)), thirds, fill]
    got = exchange(jnp.concatenate(sends, axis=1))
    thirds = got[:, 2 * half : 2 * half + 3 * chunks].astype(F32).reshape(devices, 3, chunks, BLOCK)
    rates = jnp.exp(-(thirds[:, 0] + thirds[:, 1] + thirds[:, 2]))
    rates = jnp.repeat(rates, part, axis=1)
    given = chain(got[:, : 2 * half], rates)
    given = exchange(given)
    return tuple(
        final(parts, light_key, light_value, decays, gather(given[:, :half]), gather(given[:, half:]), scale)
    )


def solution(mesh):
    rows = P(AXES, None)
    return jax.shard_map(
        program,
        mesh=mesh,
        in_specs=(rows,) * 7 + (P("ctx", None),),
        out_specs=(rows,) * 3,
        check_vma=False,
    )
```

profile of v0, /device:TPU:0, one launch (start us, length us, event | category | flops | bytes accessed | tf_op | source)
XLA Modules:
  0.0 293.7 jit_solution(17956094558064839376)
XLA Ops:
  0.6 1.6 copy-done
  2.2 2.9 pack.3
  5.1 3.1 %collective-permute-start.6 = (bf16[3,512,256]{2,1,0:T(8,128)(2,1)S(1)}, bf16[3,512,256]{2,1,0:T(8,128)(2,1)S(1)}, u32[]{:S(2)}, u32[]{:S(2)}) collective-permute-start(bf16[3,512,256]{2,1,0:T(8,128)(2,1)S(1)} %get-tuple-element.43), channel_id=1, source_target_pairs={{0,1},{1,2},{2,3},{3,0},{4,5},{5,6},{6,7},{7,4},{8,9},{9,10},{10,1... | collective-permute-start | bytes 2359304 | tf_op jit(solution)/shard_map/ppermute | solution.py:496
  8.2 2.6 collective-permute-start.7
  10.7 1.3 collective-permute-start.8
  12.1 3.1 %pack.2 = (bf16[3,512,256]{2,1,0:T(8,128)(2,1)S(1)}, bf16[3,512,256]{2,1,0:T(8,128)(2,1)}, bf16[3,512,256]{2,1,0:T(8,128)(2,1)}, bf16[3,512,256]{2,1,0:T(8,128)(2,1)}) custom-call(s32[1]{0:T(128)} %bitcast._.z_ref, bf16[512,2048]{1,0:T(8,128)(2,1)S(1)} %copy-done, bf16[512,2048]{1,0:T(8,128)(2,1)} %refs_10_.3, bf16[512,2048]{1,0:T(8,128)(2,1)} %refs_11_.3, ...), custom_call_target="tpu_custom_call" | custom-call | bytes 6291456 | tf_op jit(solution)/shard_map/pack/pallas_call | solution.py:54
  16.3 12.4 %collective-permute-done.6.refs_1_ = bf16[3,512,256]{2,1,0:T(8,128)(2,1)S(1)} collective-permute-done((bf16[3,512,256]{2,1,0:T(8,128)(2,1)S(1)}, bf16[3,512,256]{2,1,0:T(8,128)(2,1)S(1)}, u32[]{:S(2)}, u32[]{:S(2)}) %collective-permute-start.6) | collective-permute-done | bytes 786464 | tf_op jit(solution)/shard_map/ppermute | solution.py:496
  29.6 2.4 collective-permute-start.2
  32.2 14.0 %state.1 = (bf16[16,64,128]{2,1,0:T(8,128)(2,1)S(1)}, f32[16,8,128]{2,1,0:T(8,128)S(1)}, bf16[512,2048]{1,0:T(8,128)(2,1)S(1)}) custom-call(bf16[512,2048]{1,0:T(8,128)(2,1)S(1)} %copy-done.2, bf16[512,2048]{1,0:T(8,128)(2,1)} %k_ref.9, bf16[512,2048]{1,0:T(8,128)(2,1)} %v_ref.9, bf16[512,32]{1,0:T(8,128)(2,1)S(1)} %copy.43.d_ref), custom_call_target="tpu_custom_call" | custom-call | flops 1073741824 | bytes 8388608 | tf_op jit(solution)/shard_map/state/pallas_call | solution.py:256
  46.2 16.4 %collective-permute-done.7.refs_2_ = bf16[3,512,256]{2,1,0:T(8,128)(2,1)} collective-permute-done((bf16[3,512,256]{2,1,0:T(8,128)(2,1)}, bf16[3,512,256]{2,1,0:T(8,128)(2,1)}, u32[]{:S(2)}, u32[]{:S(2)}) %collective-permute-start.7) | collective-permute-done | bytes 786464 | tf_op jit(solution)/shard_map/ppermute | solution.py:496
  62.6 27.1 %soft.3 = (bf16[512,256]{1,0:T(8,128)(2,1)S(1)}, bf16[512,256]{1,0:T(8,128)(2,1)S(1)}, bf16[512,256]{1,0:T(8,128)(2,1)S(1)}, bf16[512,256]{1,0:T(8,128)(2,1)S(1)}) custom-call(s32[1]{0:T(128)} %bitcast._.z_ref, s32[16,16]{1,0:T(8,128)S(1)} %copy-done.18, bf16[3,512,256]{2,1,0:T(8,128)(2,1)S(1)} %copy-done.15, bf16[3,512,256]{2,1,0:T(8,128)(2,1)S(1)} %copy-done.17, ...), custom_call_target="tpu_custom_call" | custom-call | flops 4294967296 | bytes 4194304 | tf_op jit(solution)/shard_map/soft/pallas_call | solution.py:181
  89.7 51.2 %collective-permute-start.9 = (bf16[512,256]{1,0:T(8,128)(2,1)S(1)}, bf16[512,256]{1,0:T(8,128)(2,1)S(1)}, u32[]{:S(2)}, u32[]{:S(2)}) collective-permute-start(bf16[512,256]{1,0:T(8,128)(2,1)S(1)} %get-tuple-element.47), channel_id=1, source_target_pairs={{0,1},{1,2},{2,3},{3,0},{4,5},{5,6},{6,7},{7,4},{8,9},{9,10},{10,1... | collective-permute-start | bytes 786440 | tf_op jit(solution)/shard_map/ppermute | solution.py:496
  140.8 1.8 collective-permute-start.10
  143.3 27.3 %soft.2 = (bf16[512,256]{1,0:T(8,128)(2,1)S(1)}, bf16[512,256]{1,0:T(8,128)(2,1)S(1)}, bf16[512,256]{1,0:T(8,128)(2,1)S(1)}, bf16[512,256]{1,0:T(8,128)(2,1)S(1)}) custom-call(s32[1]{0:T(128)} %bitcast._.z_ref, s32[16,16]{1,0:T(8,128)S(1)} %copy-done.18, bf16[3,512,256]{2,1,0:T(8,128)(2,1)S(1)} %get-tuple-element.34.refs_0_, ...), custom_call_target="tpu_custom_call" | custom-call | flops 4294967296 | bytes 4194304 | tf_op jit(solution)/shard_map/soft/pallas_call | solution.py:181
  170.6 14.5 %collective-permute-start.3 = (bf16[512,256]{1,0:T(8,128)(2,1)S(1)}, bf16[512,256]{1,0:T(8,128)(2,1)S(1)}, u32[]{:S(2)}, u32[]{:S(2)}) collective-permute-start(bf16[512,256]{1,0:T(8,128)(2,1)S(1)} %get-tuple-element.39), channel_id=1, source_target_pairs={{0,1},{1,2},{2,3},{3,0},{4,5},{5,6},{6,7},{7,4},{8,9},{9,10},{10,1... | collective-permute-start | bytes 786440 | tf_op jit(solution)/shard_map/ppermute | solution.py:496
  185.1 2.4 collective-permute-start.5
  188.4 3.4 %collective-permute-done.3.refs_1_ = bf16[512,256]{1,0:T(8,128)(2,1)S(1)} collective-permute-done((bf16[512,256]{1,0:T(8,128)(2,1)S(1)}, bf16[512,256]{1,0:T(8,128)(2,1)S(1)}, u32[]{:S(2)}, u32[]{:S(2)}) %collective-permute-start.3) | collective-permute-done | bytes 262176 | tf_op jit(solution)/shard_map/ppermute | solution.py:496
  191.8 7.3 %collective-permute-done.4.refs_2_ = bf16[512,256]{1,0:T(8,128)(2,1)S(1)} collective-permute-done((bf16[512,256]{1,0:T(8,128)(2,1)S(1)}, bf16[512,256]{1,0:T(8,128)(2,1)S(1)}, u32[]{:S(2)}, u32[]{:S(2)}) %collective-permute-start.4) | collective-permute-done | bytes 262176 | tf_op jit(solution)/shard_map/ppermute | solution.py:496
  199.2 2.7 collective-permute-done.5.refs_3_
  202.8 26.2 %all_to_all.10 = bf16[32,72,128]{2,1,0:T(8,128)(2,1)S(1)} all-to-all(bf16[32,72,128]{2,1,0:T(8,128)(2,1)S(1)} %maximum_maximum_fusion), channel_id=1, replica_groups=mesh['ctx'=8,'head'=4] {'ctx','head'}, dimensions={0} | all-to-all | bytes 1179648 | tf_op jit(solution)/shard_map/all_to_all | solution.py:540
  230.2 4.6 %all-to-all-start.1 = ((bf16[32,64,128]{2,1,0:T(8,128)(2,1)}), bf16[32,64,128]{2,1,0:T(8,128)(2,1)}, u32[]{:S(2)}, u32[]{:S(2)}) async-start(bf16[32,64,128]{2,1,0:T(8,128)(2,1)} %copy-done.5), calls=%async_computation.1 | async-start | bytes 1048576 | tf_op jit(solution)/shard_map/all_to_all | solution.py:540
  235.7 1.0 reshape.102.t_ref
  237.7 0.9 copy-done.9
  238.6 0.9 copy-done.11
  239.6 0.9 copy-done.13
  240.5 17.6 %local.3 = (f32[512,2048]{1,0:T(8,128)}, f32[512,2048]{1,0:T(8,128)}, f32[512,2048]{1,0:T(8,128)}, bf16[512,2048]{1,0:T(8,128)(2,1)S(1)}) custom-call(s32[1]{0:T(128)} %bitcast._.z_ref, bf16[512,2048]{1,0:T(8,128)(2,1)S(1)} %copy-done.2, bf16[512,2048]{1,0:T(8,128)(2,1)} %k_ref.9, bf16[512,2048]{1,0:T(8,128)(2,1)} %v_ref.9, bf16[512,32]{1,0:T(8,128)(2,1)S(1)} %copy.43.d_ref, ...), custom_call_target="tpu_custom_call" | custom-call | flops 2684354560 | bytes 11534336 | tf_op jit(solution)/shard_map/local/pallas_call | solution.py:424
  258.1 9.8 %local.4 = (f32[512,2048]{1,0:T(8,128)}, f32[512,2048]{1,0:T(8,128)}, f32[512,2048]{1,0:T(8,128)}, bf16[512,2048]{1,0:T(8,128)(2,1)S(1)}) custom-call(s32[1]{0:T(128)} %bitcast._.z_ref, bf16[512,2048]{1,0:T(8,128)(2,1)S(1)} %copy-done.2, bf16[512,2048]{1,0:T(8,128)(2,1)} %k_ref.9, ...), custom_call_target="tpu_custom_call", output_to_operand_aliasing={{0}: (10, {}), {1}: (11, {}), {2}: (12, {}), {3}: (13, {})} | custom-call | flops 1342177280 | bytes 5767168 | tf_op jit(solution)/shard_map/local/pallas_call | solution.py:424
  267.9 9.8 %local.5 = (f32[512,2048]{1,0:T(8,128)}, f32[512,2048]{1,0:T(8,128)}, f32[512,2048]{1,0:T(8,128)}, bf16[512,2048]{1,0:T(8,128)(2,1)S(1)}) custom-call(s32[1]{0:T(128)} %bitcast._.z_ref, bf16[512,2048]{1,0:T(8,128)(2,1)S(1)} %copy-done.2, bf16[512,2048]{1,0:T(8,128)(2,1)} %k_ref.9, ...), custom_call_target="tpu_custom_call", output_to_operand_aliasing={{0}: (10, {}), {1}: (11, {}), {2}: (12, {}), {3}: (13, {})} | custom-call | flops 1342177280 | bytes 5767168 | tf_op jit(solution)/shard_map/local/pallas_call | solution.py:424
  277.7 1.3 copy-done.3
  279.0 1.2 fusion.5
  280.8 1.6 copy-done.4
  282.4 11.3 %final.1 = (bf16[512,2048]{1,0:T(8,128)(2,1)}, bf16[512,2048]{1,0:T(8,128)(2,1)}, bf16[512,2048]{1,0:T(8,128)(2,1)}) custom-call(f32[512,2048]{1,0:T(8,128)} %get-tuple-element.58.pq_ref, f32[512,2048]{1,0:T(8,128)} %get-tuple-element.59.pk_ref, f32[512,2048]{1,0:T(8,128)} %get-tuple-element.60.pv_ref, bf16[512,2048]{1,0:T(8,128)(2,1)S(1)} %copy-done.4, ...), custom_call_target="tpu_custom_call" | custom-call | flops 805306368 | bytes 25165824 | tf_op jit(solution)/shard_map/final/pallas_call | solution.py:480
  (74 shorter events, 8.0 us)
Async XLA Ops:
  0.6 1.6 copy-start
  5.1 10.1 %copy-start.14 = (bf16[3,512,256]{2,1,0:T(8,128)(2,1)}, bf16[3,512,256]{2,1,0:T(8,128)(2,1)S(1)}, u32[]{:S(2)}) copy-start(bf16[3,512,256]{2,1,0:T(8,128)(2,1)S(1)} %get-tuple-element.42.refs_0_) | copy-start | bytes 2359300
  5.1 23.6 %collective-permute-start.6 = (bf16[3,512,256]{2,1,0:T(8,128)(2,1)S(1)}, bf16[3,512,256]{2,1,0:T(8,128)(2,1)S(1)}, u32[]{:S(2)}, u32[]{:S(2)}) collective-permute-start(bf16[3,512,256]{2,1,0:T(8,128)(2,1)S(1)} %get-tuple-element.43), channel_id=1, source_target_pairs={{0,1},{1,2},{2,3},{3,0},{4,5},{5,6},{6,7},{7,4},{8,9},{9,10},{10,1... | collective-permute-start | bytes 2359304 | tf_op jit(solution)/shard_map/ppermute | solution.py:496
  8.2 54.4 %collective-permute-start.7 = (bf16[3,512,256]{2,1,0:T(8,128)(2,1)}, bf16[3,512,256]{2,1,0:T(8,128)(2,1)}, u32[]{:S(2)}, u32[]{:S(2)}) collective-permute-start(bf16[3,512,256]{2,1,0:T(8,128)(2,1)} %get-tuple-element.44), channel_id=1, source_target_pairs={{0,2},{1,3},{2,0},{3,1},{4,6},{5,7},{6,4},{7,5},{8,10},{9,11},{10,... | collective-permute-start | bytes 2359304 | tf_op jit(solution)/shard_map/ppermute | solution.py:496
  10.7 21.3 %copy-start.19 = (bf16[512,32]{0,1:T(8,128)(2,1)S(1)}, bf16[512,32]{0,1:T(8,128)(2,1)}, u32[]{:S(2)}) copy-start(bf16[512,32]{0,1:T(8,128)(2,1)} %param.14) | copy-start | bytes 98308
  10.7 21.4 %copy-start.2 = (bf16[512,2048]{1,0:T(8,128)(2,1)S(1)}, bf16[512,2048]{1,0:T(8,128)(2,1)}, u32[]{:S(2)}) copy-start(bf16[512,2048]{1,0:T(8,128)(2,1)} %q_ref.7) | copy-start | bytes 6291460
  10.7 51.8 %collective-permute-start.8 = (bf16[3,512,256]{2,1,0:T(8,128)(2,1)}, bf16[3,512,256]{2,1,0:T(8,128)(2,1)}, u32[]{:S(2)}, u32[]{:S(2)}) collective-permute-start(bf16[3,512,256]{2,1,0:T(8,128)(2,1)} %get-tuple-element.45), channel_id=1, source_target_pairs={{0,3},{1,0},{2,1},{3,2},{4,7},{5,4},{6,5},{7,6},{8,11},{9,8},{10,9... | collective-permute-start | bytes 2359304 | tf_op jit(solution)/shard_map/ppermute | solution.py:496
  15.2 127.4 %collective-permute-start = (bf16[3,512,256]{2,1,0:T(8,128)(2,1)}, bf16[3,512,256]{2,1,0:T(8,128)(2,1)}, u32[]{:S(2)}, u32[]{:S(2)}) collective-permute-start(bf16[3,512,256]{2,1,0:T(8,128)(2,1)} %get-tuple-element.35), channel_id=1, source_target_pairs={{0,1},{1,2},{2,3},{3,0},{4,5},{5,6},{6,7},{7,4},{8,9},{9,10},{10,1... | collective-permute-start | bytes 2359304 | tf_op jit(solution)/shard_map/ppermute | solution.py:496
  15.9 127.4 %collective-permute-start.1 = (bf16[3,512,256]{2,1,0:T(8,128)(2,1)}, bf16[3,512,256]{2,1,0:T(8,128)(2,1)}, u32[]{:S(2)}, u32[]{:S(2)}) collective-permute-start(bf16[3,512,256]{2,1,0:T(8,128)(2,1)} %get-tuple-element.36), channel_id=1, source_target_pairs={{0,2},{1,3},{2,0},{3,1},{4,6},{5,7},{6,4},{7,5},{8,10},{9,11},{10,... | collective-permute-start | bytes 2359304 | tf_op jit(solution)/shard_map/ppermute | solution.py:496
  29.6 113.7 %collective-permute-start.2 = (bf16[3,512,256]{2,1,0:T(8,128)(2,1)}, bf16[3,512,256]{2,1,0:T(8,128)(2,1)}, u32[]{:S(2)}, u32[]{:S(2)}) collective-permute-start(bf16[3,512,256]{2,1,0:T(8,128)(2,1)} %get-tuple-element.37), channel_id=1, source_target_pairs={{0,3},{1,0},{2,1},{3,2},{4,7},{5,4},{6,5},{7,6},{8,11},{9,8},{10,9... | collective-permute-start | bytes 2359304 | tf_op jit(solution)/shard_map/ppermute | solution.py:496
  32.2 30.4 %copy-start.15 = (bf16[3,512,256]{2,1,0:T(8,128)(2,1)S(1)}, bf16[3,512,256]{2,1,0:T(8,128)(2,1)}, u32[]{:S(2)}) copy-start(bf16[3,512,256]{2,1,0:T(8,128)(2,1)} %copy-done.14) | copy-start | bytes 2359300
  32.2 30.4 %copy-start.17 = (bf16[3,512,256]{2,1,0:T(8,128)(2,1)S(1)}, bf16[3,512,256]{2,1,0:T(8,128)(2,1)}, u32[]{:S(2)}) copy-start(bf16[3,512,256]{2,1,0:T(8,128)(2,1)} %copy-done.16) | copy-start | bytes 2359300
  32.2 30.4 %copy-start.18 = (s32[16,16]{1,0:T(8,128)S(1)}, s32[16,16]{1,0:T(8,128)}, u32[]{:S(2)}) copy-start(s32[16,16]{1,0:T(8,128)} %flags.3) | copy-start | bytes 3076
  89.7 98.1 %copy-start.6 = (bf16[512,256]{1,0:T(8,128)(2,1)}, bf16[512,256]{1,0:T(8,128)(2,1)S(1)}, u32[]{:S(2)}) copy-start(bf16[512,256]{1,0:T(8,128)(2,1)S(1)} %get-tuple-element.46.refs_0_) | copy-start | bytes 786436
  89.7 95.5 %collective-permute-start.9 = (bf16[512,256]{1,0:T(8,128)(2,1)S(1)}, bf16[512,256]{1,0:T(8,128)(2,1)S(1)}, u32[]{:S(2)}, u32[]{:S(2)}) collective-permute-start(bf16[512,256]{1,0:T(8,128)(2,1)S(1)} %get-tuple-element.47), channel_id=1, source_target_pairs={{0,1},{1,2},{2,3},{3,0},{4,5},{5,6},{6,7},{7,4},{8,9},{9,10},{10,1... | collective-permute-start | bytes 786440 | tf_op jit(solution)/shard_map/ppermute | solution.py:496
  140.8 46.9 %collective-permute-start.10 = (bf16[512,256]{1,0:T(8,128)(2,1)S(1)}, bf16[512,256]{1,0:T(8,128)(2,1)S(1)}, u32[]{:S(2)}, u32[]{:S(2)}) collective-permute-start(bf16[512,256]{1,0:T(8,128)(2,1)S(1)} %get-tuple-element.48), channel_id=1, source_target_pairs={{0,2},{1,3},{2,0},{3,1},{4,6},{5,7},{6,4},{7,5},{8,10},{9,11},{10,... | collective-permute-start | bytes 786440 | tf_op jit(solution)/shard_map/ppermute | solution.py:496
  142.6 45.1 %collective-permute-start.11 = (bf16[512,256]{1,0:T(8,128)(2,1)S(1)}, bf16[512,256]{1,0:T(8,128)(2,1)S(1)}, u32[]{:S(2)}, u32[]{:S(2)}) collective-permute-start(bf16[512,256]{1,0:T(8,128)(2,1)S(1)} %get-tuple-element.49), channel_id=1, source_target_pairs={{0,3},{1,0},{2,1},{3,2},{4,7},{5,4},{6,5},{7,6},{8,11},{9,8},{10,9... | collective-permute-start | bytes 786440 | tf_op jit(solution)/shard_map/ppermute | solution.py:496
  170.6 21.2 %collective-permute-start.3 = (bf16[512,256]{1,0:T(8,128)(2,1)S(1)}, bf16[512,256]{1,0:T(8,128)(2,1)S(1)}, u32[]{:S(2)}, u32[]{:S(2)}) collective-permute-start(bf16[512,256]{1,0:T(8,128)(2,1)S(1)} %get-tuple-element.39), channel_id=1, source_target_pairs={{0,1},{1,2},{2,3},{3,0},{4,5},{5,6},{6,7},{7,4},{8,9},{9,10},{10,1... | collective-permute-start | bytes 786440 | tf_op jit(solution)/shard_map/ppermute | solution.py:496
  185.1 14.0 %collective-permute-start.4 = (bf16[512,256]{1,0:T(8,128)(2,1)S(1)}, bf16[512,256]{1,0:T(8,128)(2,1)S(1)}, u32[]{:S(2)}, u32[]{:S(2)}) collective-permute-start(bf16[512,256]{1,0:T(8,128)(2,1)S(1)} %get-tuple-element.40), channel_id=1, source_target_pairs={{0,2},{1,3},{2,0},{3,1},{4,6},{5,7},{6,4},{7,5},{8,10},{9,11},{10,... | collective-permute-start | bytes 786440 | tf_op jit(solution)/shard_map/ppermute | solution.py:496
  185.1 17.3 %copy-start.8 = (bf16[512,256]{1,0:T(8,128)(2,1)}, bf16[512,256]{1,0:T(8,128)(2,1)S(1)}, u32[]{:S(2)}) copy-start(bf16[512,256]{1,0:T(8,128)(2,1)S(1)} %collective-permute-done.9.refs_1_) | copy-start | bytes 786436
  185.1 16.7 %collective-permute-start.5 = (bf16[512,256]{1,0:T(8,128)(2,1)S(1)}, bf16[512,256]{1,0:T(8,128)(2,1)S(1)}, u32[]{:S(2)}, u32[]{:S(2)}) collective-permute-start(bf16[512,256]{1,0:T(8,128)(2,1)S(1)} %get-tuple-element.41), channel_id=1, source_target_pairs={{0,3},{1,0},{2,1},{3,2},{4,7},{5,4},{6,5},{7,6},{8,11},{9,8},{10,9... | collective-permute-start | bytes 786440 | tf_op jit(solution)/shard_map/ppermute | solution.py:496
  187.7 14.8 %copy-start.10 = (bf16[512,256]{1,0:T(8,128)(2,1)}, bf16[512,256]{1,0:T(8,128)(2,1)S(1)}, u32[]{:S(2)}) copy-start(bf16[512,256]{1,0:T(8,128)(2,1)S(1)} %collective-permute-done.10.refs_2_) | copy-start | bytes 786436
  187.7 14.8 %copy-start.12 = (bf16[512,256]{1,0:T(8,128)(2,1)}, bf16[512,256]{1,0:T(8,128)(2,1)S(1)}, u32[]{:S(2)}) copy-start(bf16[512,256]{1,0:T(8,128)(2,1)S(1)} %collective-permute-done.11.refs_3_) | copy-start | bytes 786436
  229.0 5.8 %copy-start.20 = (bf16[512,32]{0,1:T(8,128)(2,1)S(1)}, bf16[512,32]{0,1:T(8,128)(2,1)}, u32[]{:S(2)}) copy-start(bf16[512,32]{0,1:T(8,128)(2,1)} %param.14) | copy-start | bytes 98308
  230.2 48.8 %all-to-all-start.1 = ((bf16[32,64,128]{2,1,0:T(8,128)(2,1)}), bf16[32,64,128]{2,1,0:T(8,128)(2,1)}, u32[]{:S(2)}, u32[]{:S(2)}) async-start(bf16[32,64,128]{2,1,0:T(8,128)(2,1)} %copy-done.5), calls=%async_computation.1 | async-start | bytes 1048576 | tf_op jit(solution)/shard_map/all_to_all | solution.py:540
  236.7 1.0 copy-start.7
  237.7 0.9 copy-start.9
  238.6 0.9 copy-start.11
  239.6 0.9 copy-start.13
  277.7 1.3 copy-start.3
  279.0 1.8 copy-start.1
  280.8 1.6 copy-start.4
  (2 other events, 1.7 us)
where the time goes:
time: 295 us; the launch traced here: 294 us
  Pallas kernels  124 us (42%)
  starting transfers between devices  85.7 us (29%)
  waiting for transfers between devices  42.2 us (14%)
  blocking collectives  26.2 us (9%)
  local copies, waits for them, and re-layouts  14 us (5%)
    ppermute x12, starting transfers between devices, turn(): lax.ppermute(pieces[k], 'head', [(i, (i + k) % count) for i in range(coun...  81.2 us
    pallas_call x2, Pallas kernels, soft(): pl.pallas_call(functools.partial(soft_kernel, count, root), out_shape=[ja...  54.4 us
    ppermute x12, waiting for transfers between devices, turn(): lax.ppermute(pieces[k], 'head', [(i, (i + k) % count) for i in range(coun...  42.2 us
    pallas_call x3, Pallas kernels, local(): pl.pallas_call(functools.partial(local_kernel, count, first, skip, len(ol...  37.2 us
    all_to_all x1, blocking collectives, exchange(): return lax.all_to_all(x, AXES, split_axis=0, concat_axis=0, tiled=True)  26.2 us
    pallas_call x1, Pallas kernels, device_state(): pl.pallas_call(state_kernel, out_shape=[jax.ShapeDtypeStruct((pairs, BLOC...  14 us
    pallas_call x1, Pallas kernels, final(): pl.pallas_call(functools.partial(final_kernel, scale), out_shape=[jax.Sha...  11.3 us
    unnamed x43, local copies, waits for them, and re-layouts  10.6 us
  transfers between devices with their start and end apart: 13, of which 5 were waited for; matrix products, arithmetic and copies ran while one was open for 1% of the time, Pallas kernels for 37%

commit v1 on v0

--- a/solution.py
+++ b/solution.py
@@ -200,6 +200,377 @@
     )(here, flags, *pieces)
 
 
+OWNED = ((0, 1), (), (2, 3, 4), (5, 6, 7))
+SHARE = 8
+UNROLLS = {2: (4, 2, 1), 3: (4, 2, 1), 8: (2, 1)}
+
+
+def pack_quad_kernel(z_ref, *refs):
+    ins, outs = refs[:21], refs[21:]
+    two, three, key_c, key_d, key_all, key_two = outs
+    for n in range(3):
+        two[n] = ins[n][...]
+        for p in range(3):
+            three[n, :, p * BLOCK : (p + 1) * BLOCK] = ins[3 + 3 * n + p][...]
+        key_c[:, n * BLOCK : (n + 1) * BLOCK] = ins[12 + n][...]
+        key_d[:, n * BLOCK : (n + 1) * BLOCK] = ins[15 + n][...]
+    key_all[...] = ins[18][...]
+    key_two[...] = ins[19][...]
+
+
+def pack_quad(here, arrays, chunk):
+    rows = arrays[0].shape[0]
+    key = arrays[1]
+
+    def spec(pair_of):
+        return pl.BlockSpec((rows, BLOCK), lambda i, z: (0, SHARE * chunk + pair_of(z[0])))
+
+    def far(p):
+        return spec(lambda z: 5 - 3 * lax.div(z, 3) + p)
+
+    front = pl.BlockSpec((rows, 2 * BLOCK), lambda i, z: (0, SHARE // 2 * chunk))
+    operands = list(arrays) + [array for array in arrays for _ in range(3)] + [key] * 9
+    specs = [front] * 3
+    specs += [far(p) for p in range(3)] * 3
+    specs += [spec(lambda z, p=p: 2 + 3 * jnp.minimum(z, 1) + p) for p in range(3)]
+    specs += [spec(lambda z, p=p: 5 - 3 * jnp.minimum(z, 1) + p) for p in range(3)]
+    specs += [pl.BlockSpec((rows, SHARE * BLOCK), lambda i, z: (0, chunk))]
+    specs += [front] * 2
+    shapes = [
+        (3, rows, 2 * BLOCK), (3, rows, 3 * BLOCK), (rows, 3 * BLOCK), (rows, 3 * BLOCK),
+        (rows, SHARE * BLOCK), (rows, 2 * BLOCK),
+    ]
+    return pl.pallas_call(
+        pack_quad_kernel,
+        out_shape=[jax.ShapeDtypeStruct(shape, BF) for shape in shapes],
+        grid_spec=pltpu.PrefetchScalarGridSpec(
+            num_scalar_prefetch=1,
+            grid=(1,),
+            in_specs=specs,
+            out_specs=[pl.BlockSpec(shape, lambda i, z, n=len(shape): (0,) * n) for shape in shapes],
+        ),
+        compiler_params=params(60),
+        cost_estimate=pl.CostEstimate(flops=0, transcendentals=0, bytes_accessed=120 * rows * BLOCK),
+        name="pack",
+    )(here, *operands)
+
+
+def send(x, *routes):
+    return lax.ppermute(x, "head", routes)
+
+
+def turn_in(pieces):
+    two, three, key_c, key_d, key_all, key_two = pieces
+    return (
+        send(three, (3, 2), (2, 3)),
+        send(key_all, (0, 1)),
+        send(key_c, (0, 2), (1, 3)),
+        send(key_d, (0, 3), (1, 2)),
+        send(two, (2, 0)),
+        send(two, (3, 0)),
+        send(key_two, (1, 0)),
+    )
+
+
+def turn_out(pieces):
+    wide, three_d, three_e, three_f, two_a, two_b, two_c = pieces
+    return (
+        send(wide, (1, 0)),
+        send(three_d, (2, 0), (3, 1)),
+        send(three_e, (2, 1), (3, 0)),
+        send(three_f, (2, 3), (3, 2)),
+        send(two_a, (0, 2)),
+        send(two_b, (0, 3)),
+        send(two_c, (0, 1)),
+    )
+
+
+def rows_of(j):
+    return pl.ds(pl.multiple_of(j * BLOCK, BLOCK), BLOCK)
+
+
+def attend(i, query, cotan, key_of, add, flags, scores, tops, listed):
+    pairs = len(query)
+    groups = BLOCK // 8
+    wide = 2 * BLOCK
+    key_at = lax.broadcasted_iota(jnp.int32, (BLOCK, wide), 0)
+    query_at = lax.rem(lax.broadcasted_iota(jnp.int32, (BLOCK, wide), 1), BLOCK)
+
+    def collect(j, found):
+        listed[found] = j
+        return found + flags[i, j]
+
+    listed[0] = i
+    found = lax.fori_loop(0, i, collect, 1)
+
+    def absorb(slots, p, blocks, top, total):
+        newer = top
+        for block in blocks:
+            newer = jnp.maximum(newer, jnp.max(block, axis=0))
+        total = total * jnp.exp(top - newer)
+        for n, block in zip(slots, blocks):
+            block = jnp.exp(block - newer[None])
+            scores[p, n] = block
+            tops[p, n] = newer
+            total = total + jnp.sum(block, axis=0)
+        return newer, total
+
+    def raw(n, p):
+        return mm(key_of(listed[n], p), query[p], 1, 1).reshape(groups, 8, wide)
+
+    held = []
+    for p in range(pairs):
+        own = mm(key_of(i, p), query[p], 1, 1)
+        own = jnp.where(key_at <= query_at, own, NEG).reshape(groups, 8, wide)
+        floor = jnp.full((8, wide), NEG, F32)
+        held.append(absorb((0,), p, (own,), floor, jnp.zeros((8, wide), F32)))
+
+    def first(unroll, start):
+        def step(n, held):
+            slots = [start + unroll * n + m for m in range(unroll)]
+            blocks = [[raw(n, p) for n in slots] for p in range(pairs)]
+            return tuple(absorb(slots, p, blocks[p], *held[p]) for p in range(pairs))
+
+        return step
+
+    held, done = tuple(held), 1
+    for unroll in UNROLLS[pairs]:
+        turns = (found - done) // unroll
+        held = lax.fori_loop(0, turns, first(unroll, done), held)
+        done = done + unroll * turns
+    highest, share = [], []
+    for top, total in held:
+        most = jnp.max(top, axis=0, keepdims=True)
+        total = jnp.sum(total * jnp.exp(top - most), axis=0, keepdims=True)
+        highest.append(most)
+        share.append(1.0 / total)
+
+    def second(unroll, start):
+        def step(n, _):
+            parts = []
+            for slot in [start + unroll * n + m for m in range(unroll)]:
+                for p in range(pairs):
+                    factor = jnp.exp(tops[p, slot] - highest[p]) * share[p]
+                    block = (scores[p, slot] * factor[None]).reshape(BLOCK, wide).astype(BF)
+                    parts.append((slot, p, mm(block, cotan[p], 1, 0)))
+            for slot, p, part in parts:
+                add(listed[slot], p, part)
+            return 0
+
+        return step
+
+    done = 0
+    for unroll in UNROLLS[pairs]:
+        turns = (found - done) // unroll
+        lax.fori_loop(0, turns, second(unroll, done), 0)
+        done = done + unroll * turns
+
+
+def soft_quad_kernel(root, z_ref, flags, q_ref, k_ref, u_ref, three, key_all, key_c, key_d, two_a, two_b, key_two, *refs):
+    outs, (queries, keys, cotans, summed, near, summed_near, scores, tops, listed) = refs[:8], refs[8:]
+    wide, three_d, three_e, three_f, out_a, out_b, out_c, mine = outs
+    rows = q_ref.shape[0]
+    per = rows // BLOCK
+    z = z_ref[0]
+    root = jnp.asarray(root, BF)
+    summed[...] = jnp.zeros_like(summed)
+
+    def part(n):
+        return slice(n * rows, (n + 1) * rows)
+
+    def lanes(p):
+        return slice(p * BLOCK, (p + 1) * BLOCK)
+
+    def place(n, q, k, u, width):
+        queries[part(n), :width] = q * root
+        keys[part(2 + n), :width] = k
+        cotans[part(n), :width] = u
+
+    for me in range(4):
+
+        @pl.when(z == me)
+        def _(me=me):
+            if me == 1:
+                near[part(0), :] = key_all[...]
+                near[part(1), :] = k_ref[...]
+                return
+            pairs = len(OWNED[me])
+            width = pairs * BLOCK
+            own = slice(OWNED[me][0] * BLOCK, (OWNED[me][0] + pairs) * BLOCK)
+            if me == 0:
+                place(0, two_a[0], two_a[1], two_a[2], width)
+                place(1, two_b[0], two_b[1], two_b[2], width)
+                keys[part(0), :width] = k_ref[:, own]
+                keys[part(1), :width] = key_two[...]
+                near[part(0), :] = k_ref[...]
+            else:
+                place(me - 2, q_ref[:, own], k_ref[:, own], u_ref[:, own], width)
+                place(3 - me, three[0], three[1], three[2], width)
+                keys[part(0), :width] = (key_c if me == 2 else key_d)[...]
+                keys[part(1), :width] = (key_d if me == 2 else key_c)[...]
+
+    def far_rows(pairs):
+        def query_block(n, _):
+            at = rows_of(n)
+
+            def add(j, p, x):
+                summed[rows_of(j), lanes(p)] += x
+
+            attend(
+                n + 2 * per,
+                [split_pair(queries[at, lanes(p)]) for p in range(pairs)],
+                [split_pair(cotans[at, lanes(p)]) for p in range(pairs)],
+                lambda j, p: keys[rows_of(j), lanes(p)],
+                add, flags, scores, tops, listed,
+            )
+            return 0
+
+        lax.fori_loop(0, 2 * per, query_block, 0)
+
+    @pl.when(z >= 2)
+    def _():
+        far_rows(3)
+
+    @pl.when(z == 0)
+    def _():
+        far_rows(2)
+
+    @pl.when(z < 2)
+    def _():
+        summed_near[...] = jnp.zeros_like(summed_near)
+
+        def near_block(n, _):
+            group, block = n // per, lax.rem(n, per)
+            at = rows_of(block)
+
+            def side(p):
+                return pl.ds(pl.multiple_of((8 * group + p) * BLOCK, BLOCK), BLOCK)
+
+            def add(j, p, x):
+                summed_near[rows_of(j), side(p)] += x
+
+            attend(
+                block + z * per,
+                [split_pair(q_ref[at, side(p)] * root) for p in range(8)],
+                [split_pair(u_ref[at, side(p)]) for p in range(8)],
+                lambda j, p: near[rows_of(j), side(p)],
+                add, flags, scores, tops, listed,
+            )
+            return 0
+
+        lax.fori_loop(0, per * (SHARE // 8), near_block, 0)
+
+    for me in range(4):
+
+        @pl.when(z == me)
+        def _(me=me):
+            if me == 1:
+                wide[...] = summed_near[part(0), :].astype(BF)
+                mine[...] = summed_near[part(1), :]
+                return
+            pairs = len(OWNED[me])
+            width = pairs * BLOCK
+            own = slice(OWNED[me][0] * BLOCK, (OWNED[me][0] + pairs) * BLOCK)
+            if me == 0:
+                out_c[...] = summed[part(1), :width].astype(BF)
+                out_a[...] = summed[part(2), :width].astype(BF)
+                out_b[...] = summed[part(3), :width].astype(BF)
+                mine[...] = summed_near[part(0), :]
+                mine[:, own] += summed[part(0), :width]
+            else:
+                three_d[...] = summed[part(me - 2), :].astype(BF)
+                three_e[...] = summed[part(3 - me), :].astype(BF)
+                three_f[...] = summed[part(5 - me), :].astype(BF)
+                mine[:, own] = summed[part(me), :]
+
+
+def soft_quad(here, flags, arrays, pieces, root, chunk):
+    rows = arrays[0].shape[0]
+    span = 4 * rows
+
+    def whole(shape):
+        return pl.BlockSpec(shape, lambda i, z, f, n=len(shape): (0,) * n, pipeline_mode=pl.Buffered(1))
+
+    column = pl.BlockSpec((rows, SHARE * BLOCK), lambda i, z, f: (0, chunk), pipeline_mode=pl.Buffered(1))
+    shapes = [(rows, SHARE * BLOCK)] + [(rows, 3 * BLOCK)] * 3 + [(rows, 2 * BLOCK)] * 3 + [(rows, SHARE * BLOCK)]
+    return pl.pallas_call(
+        functools.partial(soft_quad_kernel, root),
+        out_shape=[jax.ShapeDtypeStruct(shape, BF) for shape in shapes[:-1]]
+        + [jax.ShapeDtypeStruct(shapes[-1], F32)],
+        grid_spec=pltpu.PrefetchScalarGridSpec(
+            num_scalar_prefetch=2,
+            grid=(1,),
+            in_specs=[column] * 3 + [whole(piece.shape) for piece in pieces],
+            out_specs=[whole(shape) for shape in shapes],
+            scratch_shapes=[
+                pltpu.VMEM((2 * rows, 3 * BLOCK), BF),
+                pltpu.VMEM((span, 3 * BLOCK), BF),
+                pltpu.VMEM((2 * rows, 3 * BLOCK), BF),
+                pltpu.VMEM((span, 3 * BLOCK), F32),
+                pltpu.VMEM((2 * rows, SHARE * BLOCK), BF),
+                pltpu.VMEM((2 * rows, SHARE * BLOCK), F32),
+                pltpu.VMEM((8, span // BLOCK, BLOCK // 8, 8, 2 * BLOCK), F32),
+                pltpu.VMEM((8, span // BLOCK, 8, 2 * BLOCK), F32),
+                pltpu.SMEM((span // BLOCK + 1,), jnp.int32),
+            ],
+        ),
+        compiler_params=params(56),
+        cost_estimate=pl.CostEstimate(
+            flops=8 * span * span * BLOCK, transcendentals=2 * span * span, bytes_accessed=64 * span * BLOCK
+        ),
+        name="soft",
+    )(here, flags, *arrays, *pieces)
+
+
+def merge_kernel(z_ref, mine, wide, three_d, three_e, three_f, two_a, two_b, two_c, lit_ref):
+    z = z_ref[0]
+    first = slice(0, 2 * BLOCK)
+    third, fourth = slice(2 * BLOCK, 5 * BLOCK), slice(5 * BLOCK, 8 * BLOCK)
+
+    def plus(at, x):
+        lit_ref[:, at] = (mine[:, at] + x.astype(F32)).astype(BF)
+
+    def keep(at):
+        lit_ref[:, at] = mine[:, at].astype(BF)
+
+    @pl.when(z == 0)
+    def _():
+        plus(first, wide[:, first])
+        plus(third, wide[:, third].astype(F32) + three_d[...].astype(F32))
+        plus(fourth, wide[:, fourth].astype(F32) + three_e[...].astype(F32))
+
+    @pl.when(z == 1)
+    def _():
+        plus(first, two_c[...])
+        plus(third, three_e[...])
+        plus(fourth, three_d[...])
+
+    @pl.when(z == 2)
+    def _():
+        lit_ref[:, first] = two_a[...]
+        keep(third)
+        lit_ref[:, fourth] = three_f[...]
+
+    @pl.when(z == 3)
+    def _():
+        lit_ref[:, first] = two_b[...]
+        lit_ref[:, third] = three_f[...]
+        keep(fourth)
+
+
+def merge(here, mine, pieces):
+    vmem = pl.BlockSpec(memory_space=pltpu.VMEM)
+    return pl.pallas_call(
+        merge_kernel,
+        out_shape=jax.ShapeDtypeStruct(mine.shape, BF),
+        in_specs=[pl.BlockSpec(memory_space=pltpu.SMEM)] + [vmem] * 8,
+        out_specs=vmem,
+        compiler_params=params(24),
+        cost_estimate=pl.CostEstimate(flops=4 * mine.size, transcendentals=0, bytes_accessed=10 * mine.size),
+        name="merge",
+    )(here, mine, *pieces)
+
+
 def triangle():
     row = lax.broadcasted_iota(jnp.int32, (BLOCK, BLOCK), 0)
     column = lax.broadcasted_iota(jnp.int32, (BLOCK, BLOCK), 1)
@@ -246,7 +617,12 @@
     level, last = device_levels(d_ref[...], 2 * pl.program_id(0), BLOCK)
     key = (k_ref[...].astype(F32) * jnp.exp(level - last)).astype(BF)
     sum_ref[0] = fold(on_diagonal(mm(key, v_ref[...], 0, 0))).astype(BF)
-    total_ref[0] = jnp.broadcast_to(last, total_ref.shape[1:])
+    thirds, rest = [], last
+    for _ in range(3):
+        thirds.append(rest.astype(BF))
+        rest = rest - thirds[-1].astype(F32)
+    blank = jnp.zeros((total_ref.shape[1] - 3, BLOCK), BF)
+    total_ref[0] = jnp.concatenate(thirds + [blank], axis=0)
     scaled_ref[...] = (q_ref[...].astype(F32) * jnp.exp(-level)).astype(BF)
 
 
@@ -257,7 +633,7 @@
         state_kernel,
         out_shape=[
             jax.ShapeDtypeStruct((pairs, BLOCK // 2, BLOCK), BF),
-            jax.ShapeDtypeStruct((pairs, 8, BLOCK), F32),
+            jax.ShapeDtypeStruct((pairs, 8, BLOCK), BF),
             jax.ShapeDtypeStruct(light_query.shape, BF),
         ],
         grid=(pairs,),
@@ -267,7 +643,7 @@
             pl.BlockSpec((1, 8, BLOCK), lambda p: (p, 0, 0)),
             block,
         ],
-        compiler_params=params(),
+        compiler_params=params(60),
         cost_estimate=pl.CostEstimate(
             flops=8 * rows * pairs * BLOCK * BLOCK, transcendentals=rows * pairs * BLOCK, bytes_accessed=8 * rows * pairs * BLOCK
         ),
@@ -348,7 +724,7 @@
     )(items, totals)
 
 
-def local_kernel(count, first_pair, skip, olds, z_ref, q_ref, k_ref, v_ref, d_ref, t_ref, *refs):
+def local_kernel(count, first_pair, skip, olds, z_ref, q_ref, k_ref, v_ref, d_ref, *refs):
     lits = refs[:count]
     gq_ref, gk_ref, gv_ref, lit_ref, held = refs[count + olds :]
     take_lit(count, z_ref[0], lits, held)
@@ -361,7 +737,10 @@
     ones_lower, ones_upper = (side.astype(F32).astype(BF) for side in (lower, upper))
     slot = skip + here
     spread = spread_decays(d_ref[...], 2 * (first_pair + slot), 2 * BLOCK, BLOCK)
-    lines = t_ref[0].astype(BF)
+    heads = d_ref.shape[1]
+    picked = lax.broadcasted_iota(jnp.int32, (8, heads), 1) - 2 * (first_pair + slot)
+    picked = picked == lax.broadcasted_iota(jnp.int32, (8, heads), 0) // 4
+    lines = mm(picked.astype(F32).astype(BF), d_ref[...], 1, 1).astype(BF)
     lit_ref[...] = held[slot]
     state = None
     kept = []
@@ -414,13 +793,13 @@
             state = query if state is None else decay * state + query
 
 
-def local(here, light_query, light_key, light_value, decays, lines, lits, first, skip, many, olds):
+def local(here, light_query, light_key, light_value, decays, lits, first, skip, many, olds):
     count = len(lits)
     rows, columns = light_query.shape
     width = lits[0].shape[1]
     pairs = count * width // BLOCK
     block = pl.BlockSpec((rows, BLOCK), lambda p, z: (0, first + skip + p))
-    base = 6 + count
+    base = 5 + count
     return pl.pallas_call(
         functools.partial(local_kernel, count, first, skip, len(olds)),
         out_shape=[jax.ShapeDtypeStruct((rows, columns), F32)] * 3 + [jax.ShapeDtypeStruct((rows, columns), BF)],
@@ -432,7 +811,6 @@
                 block,
                 block,
                 pl.BlockSpec(decays.shape, lambda p, z: (0, 0)),
-                pl.BlockSpec((1, 8, rows), lambda p, z: (first + skip + p, 0, 0)),
             ]
             + [pl.BlockSpec((rows, width), lambda p, z: (0, 0))] * count
             + [pl.BlockSpec(memory_space=pl.ANY)] * len(olds),
@@ -440,12 +818,12 @@
             scratch_shapes=[pltpu.VMEM((pairs, rows, BLOCK), BF)],
         ),
         input_output_aliases={base + n: n for n in range(len(olds))},
-        compiler_params=params(),
+        compiler_params=params(60),
         cost_estimate=pl.CostEstimate(
             flops=40 * rows * many * BLOCK * BLOCK, transcendentals=4 * rows * many * BLOCK, bytes_accessed=22 * rows * many * BLOCK
         ),
         name="local",
-    )(here, light_query, light_key, light_value, decays, lines, *lits, *olds)
+    )(here, light_query, light_key, light_value, decays, *lits, *olds)
 
 
 def wide_state(x):
@@ -483,7 +861,7 @@
         grid=(pairs // step,),
         in_specs=[block] * 6 + [pl.BlockSpec(decays.shape, lambda p: (0, 0)), small, small],
         out_specs=[block] * 3,
-        compiler_params=params(),
+        compiler_params=params(60),
         cost_estimate=pl.CostEstimate(
             flops=6 * rows * columns * BLOCK, transcendentals=2 * rows * columns, bytes_accessed=24 * rows * columns
         ),
@@ -501,7 +879,7 @@
 def program(light_query, light_key, light_value, soft_query, soft_key, upstream, decays, block_mask):
     count, spans = lax.axis_size("head"), lax.axis_size("ctx")
     devices = count * spans
-    rows, columns = light_query.shape
+    _, columns = light_query.shape
     heads = decays.shape[1]
     head_width = columns // heads
     pairs = heads // 2
@@ -516,23 +894,32 @@
     root = 1.0 / math.sqrt(head_width)
     here = lax.axis_index("head").astype(jnp.int32).reshape(1)
 
+    arrays = (soft_query, soft_key, upstream)
+    quad = count == 4 and chunks * SHARE == pairs
     packed = []
     for c in range(chunks):
-        pieces = pack(here, (soft_query, soft_key, upstream), c, count, per * BLOCK)
-        packed.append(turn(pieces, count))
+        if quad:
+            pieces = pack_quad(here, arrays, c)
+        else:
+            pieces = pack(here, arrays, c, count, per * BLOCK)
+        packed.append(turn_in(pieces) if quad else turn(pieces, count))
     sums, totals, scaled = device_state(light_query, light_key, light_value, decays, pairs)
-    lines = jnp.repeat(decays.T.astype(F32).reshape(pairs, 2, rows), 4, axis=1)
 
     parts, reaches = (), []
     for c in range(chunks):
-        lits = soft(here, block_mask, packed[c], root)
-        lits = turn(lits, count)
+        if quad:
+            *lits, mine = soft_quad(here, block_mask, arrays, packed[c], root, c)
+        else:
+            lits = soft(here, block_mask, packed[c], root)
+        lits = turn_out(lits) if quad else turn(lits, count)
+        if quad:
+            lits = (merge(here, mine, lits),)
         reaches.append(device_reach(here, scaled, lits, c))
         first, many = c * count * per, count * per
         cuts = (0, many // 2, many) if c == chunks - 1 else (0, many)
         for n in range(len(cuts) - 1):
             parts = local(
-                here, light_query, light_key, light_value, decays, lines, lits, first,
+                here, light_query, light_key, light_value, decays, lits, first,
                 cuts[n], cuts[n + 1] - cuts[n], tuple(parts),
             )
 
@@ -547,13 +934,8 @@
         x = x.reshape(devices, chunks, part, BLOCK)
         return jnp.swapaxes(x, 0, 1).reshape(pairs, head_width, BLOCK)
 
-    rates = jnp.swapaxes(totals[:, 0].reshape(chunks, count * per, BLOCK), 0, 1)
-    rates = jnp.repeat(rates, again, axis=0)
-    thirds = []
-    for _ in range(3):
-        thirds.append(lax.reduce_precision(rates, 8, 7))
-        rates = rates - thirds[-1]
-    thirds = jnp.stack(thirds, axis=1).reshape(devices, 3 * chunks, BLOCK).astype(BF)
+    thirds = jnp.transpose(totals[:, :3].reshape(chunks, count * per, 3, BLOCK), (1, 2, 0, 3))
+    thirds = jnp.repeat(thirds.reshape(count * per, 3 * chunks, BLOCK), again, axis=0)
     half = chunks * part
     fill = jnp.zeros((devices, -(2 * half + 3 * chunks) % 8, BLOCK), BF)
     sends = [spread(sums), spread(jnp.concatenate(reaches, axis=0)), thirds, fill]

time: 295 us -> 331 us (1.12)
  starting transfers between devices: 85.7 us -> 104 us
  Pallas kernels: 124 us -> 133 us
  local copies, waits for them, and re-layouts: 14 us -> 20.9 us
  waiting for transfers between devices: 42.2 us -> 47.1 us
  blocking collectives: 26.2 us -> 22.2 us
    ppermute x12 -> x28, starting transfers between devices: 81.2 us -> 99.4 us  [send(): return lax.ppermute(x, 'head', routes)]
    unnamed x43 -> x87, local copies, waits for them, and re-layouts: 10.6 us -> 17.4 us
    pallas_call x4 -> x6, Pallas kernels: 60.3 us -> 65.5 us  [the longest x2 53.7 us: soft_quad(): pl.pallas_call(functools.partial(soft_quad_kernel, root), out_shape=[jax....]
    ppermute x12 -> x28, waiting for transfers between devices: 42.2 us -> 47.1 us  [send(): return lax.ppermute(x, 'head', routes)]
    all_to_all x1, blocking collectives: 26.2 us -> 22.2 us  [exchange(): return lax.all_to_all(x, AXES, split_axis=0, concat_axis=0, tiled=True)]
  transfers between devices with their start and end apart: 13 -> 29, of which waited for: 5 -> 6; matrix products, arithmetic and copies ran while one was open for 1% -> 1% of each run, Pallas kernels for 37% -> 34%
where the time goes in v1:
time: 331 us; the launch traced here: 329 us
  Pallas kernels  133 us (40%)
  starting transfers between devices  104 us (31%)
  waiting for transfers between devices  47.1 us (14%)
  blocking collectives  22.2 us (7%)
  local copies, waits for them, and re-layouts  20.9 us (6%)
    ppermute x28, starting transfers between devices, send(): return lax.ppermute(x, 'head', routes)  99.4 us
    pallas_call x2, Pallas kernels, soft_quad(): pl.pallas_call(functools.partial(soft_quad_kernel, root), out_shape=[jax....  53.7 us
    ppermute x28, waiting for transfers between devices, send(): return lax.ppermute(x, 'head', routes)  47.1 us
    pallas_call x3, Pallas kernels, local(): pl.pallas_call(functools.partial(local_kernel, count, first, skip, len(ol...  37.8 us
    all_to_all x1, blocking collectives, exchange(): return lax.all_to_all(x, AXES, split_axis=0, concat_axis=0, tiled=True)  22.2 us
    unnamed x87, local copies, waits for them, and re-layouts  17.4 us
    pallas_call x1, Pallas kernels, device_state(): pl.pallas_call(state_kernel, out_shape=[jax.ShapeDtypeStruct((pairs, BLOC...  14.8 us
    pallas_call x1, Pallas kernels, final(): pl.pallas_call(functools.partial(final_kernel, scale), out_shape=[jax.Sha...  13 us
  transfers between devices with their start and end apart: 29, of which 6 were waited for; matrix products, arithmetic and copies ran while one was open for 1% of the time, Pallas kernels for 34%

profile of v1, /device:TPU:0, one launch (start us, length us, event | category | flops | bytes accessed | tf_op | source)
XLA Modules:
  0.0 329.1 jit_solution(11329952118350220999)
XLA Ops:
  0.6 4.8 %pack.2 = (bf16[3,512,256]{2,1,0:T(8,128)(2,1)}, bf16[3,512,384]{2,1,0:T(8,128)(2,1)}, bf16[512,384]{1,0:T(8,128)(2,1)}, bf16[512,384]{1,0:T(8,128)(2,1)}, bf16[...) custom-call(s32[1]{0:T(128)} %bitcast.z_ref, bf16[512,2048]{1,0:T(8,128)(2,1)} %q_ref.7, bf16[512,2048]{1,0:T(8,128)(2,1)} %k_ref.8, ...), custom_call_target="tpu_custom_call" | custom-call | bytes 7864320 | tf_op jit(solution)/shard_map/pack/pallas_call | solution.py:243
  6.7 6.0 %collective-permute-start.2 = (bf16[512,384]{1,0:T(8,128)(2,1)}, bf16[512,384]{1,0:T(8,128)(2,1)S(1)}, u32[]{:S(2)}, u32[]{:S(2)}) collective-permute-start(bf16[512,384]{1,0:T(8,128)(2,1)} %get-tuple-element.48), channel_id=1, source_target_pairs={{0,2},{1,3},{4,6},{5,7},{8,10},{9,11},{12,14},{13,15},{16,18},{17,... | collective-permute-start | bytes 1179656 | tf_op jit(solution)/shard_map/ppermute | solution.py:259
  12.8 2.7 collective-permute-start.3
  15.4 4.8 %pack.3 = (bf16[3,512,256]{2,1,0:T(8,128)(2,1)}, bf16[3,512,384]{2,1,0:T(8,128)(2,1)}, bf16[512,384]{1,0:T(8,128)(2,1)}, bf16[512,384]{1,0:T(8,128)(2,1)}, bf16[...) custom-call(s32[1]{0:T(128)} %bitcast.z_ref, bf16[512,2048]{1,0:T(8,128)(2,1)} %q_ref.7, bf16[512,2048]{1,0:T(8,128)(2,1)} %k_ref.8, ...), custom_call_target="tpu_custom_call" | custom-call | bytes 7864320 | tf_op jit(solution)/shard_map/pack/pallas_call | solution.py:243
  21.5 4.6 %collective-permute-start.1 = (bf16[512,1024]{1,0:T(8,128)(2,1)S(1)}, bf16[512,1024]{1,0:T(8,128)(2,1)S(1)}, u32[]{:S(2)}, u32[]{:S(2)}) collective-permute-start(bf16[512,1024]{1,0:T(8,128)(2,1)S(1)} %copy-done.29), channel_id=1, source_target_pairs={{0,1},{4,5},{8,9},{12,13},{16,17},{20,21},{24,25},{28,29}} | collective-permute-start | bytes 3145736 | tf_op jit(solution)/shard_map/ppermute | solution.py:259
  27.5 2.6 collective-permute-done.20.key_two
  32.9 19.7 %collective-permute-start.16 = (bf16[512,384]{1,0:T(8,128)(2,1)}, bf16[512,384]{1,0:T(8,128)(2,1)S(1)}, u32[]{:S(2)}, u32[]{:S(2)}) collective-permute-start(bf16[512,384]{1,0:T(8,128)(2,1)} %get-tuple-element.62), channel_id=1, source_target_pairs={{0,2},{1,3},{4,6},{5,7},{8,10},{9,11},{12,14},{13,15},{16,18},{17,... | collective-permute-start | bytes 1179656 | tf_op jit(solution)/shard_map/ppermute | solution.py:259
  52.7 8.9 %collective-permute-done.16.key_c = bf16[512,384]{1,0:T(8,128)(2,1)S(1)} collective-permute-done((bf16[512,384]{1,0:T(8,128)(2,1)}, bf16[512,384]{1,0:T(8,128)(2,1)S(1)}, u32[]{:S(2)}, u32[]{:S(2)}) %collective-permute-start.16) | collective-permute-done | bytes 393248 | tf_op jit(solution)/shard_map/ppermute | solution.py:259
  62.3 8.3 %collective-permute-start.15 = (bf16[512,1024]{1,0:T(8,128)(2,1)}, bf16[512,1024]{1,0:T(8,128)(2,1)S(1)}, u32[]{:S(2)}, u32[]{:S(2)}) collective-permute-start(bf16[512,1024]{1,0:T(8,128)(2,1)} %get-tuple-element.61), channel_id=1, source_target_pairs={{0,1},{4,5},{8,9},{12,13},{16,17},{20,21},{24,25},{28,29}} | collective-permute-start | bytes 3145736 | tf_op jit(solution)/shard_map/ppermute | solution.py:259
  73.3 5.8 %collective-permute-start.17 = (bf16[512,384]{1,0:T(8,128)(2,1)}, bf16[512,384]{1,0:T(8,128)(2,1)S(1)}, u32[]{:S(2)}, u32[]{:S(2)}) collective-permute-start(bf16[512,384]{1,0:T(8,128)(2,1)} %get-tuple-element.63), channel_id=1, source_target_pairs={{0,3},{1,2},{4,7},{5,6},{8,11},{9,10},{12,15},{13,14},{16,19},{17,... | collective-permute-start | bytes 1179656 | tf_op jit(solution)/shard_map/ppermute | solution.py:259
  79.2 26.8 %soft.2 = (bf16[512,1024]{1,0:T(8,128)(2,1)}, bf16[512,384]{1,0:T(8,128)(2,1)}, bf16[512,384]{1,0:T(8,128)(2,1)}, bf16[512,384]{1,0:T(8,128)(2,1)}, bf16[512,256...) custom-call(s32[1]{0:T(128)} %bitcast.z_ref, s32[16,16]{1,0:T(8,128)} %flags.3, ...), custom_call_target="tpu_custom_call" | custom-call | flops 4294967296 | bytes 16777216 | tf_op jit(solution)/shard_map/soft/pallas_call | solution.py:496
  106.0 1.3 collective-permute-start.11
  107.3 8.5 %collective-permute-done.19.two_b = bf16[3,512,256]{2,1,0:T(8,128)(2,1)S(1)} collective-permute-done((bf16[3,512,256]{2,1,0:T(8,128)(2,1)}, bf16[3,512,256]{2,1,0:T(8,128)(2,1)S(1)}, u32[]{:S(2)}, u32[]{:S(2)}) %collective-permute-start.19) | collective-permute-done | bytes 786464 | tf_op jit(solution)/shard_map/ppermute | solution.py:259
  115.8 1.6 collective-permute-start.12
  117.4 1.3 collective-permute-start.13
  118.7 1.4 collective-permute-start.7
  121.2 26.9 %soft.3 = (bf16[512,1024]{1,0:T(8,128)(2,1)}, bf16[512,384]{1,0:T(8,128)(2,1)}, bf16[512,384]{1,0:T(8,128)(2,1)}, bf16[512,384]{1,0:T(8,128)(2,1)}, bf16[512,256...) custom-call(s32[1]{0:T(128)} %bitcast.z_ref, s32[16,16]{1,0:T(8,128)} %flags.3, ...), custom_call_target="tpu_custom_call" | custom-call | flops 4294967296 | bytes 16777216 | tf_op jit(solution)/shard_map/soft/pallas_call | solution.py:496
  148.2 1.3 collective-permute-start.25
  150.2 1.3 collective-permute-start.26
  158.4 3.1 collective-permute-done.26.two_b
  162.9 23.0 %collective-permute-done.8.three_d = bf16[512,384]{1,0:T(8,128)(2,1)S(1)} collective-permute-done((bf16[512,384]{1,0:T(8,128)(2,1)S(1)}, bf16[512,384]{1,0:T(8,128)(2,1)S(1)}, u32[]{:S(2)}, u32[]{:S(2)}) %collective-permute-start.8) | collective-permute-done | bytes 393248 | tf_op jit(solution)/shard_map/ppermute | solution.py:259
  190.8 1.4 collective-permute-start.24
  193.2 26.4 %collective-permute-start.27 = (bf16[512,256]{1,0:T(8,128)(2,1)}, bf16[512,256]{1,0:T(8,128)(2,1)}, u32[]{:S(2)}, u32[]{:S(2)}) collective-permute-start(bf16[512,256]{1,0:T(8,128)(2,1)} %get-tuple-element.73), channel_id=1, source_target_pairs={{0,1},{4,5},{8,9},{12,13},{16,17},{20,21},{24,25},{28,29}} | collective-permute-start | bytes 786440 | tf_op jit(solution)/shard_map/ppermute | solution.py:259
  220.4 14.8 %state.1 = (bf16[16,64,128]{2,1,0:T(8,128)(2,1)}, bf16[16,8,128]{2,1,0:T(8,128)(2,1)}, bf16[512,2048]{1,0:T(8,128)(2,1)}) custom-call(bf16[512,2048]{1,0:T(8,128)(2,1)} %q_ref.11, bf16[512,2048]{1,0:T(8,128)(2,1)} %k_ref.13, bf16[512,2048]{1,0:T(8,128)(2,1)} %v_ref.9, bf16[512,32]{1,0:T(8,128)(2,1)} %copy.43.d_ref), custom_call_target="tpu_custom_call" | custom-call | flops 1073741824 | bytes 8388608 | tf_op jit(solution)/shard_map/state/pallas_call | solution.py:632
  243.5 1.5 copy-done.1
  245.8 1.9 merge.3.refs_0_
  248.9 22.2 %all_to_all.10 = bf16[32,72,128]{2,1,0:T(8,128)(2,1)S(1)} all-to-all(bf16[32,72,128]{2,1,0:T(8,128)(2,1)S(1)} %maximum_maximum_fusion), channel_id=1, replica_groups=mesh['ctx'=8,'head'=4] {'ctx','head'}, dimensions={0} | all-to-all | bytes 1179648 | tf_op jit(solution)/shard_map/all_to_all | solution.py:927
  272.3 4.3 %all-to-all-start.1 = ((bf16[32,64,128]{2,1,0:T(8,128)(2,1)}), bf16[32,64,128]{2,1,0:T(8,128)(2,1)S(1)}, u32[]{:S(2)}, u32[]{:S(2)}) async-start(bf16[32,64,128]{2,1,0:T(8,128)(2,1)} %chain.1), calls=%async_computation.1 | async-start | bytes 1048576 | tf_op jit(solution)/shard_map/all_to_all | solution.py:927
  276.6 17.7 %local.3 = (f32[512,2048]{1,0:T(8,128)}, f32[512,2048]{1,0:T(8,128)}, f32[512,2048]{1,0:T(8,128)}, bf16[512,2048]{1,0:T(8,128)(2,1)}) custom-call(s32[1]{0:T(128)} %bitcast.z_ref, bf16[512,2048]{1,0:T(8,128)(2,1)} %q_ref.11, bf16[512,2048]{1,0:T(8,128)(2,1)} %k_ref.13, bf16[512,2048]{1,0:T(8,128)(2,1)} %v_ref.9, bf16[512,32]{1,0:T(8,128)(2,1)} %copy.43.d_ref, ...), custom_call_target="tpu_custom_call" | custom-call | flops 2684354560 | bytes 11534336 | tf_op jit(solution)/shard_map/local/pallas_call | solution.py:803
  294.3 10.1 %local.4 = (f32[512,2048]{1,0:T(8,128)}, f32[512,2048]{1,0:T(8,128)}, f32[512,2048]{1,0:T(8,128)}, bf16[512,2048]{1,0:T(8,128)(2,1)}) custom-call(s32[1]{0:T(128)} %bitcast.z_ref, bf16[512,2048]{1,0:T(8,128)(2,1)} %q_ref.11, bf16[512,2048]{1,0:T(8,128)(2,1)} %k_ref.13, ...), custom_call_target="tpu_custom_call", output_to_operand_aliasing={{0}: (6, {}), {1}: (7, {}), {2}: (8, {}), {3}: (9, {})} | custom-call | flops 1342177280 | bytes 5767168 | tf_op jit(solution)/shard_map/local/pallas_call | solution.py:803
  304.4 10.1 %local.5 = (f32[512,2048]{1,0:T(8,128)}, f32[512,2048]{1,0:T(8,128)}, f32[512,2048]{1,0:T(8,128)}, bf16[512,2048]{1,0:T(8,128)(2,1)}) custom-call(s32[1]{0:T(128)} %bitcast.z_ref, bf16[512,2048]{1,0:T(8,128)(2,1)} %q_ref.11, bf16[512,2048]{1,0:T(8,128)(2,1)} %k_ref.13, ...), custom_call_target="tpu_custom_call", output_to_operand_aliasing={{0}: (6, {}), {1}: (7, {}), {2}: (8, {}), {3}: (9, {})} | custom-call | flops 1342177280 | bytes 5767168 | tf_op jit(solution)/shard_map/local/pallas_call | solution.py:803
  316.0 13.0 %final.1 = (bf16[512,2048]{1,0:T(8,128)(2,1)}, bf16[512,2048]{1,0:T(8,128)(2,1)}, bf16[512,2048]{1,0:T(8,128)(2,1)}) custom-call(f32[512,2048]{1,0:T(8,128)} %get-tuple-element.82.pq_ref, f32[512,2048]{1,0:T(8,128)} %get-tuple-element.83.pk_ref, f32[512,2048]{1,0:T(8,128)} %get-tuple-element.84.pv_ref, bf16[512,2048]{1,0:T(8,128)(2,1)} %get-tuple-element.85.lit_ref, ...), custom_call_target="tpu_custom_call" | custom-call | flops 805306368 | bytes 25165824 | tf_op jit(solution)/shard_map/final/pallas_call | solution.py:858
  (147 shorter events, 39.4 us)
Async XLA Ops:
  5.4 20.8 %collective-permute-start.6 = (bf16[512,256]{1,0:T(8,128)(2,1)}, bf16[512,256]{1,0:T(8,128)(2,1)}, u32[]{:S(2)}, u32[]{:S(2)}) collective-permute-start(bf16[512,256]{1,0:T(8,128)(2,1)} %get-tuple-element.51), channel_id=1, source_target_pairs={{1,0},{5,4},{9,8},{13,12},{17,16},{21,20},{25,24},{29,28}} | collective-permute-start | bytes 786440 | tf_op jit(solution)/shard_map/ppermute | solution.py:259
  6.7 24.2 %collective-permute-start.2 = (bf16[512,384]{1,0:T(8,128)(2,1)}, bf16[512,384]{1,0:T(8,128)(2,1)S(1)}, u32[]{:S(2)}, u32[]{:S(2)}) collective-permute-start(bf16[512,384]{1,0:T(8,128)(2,1)} %get-tuple-element.48), channel_id=1, source_target_pairs={{0,2},{1,3},{4,6},{5,7},{8,10},{9,11},{12,14},{13,15},{16,18},{17,... | collective-permute-start | bytes 1179656 | tf_op jit(solution)/shard_map/ppermute | solution.py:259
  12.8 19.4 %collective-permute-start.3 = (bf16[512,384]{1,0:T(8,128)(2,1)}, bf16[512,384]{1,0:T(8,128)(2,1)S(1)}, u32[]{:S(2)}, u32[]{:S(2)}) collective-permute-start(bf16[512,384]{1,0:T(8,128)(2,1)} %get-tuple-element.49), channel_id=1, source_target_pairs={{0,3},{1,2},{4,7},{5,6},{8,11},{9,10},{12,15},{13,14},{16,19},{17,... | collective-permute-start | bytes 1179656 | tf_op jit(solution)/shard_map/ppermute | solution.py:259
  20.2 9.9 %collective-permute-start.20 = (bf16[512,256]{1,0:T(8,128)(2,1)}, bf16[512,256]{1,0:T(8,128)(2,1)S(1)}, u32[]{:S(2)}, u32[]{:S(2)}) collective-permute-start(bf16[512,256]{1,0:T(8,128)(2,1)} %get-tuple-element.65), channel_id=1, source_target_pairs={{1,0},{5,4},{9,8},{13,12},{17,16},{21,20},{25,24},{29,28}} | collective-permute-start | bytes 786440 | tf_op jit(solution)/shard_map/ppermute | solution.py:259
  21.5 50.4 %collective-permute-start.1 = (bf16[512,1024]{1,0:T(8,128)(2,1)S(1)}, bf16[512,1024]{1,0:T(8,128)(2,1)S(1)}, u32[]{:S(2)}, u32[]{:S(2)}) collective-permute-start(bf16[512,1024]{1,0:T(8,128)(2,1)S(1)} %copy-done.29), channel_id=1, source_target_pairs={{0,1},{4,5},{8,9},{12,13},{16,17},{20,21},{24,25},{28,29}} | collective-permute-start | bytes 3145736 | tf_op jit(solution)/shard_map/ppermute | solution.py:259
  26.2 36.1 %collective-permute-start.5 = (bf16[3,512,256]{2,1,0:T(8,128)(2,1)S(1)}, bf16[3,512,256]{2,1,0:T(8,128)(2,1)S(1)}, u32[]{:S(2)}, u32[]{:S(2)}) collective-permute-start(bf16[3,512,256]{2,1,0:T(8,128)(2,1)S(1)} %copy-done.32), channel_id=1, source_target_pairs={{3,0},{7,4},{11,8},{15,12},{19,16},{23,20},{27,24},{31,28}} | collective-permute-start | bytes 2359304 | tf_op jit(solution)/shard_map/ppermute | solution.py:259
  30.1 43.2 %collective-permute-start = (bf16[3,512,384]{2,1,0:T(8,128)(2,1)S(1)}, bf16[3,512,384]{2,1,0:T(8,128)(2,1)S(1)}, u32[]{:S(2)}, u32[]{:S(2)}) collective-permute-start(bf16[3,512,384]{2,1,0:T(8,128)(2,1)S(1)} %copy-done.25), channel_id=1, source_target_pairs={{3,2},{2,3},{7,6},{6,7},{11,10},{10,11},{15,14},{14,15},{19,18},{1... | collective-permute-start | bytes 3538952 | tf_op jit(solution)/shard_map/ppermute | solution.py:259
  30.8 39.8 %collective-permute-start.4 = (bf16[3,512,256]{2,1,0:T(8,128)(2,1)S(1)}, bf16[3,512,256]{2,1,0:T(8,128)(2,1)S(1)}, u32[]{:S(2)}, u32[]{:S(2)}) collective-permute-start(bf16[3,512,256]{2,1,0:T(8,128)(2,1)S(1)} %copy-done.32), channel_id=1, source_target_pairs={{2,0},{6,4},{10,8},{14,12},{18,16},{22,20},{26,24},{30,28}} | collective-permute-start | bytes 2359304 | tf_op jit(solution)/shard_map/ppermute | solution.py:259
  32.9 28.6 %collective-permute-start.16 = (bf16[512,384]{1,0:T(8,128)(2,1)}, bf16[512,384]{1,0:T(8,128)(2,1)S(1)}, u32[]{:S(2)}, u32[]{:S(2)}) collective-permute-start(bf16[512,384]{1,0:T(8,128)(2,1)} %get-tuple-element.62), channel_id=1, source_target_pairs={{0,2},{1,3},{4,6},{5,7},{8,10},{9,11},{12,14},{13,15},{16,18},{17,... | collective-permute-start | bytes 1179656 | tf_op jit(solution)/shard_map/ppermute | solution.py:259
  61.5 58.6 %collective-permute-start.14 = (bf16[3,512,384]{2,1,0:T(8,128)(2,1)}, bf16[3,512,384]{2,1,0:T(8,128)(2,1)S(1)}, u32[]{:S(2)}, u32[]{:S(2)}) collective-permute-start(bf16[3,512,384]{2,1,0:T(8,128)(2,1)} %get-tuple-element.60), channel_id=1, source_target_pairs={{3,2},{2,3},{7,6},{6,7},{11,10},{10,11},{15,14},{14,15},{19,18},{1... | collective-permute-start | bytes 3538952 | tf_op jit(solution)/shard_map/ppermute | solution.py:259
  62.3 56.3 %collective-permute-start.15 = (bf16[512,1024]{1,0:T(8,128)(2,1)}, bf16[512,1024]{1,0:T(8,128)(2,1)S(1)}, u32[]{:S(2)}, u32[]{:S(2)}) collective-permute-start(bf16[512,1024]{1,0:T(8,128)(2,1)} %get-tuple-element.61), channel_id=1, source_target_pairs={{0,1},{4,5},{8,9},{12,13},{16,17},{20,21},{24,25},{28,29}} | collective-permute-start | bytes 3145736 | tf_op jit(solution)/shard_map/ppermute | solution.py:259
  70.6 45.1 %collective-permute-start.19 = (bf16[3,512,256]{2,1,0:T(8,128)(2,1)}, bf16[3,512,256]{2,1,0:T(8,128)(2,1)S(1)}, u32[]{:S(2)}, u32[]{:S(2)}) collective-permute-start(bf16[3,512,256]{2,1,0:T(8,128)(2,1)} %get-tuple-element.64), channel_id=1, source_target_pairs={{3,0},{7,4},{11,8},{15,12},{19,16},{23,20},{27,24},{31,28}} | collective-permute-start | bytes 2359304 | tf_op jit(solution)/shard_map/ppermute | solution.py:259
  72.0 45.4 %collective-permute-start.18 = (bf16[3,512,256]{2,1,0:T(8,128)(2,1)}, bf16[3,512,256]{2,1,0:T(8,128)(2,1)S(1)}, u32[]{:S(2)}, u32[]{:S(2)}) collective-permute-start(bf16[3,512,256]{2,1,0:T(8,128)(2,1)} %get-tuple-element.64), channel_id=1, source_target_pairs={{2,0},{6,4},{10,8},{14,12},{18,16},{22,20},{26,24},{30,28}} | collective-permute-start | bytes 2359304 | tf_op jit(solution)/shard_map/ppermute | solution.py:259
  73.3 32.7 %collective-permute-start.17 = (bf16[512,384]{1,0:T(8,128)(2,1)}, bf16[512,384]{1,0:T(8,128)(2,1)S(1)}, u32[]{:S(2)}, u32[]{:S(2)}) collective-permute-start(bf16[512,384]{1,0:T(8,128)(2,1)} %get-tuple-element.63), channel_id=1, source_target_pairs={{0,3},{1,2},{4,7},{5,6},{8,11},{9,10},{12,15},{13,14},{16,19},{17,... | collective-permute-start | bytes 1179656 | tf_op jit(solution)/shard_map/ppermute | solution.py:259
  106.0 43.5 %collective-permute-start.11 = (bf16[512,256]{1,0:T(8,128)(2,1)}, bf16[512,256]{1,0:T(8,128)(2,1)S(1)}, u32[]{:S(2)}, u32[]{:S(2)}) collective-permute-start(bf16[512,256]{1,0:T(8,128)(2,1)} %get-tuple-element.57), channel_id=1, source_target_pairs={{0,2},{4,6},{8,10},{12,14},{16,18},{20,22},{24,26},{28,30}} | collective-permute-start | bytes 786440 | tf_op jit(solution)/shard_map/ppermute | solution.py:259
  115.8 35.7 %collective-permute-start.12 = (bf16[512,256]{1,0:T(8,128)(2,1)}, bf16[512,256]{1,0:T(8,128)(2,1)S(1)}, u32[]{:S(2)}, u32[]{:S(2)}) collective-permute-start(bf16[512,256]{1,0:T(8,128)(2,1)} %get-tuple-element.58), channel_id=1, source_target_pairs={{0,3},{4,7},{8,11},{12,15},{16,19},{20,23},{24,27},{28,31}} | collective-permute-start | bytes 786440 | tf_op jit(solution)/shard_map/ppermute | solution.py:259
  117.4 36.1 %collective-permute-start.13 = (bf16[512,256]{1,0:T(8,128)(2,1)}, bf16[512,256]{1,0:T(8,128)(2,1)S(1)}, u32[]{:S(2)}, u32[]{:S(2)}) collective-permute-start(bf16[512,256]{1,0:T(8,128)(2,1)} %get-tuple-element.59), channel_id=1, source_target_pairs={{0,1},{4,5},{8,9},{12,13},{16,17},{20,21},{24,25},{28,29}} | collective-permute-start | bytes 786440 | tf_op jit(solution)/shard_map/ppermute | solution.py:259
  118.7 38.4 %copy-start.36 = (bf16[512,384]{1,0:T(8,128)(2,1)S(1)}, bf16[512,384]{1,0:T(8,128)(2,1)}, u32[]{:S(2)}) copy-start(bf16[512,384]{1,0:T(8,128)(2,1)} %get-tuple-element.55) | copy-start | bytes 1179652
  118.7 43.5 %copy-start.35 = (bf16[512,384]{1,0:T(8,128)(2,1)S(1)}, bf16[512,384]{1,0:T(8,128)(2,1)}, u32[]{:S(2)}) copy-start(bf16[512,384]{1,0:T(8,128)(2,1)} %get-tuple-element.56) | copy-start | bytes 1179652
  118.7 100.9 %copy-start.23 = (bf16[512,32]{0,1:T(8,128)(2,1)S(1)}, bf16[512,32]{0,1:T(8,128)(2,1)}, u32[]{:S(2)}) copy-start(bf16[512,32]{0,1:T(8,128)(2,1)} %param.14) | copy-start | bytes 98308
  118.7 73.5 %collective-permute-start.7 = (bf16[512,1024]{1,0:T(8,128)(2,1)}, bf16[512,1024]{1,0:T(8,128)(2,1)S(1)}, u32[]{:S(2)}, u32[]{:S(2)}) collective-permute-start(bf16[512,1024]{1,0:T(8,128)(2,1)} %get-tuple-element.53), channel_id=1, source_target_pairs={{1,0},{5,4},{9,8},{13,12},{17,16},{21,20},{25,24},{29,28}} | collective-permute-start | bytes 3145736 | tf_op jit(solution)/shard_map/ppermute | solution.py:259
  148.2 8.3 %collective-permute-start.25 = (bf16[512,256]{1,0:T(8,128)(2,1)}, bf16[512,256]{1,0:T(8,128)(2,1)S(1)}, u32[]{:S(2)}, u32[]{:S(2)}) collective-permute-start(bf16[512,256]{1,0:T(8,128)(2,1)} %get-tuple-element.71), channel_id=1, source_target_pairs={{0,2},{4,6},{8,10},{12,14},{16,18},{20,22},{24,26},{28,30}} | collective-permute-start | bytes 786440 | tf_op jit(solution)/shard_map/ppermute | solution.py:259
  150.2 11.4 %collective-permute-start.26 = (bf16[512,256]{1,0:T(8,128)(2,1)}, bf16[512,256]{1,0:T(8,128)(2,1)S(1)}, u32[]{:S(2)}, u32[]{:S(2)}) collective-permute-start(bf16[512,256]{1,0:T(8,128)(2,1)} %get-tuple-element.72), channel_id=1, source_target_pairs={{0,3},{4,7},{8,11},{12,15},{16,19},{20,23},{24,27},{28,31}} | collective-permute-start | bytes 786440 | tf_op jit(solution)/shard_map/ppermute | solution.py:259
  152.2 93.5 %collective-permute-start.21 = (bf16[512,1024]{1,0:T(8,128)(2,1)}, bf16[512,1024]{1,0:T(8,128)(2,1)}, u32[]{:S(2)}, u32[]{:S(2)}) collective-permute-start(bf16[512,1024]{1,0:T(8,128)(2,1)} %get-tuple-element.67), channel_id=1, source_target_pairs={{1,0},{5,4},{9,8},{13,12},{17,16},{21,20},{25,24},{29,28}} | collective-permute-start | bytes 3145736 | tf_op jit(solution)/shard_map/ppermute | solution.py:259
  154.2 31.7 %collective-permute-start.8 = (bf16[512,384]{1,0:T(8,128)(2,1)S(1)}, bf16[512,384]{1,0:T(8,128)(2,1)S(1)}, u32[]{:S(2)}, u32[]{:S(2)}) collective-permute-start(bf16[512,384]{1,0:T(8,128)(2,1)S(1)} %copy-done.37), channel_id=1, source_target_pairs={{2,0},{3,1},{6,4},{7,5},{10,8},{11,9},{14,12},{15,13},{18,16},{19,... | collective-permute-start | bytes 1179656 | tf_op jit(solution)/shard_map/ppermute | solution.py:259
  157.1 30.8 %collective-permute-start.9 = (bf16[512,384]{1,0:T(8,128)(2,1)S(1)}, bf16[512,384]{1,0:T(8,128)(2,1)S(1)}, u32[]{:S(2)}, u32[]{:S(2)}) collective-permute-start(bf16[512,384]{1,0:T(8,128)(2,1)S(1)} %copy-done.36), channel_id=1, source_target_pairs={{2,1},{3,0},{6,5},{7,4},{10,9},{11,8},{14,13},{15,12},{18,17},{19,... | collective-permute-start | bytes 1179656 | tf_op jit(solution)/shard_map/ppermute | solution.py:259
  162.3 27.8 %collective-permute-start.10 = (bf16[512,384]{1,0:T(8,128)(2,1)S(1)}, bf16[512,384]{1,0:T(8,128)(2,1)S(1)}, u32[]{:S(2)}, u32[]{:S(2)}) collective-permute-start(bf16[512,384]{1,0:T(8,128)(2,1)S(1)} %copy-done.35), channel_id=1, source_target_pairs={{2,3},{3,2},{6,7},{7,6},{10,11},{11,10},{14,15},{15,14},{18,19},{1... | collective-permute-start | bytes 1179656 | tf_op jit(solution)/shard_map/ppermute | solution.py:259
  186.7 59.0 %collective-permute-start.22 = (bf16[512,384]{1,0:T(8,128)(2,1)}, bf16[512,384]{1,0:T(8,128)(2,1)S(1)}, u32[]{:S(2)}, u32[]{:S(2)}) collective-permute-start(bf16[512,384]{1,0:T(8,128)(2,1)} %get-tuple-element.68), channel_id=1, source_target_pairs={{2,0},{3,1},{6,4},{7,5},{10,8},{11,9},{14,12},{15,13},{18,16},{19,... | collective-permute-start | bytes 1179656 | tf_op jit(solution)/shard_map/ppermute | solution.py:259
  188.7 56.9 %collective-permute-start.23 = (bf16[512,384]{1,0:T(8,128)(2,1)}, bf16[512,384]{1,0:T(8,128)(2,1)}, u32[]{:S(2)}, u32[]{:S(2)}) collective-permute-start(bf16[512,384]{1,0:T(8,128)(2,1)} %get-tuple-element.69), channel_id=1, source_target_pairs={{2,1},{3,0},{6,5},{7,4},{10,9},{11,8},{14,13},{15,12},{18,17},{19,... | collective-permute-start | bytes 1179656 | tf_op jit(solution)/shard_map/ppermute | solution.py:259
  190.8 54.9 %collective-permute-start.24 = (bf16[512,384]{1,0:T(8,128)(2,1)}, bf16[512,384]{1,0:T(8,128)(2,1)}, u32[]{:S(2)}, u32[]{:S(2)}) collective-permute-start(bf16[512,384]{1,0:T(8,128)(2,1)} %get-tuple-element.70), channel_id=1, source_target_pairs={{2,3},{3,2},{6,7},{7,6},{10,11},{11,10},{14,15},{15,14},{18,19},{1... | collective-permute-start | bytes 1179656 | tf_op jit(solution)/shard_map/ppermute | solution.py:259
  193.2 52.4 %collective-permute-start.27 = (bf16[512,256]{1,0:T(8,128)(2,1)}, bf16[512,256]{1,0:T(8,128)(2,1)}, u32[]{:S(2)}, u32[]{:S(2)}) collective-permute-start(bf16[512,256]{1,0:T(8,128)(2,1)} %get-tuple-element.73), channel_id=1, source_target_pairs={{0,1},{4,5},{8,9},{12,13},{16,17},{20,21},{24,25},{28,29}} | collective-permute-start | bytes 786440 | tf_op jit(solution)/shard_map/ppermute | solution.py:259
  272.3 42.1 %all-to-all-start.1 = ((bf16[32,64,128]{2,1,0:T(8,128)(2,1)}), bf16[32,64,128]{2,1,0:T(8,128)(2,1)S(1)}, u32[]{:S(2)}, u32[]{:S(2)}) async-start(bf16[32,64,128]{2,1,0:T(8,128)(2,1)} %chain.1), calls=%async_computation.1 | async-start | bytes 1048576 | tf_op jit(solution)/shard_map/all_to_all | solution.py:927
  (40 other events, 256.8 us)

commit v2 on v1

--- a/solution.py
+++ b/solution.py
@@ -200,14 +200,14 @@
     )(here, flags, *pieces)
 
 
-OWNED = ((0, 1), (), (2, 3, 4), (5, 6, 7))
+OWNED = ((), (0, 1), (2, 3, 4), (5, 6, 7))
 SHARE = 8
 UNROLLS = {2: (4, 2, 1), 3: (4, 2, 1), 8: (2, 1)}
 
 
 def pack_quad_kernel(z_ref, *refs):
-    ins, outs = refs[:21], refs[21:]
-    two, three, key_c, key_d, key_all, key_two = outs
+    ins, outs = refs[:19], refs[19:]
+    two, three, key_c, key_d, key_all = outs
     for n in range(3):
         two[n] = ins[n][...]
         for p in range(3):
@@ -215,7 +215,6 @@
         key_c[:, n * BLOCK : (n + 1) * BLOCK] = ins[12 + n][...]
         key_d[:, n * BLOCK : (n + 1) * BLOCK] = ins[15 + n][...]
     key_all[...] = ins[18][...]
-    key_two[...] = ins[19][...]
 
 
 def pack_quad(here, arrays, chunk):
@@ -229,16 +228,15 @@
         return spec(lambda z: 5 - 3 * lax.div(z, 3) + p)
 
     front = pl.BlockSpec((rows, 2 * BLOCK), lambda i, z: (0, SHARE // 2 * chunk))
-    operands = list(arrays) + [array for array in arrays for _ in range(3)] + [key] * 9
+    operands = list(arrays) + [array for array in arrays for _ in range(3)] + [key] * 7
     specs = [front] * 3
     specs += [far(p) for p in range(3)] * 3
     specs += [spec(lambda z, p=p: 2 + 3 * jnp.minimum(z, 1) + p) for p in range(3)]
     specs += [spec(lambda z, p=p: 5 - 3 * jnp.minimum(z, 1) + p) for p in range(3)]
     specs += [pl.BlockSpec((rows, SHARE * BLOCK), lambda i, z: (0, chunk))]
-    specs += [front] * 2
     shapes = [
         (3, rows, 2 * BLOCK), (3, rows, 3 * BLOCK), (rows, 3 * BLOCK), (rows, 3 * BLOCK),
-        (rows, SHARE * BLOCK), (rows, 2 * BLOCK),
+        (rows, SHARE * BLOCK),
     ]
     return pl.pallas_call(
         pack_quad_kernel,
@@ -260,28 +258,27 @@
 
 
 def turn_in(pieces):
-    two, three, key_c, key_d, key_all, key_two = pieces
+    two, three, key_c, key_d, key_all = pieces
+    key_all = send(key_all, (0, 1))
     return (
+        key_all,
         send(three, (3, 2), (2, 3)),
-        send(key_all, (0, 1)),
         send(key_c, (0, 2), (1, 3)),
         send(key_d, (0, 3), (1, 2)),
-        send(two, (2, 0)),
-        send(two, (3, 0)),
-        send(key_two, (1, 0)),
+        send(two, (2, 1)),
+        send(two, (3, 1)),
     )
 
 
 def turn_out(pieces):
-    wide, three_d, three_e, three_f, two_a, two_b, two_c = pieces
+    three_d, three_e, three_f, two_a, two_b, two_c = pieces
     return (
-        send(wide, (1, 0)),
         send(three_d, (2, 0), (3, 1)),
         send(three_e, (2, 1), (3, 0)),
         send(three_f, (2, 3), (3, 2)),
-        send(two_a, (0, 2)),
-        send(two_b, (0, 3)),
-        send(two_c, (0, 1)),
+        send(two_a, (1, 2)),
+        send(two_b, (1, 3)),
+        send(two_c, (1, 0)),
     )
 
 
@@ -366,14 +363,99 @@
         done = done + unroll * turns
 
 
-def soft_quad_kernel(root, z_ref, flags, q_ref, k_ref, u_ref, three, key_all, key_c, key_d, two_a, two_b, key_two, *refs):
-    outs, (queries, keys, cotans, summed, near, summed_near, scores, tops, listed) = refs[:8], refs[8:]
-    wide, three_d, three_e, three_f, out_a, out_b, out_c, mine = outs
+def near_kernel(root, z_ref, flags, q_ref, k_ref, u_ref, key_all, wide, mine, near, summed, scores, tops, listed):
     rows = q_ref.shape[0]
     per = rows // BLOCK
     z = z_ref[0]
     root = jnp.asarray(root, BF)
-    summed[...] = jnp.zeros_like(summed)
+    upper, lower = slice(0, rows), slice(rows, 2 * rows)
+
+    @pl.when(z == 0)
+    def _():
+        near[upper, :] = k_ref[...]
+
+    @pl.when(z == 1)
+    def _():
+        near[upper, :] = key_all[...]
+        near[lower, :] = k_ref[...]
+
+    @pl.when(z < 2)
+    def _():
+        summed[...] = jnp.zeros_like(summed)
+
+        def query_block(n, _):
+            at = rows_of(n)
+
+            def side(p):
+                return slice(p * BLOCK, (p + 1) * BLOCK)
+
+            def add(j, p, x):
+                summed[rows_of(j), side(p)] += x
+
+            attend(
+                n + z * per,
+                [split_pair(q_ref[at, side(p)] * root) for p in range(SHARE)],
+                [split_pair(u_ref[at, side(p)]) for p in range(SHARE)],
+                lambda j, p: near[rows_of(j), side(p)],
+                add, flags, scores, tops, listed,
+            )
+            return 0
+
+        lax.fori_loop(0, per, query_block, 0)
+
+    @pl.when(z == 0)
+    def _():
+        mine[...] = summed[upper, :]
+
+    @pl.when(z == 1)
+    def _():
+        wide[...] = summed[upper, :].astype(BF)
+        mine[...] = summed[lower, :]
+
+
+def whole(shape):
+    return pl.BlockSpec(shape, lambda i, z, f, n=len(shape): (0,) * n, pipeline_mode=pl.Buffered(1))
+
+
+def own_columns(rows, chunk):
+    return pl.BlockSpec((rows, SHARE * BLOCK), lambda i, z, f: (0, chunk), pipeline_mode=pl.Buffered(1))
+
+
+def soft_near(here, flags, arrays, key_all, root, chunk):
+    rows = arrays[0].shape[0]
+    shape = (rows, SHARE * BLOCK)
+    blocks = 2 * rows // BLOCK
+    return pl.pallas_call(
+        functools.partial(near_kernel, root),
+        out_shape=[jax.ShapeDtypeStruct(shape, BF), jax.ShapeDtypeStruct(shape, F32)],
+        grid_spec=pltpu.PrefetchScalarGridSpec(
+            num_scalar_prefetch=2,
+            grid=(1,),
+            in_specs=[own_columns(rows, chunk)] * 3 + [whole(shape)],
+            out_specs=[whole(shape)] * 2,
+            scratch_shapes=[
+                pltpu.VMEM((2 * rows, SHARE * BLOCK), BF),
+                pltpu.VMEM((2 * rows, SHARE * BLOCK), F32),
+                pltpu.VMEM((SHARE, blocks, BLOCK // 8, 8, 2 * BLOCK), F32),
+                pltpu.VMEM((SHARE, blocks, 8, 2 * BLOCK), F32),
+                pltpu.SMEM((blocks + 1,), jnp.int32),
+            ],
+        ),
+        compiler_params=params(),
+        cost_estimate=pl.CostEstimate(
+            flops=8 * rows * rows * SHARE * BLOCK, transcendentals=2 * rows * rows * SHARE, bytes_accessed=16 * rows * SHARE * BLOCK
+        ),
+        name="near",
+    )(here, flags, *arrays, key_all)
+
+
+def far_kernel(root, z_ref, flags, q_ref, k_ref, u_ref, key_all, three, key_c, key_d, two_a, two_b, *refs):
+    outs, (queries, keys, cotans, summed, scores, tops, listed) = refs[:7], refs[7:]
+    three_d, three_e, three_f, out_a, out_b, out_c, mine = outs
+    rows = q_ref.shape[0]
+    per = rows // BLOCK
+    z = z_ref[0]
+    root = jnp.asarray(root, BF)
 
     def part(n):
         return slice(n * rows, (n + 1) * rows)
@@ -386,23 +468,20 @@
         keys[part(2 + n), :width] = k
         cotans[part(n), :width] = u
 
-    for me in range(4):
+    def own_of(me):
+        pairs = len(OWNED[me])
+        return pairs * BLOCK, slice(OWNED[me][0] * BLOCK, (OWNED[me][0] + pairs) * BLOCK)
+
+    for me in range(1, 4):
 
         @pl.when(z == me)
         def _(me=me):
+            width, own = own_of(me)
             if me == 1:
-                near[part(0), :] = key_all[...]
-                near[part(1), :] = k_ref[...]
-                return
-            pairs = len(OWNED[me])
-            width = pairs * BLOCK
-            own = slice(OWNED[me][0] * BLOCK, (OWNED[me][0] + pairs) * BLOCK)
-            if me == 0:
                 place(0, two_a[0], two_a[1], two_a[2], width)
                 place(1, two_b[0], two_b[1], two_b[2], width)
-                keys[part(0), :width] = k_ref[:, own]
-                keys[part(1), :width] = key_two[...]
-                near[part(0), :] = k_ref[...]
+                keys[part(0), :width] = key_all[:, own]
+                keys[part(1), :width] = k_ref[:, own]
             else:
                 place(me - 2, q_ref[:, own], k_ref[:, own], u_ref[:, own], width)
                 place(3 - me, three[0], three[1], three[2], width)
@@ -410,6 +489,8 @@
                 keys[part(1), :width] = (key_d if me == 2 else key_c)[...]
 
     def far_rows(pairs):
+        summed[...] = jnp.zeros_like(summed)
+
         def query_block(n, _):
             at = rows_of(n)
 
@@ -431,144 +512,97 @@
     def _():
         far_rows(3)
 
-    @pl.when(z == 0)
+    @pl.when(z == 1)
     def _():
         far_rows(2)
 
-    @pl.when(z < 2)
-    def _():
-        summed_near[...] = jnp.zeros_like(summed_near)
-
-        def near_block(n, _):
-            group, block = n // per, lax.rem(n, per)
-            at = rows_of(block)
-
-            def side(p):
-                return pl.ds(pl.multiple_of((8 * group + p) * BLOCK, BLOCK), BLOCK)
-
-            def add(j, p, x):
-                summed_near[rows_of(j), side(p)] += x
-
-            attend(
-                block + z * per,
-                [split_pair(q_ref[at, side(p)] * root) for p in range(8)],
-                [split_pair(u_ref[at, side(p)]) for p in range(8)],
-                lambda j, p: near[rows_of(j), side(p)],
-                add, flags, scores, tops, listed,
-            )
-            return 0
-
-        lax.fori_loop(0, per * (SHARE // 8), near_block, 0)
-
-    for me in range(4):
+    for me in range(1, 4):
 
         @pl.when(z == me)
         def _(me=me):
+            width, _ = own_of(me)
+            mine[:, :width] = summed[part(me), :width]
             if me == 1:
-                wide[...] = summed_near[part(0), :].astype(BF)
-                mine[...] = summed_near[part(1), :]
-                return
-            pairs = len(OWNED[me])
-            width = pairs * BLOCK
-            own = slice(OWNED[me][0] * BLOCK, (OWNED[me][0] + pairs) * BLOCK)
-            if me == 0:
-                out_c[...] = summed[part(1), :width].astype(BF)
+                out_c[...] = summed[part(0), :width].astype(BF)
                 out_a[...] = summed[part(2), :width].astype(BF)
                 out_b[...] = summed[part(3), :width].astype(BF)
-                mine[...] = summed_near[part(0), :]
-                mine[:, own] += summed[part(0), :width]
             else:
                 three_d[...] = summed[part(me - 2), :].astype(BF)
                 three_e[...] = summed[part(3 - me), :].astype(BF)
                 three_f[...] = summed[part(5 - me), :].astype(BF)
-                mine[:, own] = summed[part(me), :]
-
-
-def soft_quad(here, flags, arrays, pieces, root, chunk):
+
+
+def soft_far(here, flags, arrays, pieces, root, chunk):
     rows = arrays[0].shape[0]
     span = 4 * rows
-
-    def whole(shape):
-        return pl.BlockSpec(shape, lambda i, z, f, n=len(shape): (0,) * n, pipeline_mode=pl.Buffered(1))
-
-    column = pl.BlockSpec((rows, SHARE * BLOCK), lambda i, z, f: (0, chunk), pipeline_mode=pl.Buffered(1))
-    shapes = [(rows, SHARE * BLOCK)] + [(rows, 3 * BLOCK)] * 3 + [(rows, 2 * BLOCK)] * 3 + [(rows, SHARE * BLOCK)]
+    shapes = [(rows, 3 * BLOCK)] * 3 + [(rows, 2 * BLOCK)] * 3
+    last = (rows, 3 * BLOCK)
     return pl.pallas_call(
-        functools.partial(soft_quad_kernel, root),
-        out_shape=[jax.ShapeDtypeStruct(shape, BF) for shape in shapes[:-1]]
-        + [jax.ShapeDtypeStruct(shapes[-1], F32)],
+        functools.partial(far_kernel, root),
+        out_shape=[jax.ShapeDtypeStruct(shape, BF) for shape in shapes] + [jax.ShapeDtypeStruct(last, F32)],
         grid_spec=pltpu.PrefetchScalarGridSpec(
             num_scalar_prefetch=2,
             grid=(1,),
-            in_specs=[column] * 3 + [whole(piece.shape) for piece in pieces],
-            out_specs=[whole(shape) for shape in shapes],
+            in_specs=[own_columns(rows, chunk)] * 3 + [whole(piece.shape) for piece in pieces],
+            out_specs=[whole(shape) for shape in shapes + [last]],
             scratch_shapes=[
                 pltpu.VMEM((2 * rows, 3 * BLOCK), BF),
                 pltpu.VMEM((span, 3 * BLOCK), BF),
                 pltpu.VMEM((2 * rows, 3 * BLOCK), BF),
                 pltpu.VMEM((span, 3 * BLOCK), F32),
-                pltpu.VMEM((2 * rows, SHARE * BLOCK), BF),
-                pltpu.VMEM((2 * rows, SHARE * BLOCK), F32),
-                pltpu.VMEM((8, span // BLOCK, BLOCK // 8, 8, 2 * BLOCK), F32),
-                pltpu.VMEM((8, span // BLOCK, 8, 2 * BLOCK), F32),
+                pltpu.VMEM((3, span // BLOCK, BLOCK // 8, 8, 2 * BLOCK), F32),
+                pltpu.VMEM((3, span // BLOCK, 8, 2 * BLOCK), F32),
                 pltpu.SMEM((span // BLOCK + 1,), jnp.int32),
             ],
         ),
-        compiler_params=params(56),
+        compiler_params=params(),
         cost_estimate=pl.CostEstimate(
             flops=8 * span * span * BLOCK, transcendentals=2 * span * span, bytes_accessed=64 * span * BLOCK
         ),
-        name="soft",
+        name="far",
     )(here, flags, *arrays, *pieces)
 
 
-def merge_kernel(z_ref, mine, wide, three_d, three_e, three_f, two_a, two_b, two_c, lit_ref):
+def merge_kernel(z_ref, near, far, wide, three_d, three_e, three_f, two_a, two_b, two_c, lit_ref):
     z = z_ref[0]
     first = slice(0, 2 * BLOCK)
     third, fourth = slice(2 * BLOCK, 5 * BLOCK), slice(5 * BLOCK, 8 * BLOCK)
 
-    def plus(at, x):
-        lit_ref[:, at] = (mine[:, at] + x.astype(F32)).astype(BF)
-
-    def keep(at):
-        lit_ref[:, at] = mine[:, at].astype(BF)
-
     @pl.when(z == 0)
     def _():
-        plus(first, wide[:, first])
-        plus(third, wide[:, third].astype(F32) + three_d[...].astype(F32))
-        plus(fourth, wide[:, fourth].astype(F32) + three_e[...].astype(F32))
+        for at, x in ((first, two_c), (third, three_d), (fourth, three_e)):
+            lit_ref[:, at] = (near[:, at] + wide[:, at].astype(F32) + x[...].astype(F32)).astype(BF)
 
     @pl.when(z == 1)
     def _():
-        plus(first, two_c[...])
-        plus(third, three_e[...])
-        plus(fourth, three_d[...])
+        lit_ref[:, first] = (near[:, first] + far[:, first]).astype(BF)
+        lit_ref[:, third] = (near[:, third] + three_e[...].astype(F32)).astype(BF)
+        lit_ref[:, fourth] = (near[:, fourth] + three_d[...].astype(F32)).astype(BF)
 
     @pl.when(z == 2)
     def _():
         lit_ref[:, first] = two_a[...]
-        keep(third)
+        lit_ref[:, third] = far[...].astype(BF)
         lit_ref[:, fourth] = three_f[...]
 
     @pl.when(z == 3)
     def _():
         lit_ref[:, first] = two_b[...]
         lit_ref[:, third] = three_f[...]
-        keep(fourth)
-
-
-def merge(here, mine, pieces):
+        lit_ref[:, fourth] = far[...].astype(BF)
+
+
+def merge(here, near, far, wide, pieces):
     vmem = pl.BlockSpec(memory_space=pltpu.VMEM)
     return pl.pallas_call(
         merge_kernel,
-        out_shape=jax.ShapeDtypeStruct(mine.shape, BF),
-        in_specs=[pl.BlockSpec(memory_space=pltpu.SMEM)] + [vmem] * 8,
+        out_shape=jax.ShapeDtypeStruct(near.shape, BF),
+        in_specs=[pl.BlockSpec(memory_space=pltpu.SMEM)] + [vmem] * 9,
         out_specs=vmem,
         compiler_params=params(24),
-        cost_estimate=pl.CostEstimate(flops=4 * mine.size, transcendentals=0, bytes_accessed=10 * mine.size),
+        cost_estimate=pl.CostEstimate(flops=4 * near.size, transcendentals=0, bytes_accessed=10 * near.size),
         name="merge",
-    )(here, mine, *pieces)
+    )(here, near, far, wide, *pieces)
 
 
 def triangle():
@@ -903,17 +937,23 @@
         else:
             pieces = pack(here, arrays, c, count, per * BLOCK)
         packed.append(turn_in(pieces) if quad else turn(pieces, count))
+    near, wide = [], []
+    if quad:
+        for c in range(chunks):
+            sent, kept = soft_near(here, block_mask, arrays, packed[c][0], root, c)
+            near.append(kept)
+            wide.append(send(sent, (1, 0)))
     sums, totals, scaled = device_state(light_query, light_key, light_value, decays, pairs)
 
     parts, reaches = (), []
     for c in range(chunks):
         if quad:
-            *lits, mine = soft_quad(here, block_mask, arrays, packed[c], root, c)
+            *lits, far = soft_far(here, block_mask, arrays, packed[c], root, c)
         else:
             lits = soft(here, block_mask, packed[c], root)
         lits = turn_out(lits) if quad else turn(lits, count)
         if quad:
-            lits = (merge(here, mine, lits),)
+            lits = (merge(here, near[c], far, wide[c], lits),)
         reaches.append(device_reach(here, scaled, lits, c))
         first, many = c * count * per, count * per
         cuts = (0, many // 2, many) if c == chunks - 1 else (0, many)

time: 331 us -> 318 us (0.961)
  starting transfers between devices: 104 us -> 66.3 us
  waiting for transfers between devices: 47.1 us -> 84.8 us
  Pallas kernels: 133 us -> 103 us
  blocking collectives: 22.2 us -> 39.3 us
    ppermute x28 -> x26, waiting for transfers between devices: 47.1 us -> 84.8 us  [send(): return lax.ppermute(x, 'head', routes)]
    ppermute x28 -> x26, starting transfers between devices: 99.4 us -> 62.1 us  [send(): return lax.ppermute(x, 'head', routes)]
    pallas_call x4 -> x6, Pallas kernels: 56 us -> 26 us  [the longest x2 16.9 us: soft_near(): pl.pallas_call(functools.partial(near_kernel, root), out_shape=[jax.Shape...]
    all_to_all x1, blocking collectives: 22.2 us -> 39.3 us  [exchange(): return lax.all_to_all(x, AXES, split_axis=0, concat_axis=0, tiled=True)]
    unnamed x87 -> x63, local copies, waits for them, and re-layouts: 17.4 us -> 18.4 us
  transfers between devices with their start and end apart: 29 -> 27, of which waited for: 6 -> 8; matrix products, arithmetic and copies ran while one was open for 1% -> 1% of each run, Pallas kernels for 34% -> 26%
where the time goes in v2:
time: 318 us; the launch traced here: 317 us
  Pallas kernels  103 us (32%)
  waiting for transfers between devices  84.8 us (27%)
  starting transfers between devices  66.3 us (21%)
  blocking collectives  39.3 us (12%)
  local copies, waits for them, and re-layouts  21.9 us (7%)
    ppermute x26, waiting for transfers between devices, send(): return lax.ppermute(x, 'head', routes)  84.8 us
    ppermute x26, starting transfers between devices, send(): return lax.ppermute(x, 'head', routes)  62.1 us
    all_to_all x1, blocking collectives, exchange(): return lax.all_to_all(x, AXES, split_axis=0, concat_axis=0, tiled=True)  39.3 us
    pallas_call x3, Pallas kernels, local(): pl.pallas_call(functools.partial(local_kernel, count, first, skip, len(ol...  37.8 us
    unnamed x63, local copies, waits for them, and re-layouts  18.4 us
    pallas_call x2, Pallas kernels, soft_near(): pl.pallas_call(functools.partial(near_kernel, root), out_shape=[jax.Shape...  16.9 us
    pallas_call x1, Pallas kernels, device_state(): pl.pallas_call(state_kernel, out_shape=[jax.ShapeDtypeStruct((pairs, BLOC...  14.7 us
    pallas_call x1, Pallas kernels, final(): pl.pallas_call(functools.partial(final_kernel, scale), out_shape=[jax.Sha...  13 us
  transfers between devices with their start and end apart: 27, of which 8 were waited for; matrix products, arithmetic and copies ran while one was open for 1% of the time, Pallas kernels for 26%

profile of v2, /device:TPU:0, one launch (start us, length us, event | category | flops | bytes accessed | tf_op | source)
XLA Modules:
  0.0 316.6 jit_solution(6133847361907585387)
XLA Ops:
  0.6 4.5 %pack.3 = (bf16[3,512,256]{2,1,0:T(8,128)(2,1)}, bf16[3,512,384]{2,1,0:T(8,128)(2,1)}, bf16[512,384]{1,0:T(8,128)(2,1)}, bf16[512,384]{1,0:T(8,128)(2,1)}, bf16[512,1024]{1,0:T(8,128)(2,1)}) custom-call(s32[1]{0:T(128)} %bitcast.z_ref, bf16[512,2048]{1,0:T(8,128)(2,1)} %q_ref.11, bf16[512,2048]{1,0:T(8,128)(2,1)} %k_ref.12, bf16[512,2048]{1,0:T(8,128)(2,1)} %u_ref.7, ...), custom_call_target="tpu_custom_call" | custom-call | bytes 7864320 | tf_op jit(solution)/shard_map/pack/pallas_call | solution.py:241
  5.1 6.0 %collective-permute-start.15 = (bf16[512,384]{1,0:T(8,128)(2,1)}, bf16[512,384]{1,0:T(8,128)(2,1)S(1)}, u32[]{:S(2)}, u32[]{:S(2)}) collective-permute-start(bf16[512,384]{1,0:T(8,128)(2,1)} %get-tuple-element.63), channel_id=1, source_target_pairs={{0,2},{1,3},{4,6},{5,7},{8,10},{9,11},{12,14},{13,15},{16,18},{17,... | collective-permute-start | bytes 1179656 | tf_op jit(solution)/shard_map/ppermute | solution.py:257
  11.1 2.2 collective-permute-start.16
  13.3 2.6 collective-permute-start.13
  16.6 1.7 collective-permute-start.14
  18.4 2.6 collective-permute-done.15.key_c
  21.6 4.4 %pack.2 = (bf16[3,512,256]{2,1,0:T(8,128)(2,1)}, bf16[3,512,384]{2,1,0:T(8,128)(2,1)}, bf16[512,384]{1,0:T(8,128)(2,1)}, bf16[512,384]{1,0:T(8,128)(2,1)}, bf16[512,1024]{1,0:T(8,128)(2,1)}) custom-call(s32[1]{0:T(128)} %bitcast.z_ref, bf16[512,2048]{1,0:T(8,128)(2,1)} %q_ref.11, bf16[512,2048]{1,0:T(8,128)(2,1)} %k_ref.12, bf16[512,2048]{1,0:T(8,128)(2,1)} %u_ref.7, ...), custom_call_target="tpu_custom_call" | custom-call | bytes 7864320 | tf_op jit(solution)/shard_map/pack/pallas_call | solution.py:241
  26.0 3.4 %collective-permute-done.16.key_d = bf16[512,384]{1,0:T(8,128)(2,1)S(1)} collective-permute-done((bf16[512,384]{1,0:T(8,128)(2,1)}, bf16[512,384]{1,0:T(8,128)(2,1)S(1)}, u32[]{:S(2)}, u32[]{:S(2)}) %collective-permute-start.16) | collective-permute-done | bytes 393248 | tf_op jit(solution)/shard_map/ppermute | solution.py:257
  29.4 20.9 %collective-permute-start.2 = (bf16[512,384]{1,0:T(8,128)(2,1)}, bf16[512,384]{1,0:T(8,128)(2,1)S(1)}, u32[]{:S(2)}, u32[]{:S(2)}) collective-permute-start(bf16[512,384]{1,0:T(8,128)(2,1)} %get-tuple-element.49), channel_id=1, source_target_pairs={{0,2},{1,3},{4,6},{5,7},{8,10},{9,11},{12,14},{13,15},{16,18},{17,... | collective-permute-start | bytes 1179656 | tf_op jit(solution)/shard_map/ppermute | solution.py:257
  50.3 9.0 %collective-permute-done.2.key_c = bf16[512,384]{1,0:T(8,128)(2,1)S(1)} collective-permute-done((bf16[512,384]{1,0:T(8,128)(2,1)}, bf16[512,384]{1,0:T(8,128)(2,1)S(1)}, u32[]{:S(2)}, u32[]{:S(2)}) %collective-permute-start.2) | collective-permute-done | bytes 393248 | tf_op jit(solution)/shard_map/ppermute | solution.py:257
  60.0 8.5 %collective-permute-start = (bf16[512,1024]{1,0:T(8,128)(2,1)}, bf16[512,1024]{1,0:T(8,128)(2,1)S(1)}, u32[]{:S(2)}, u32[]{:S(2)}) collective-permute-start(bf16[512,1024]{1,0:T(8,128)(2,1)} %get-tuple-element.46), channel_id=1, source_target_pairs={{0,1},{4,5},{8,9},{12,13},{16,17},{20,21},{24,25},{28,29}} | collective-permute-start | bytes 3145736 | tf_op jit(solution)/shard_map/ppermute | solution.py:257
  70.1 7.9 %near.3 = (bf16[512,1024]{1,0:T(8,128)(2,1)S(1)}, f32[512,1024]{1,0:T(8,128)S(1)}) custom-call(s32[1]{0:T(128)} %bitcast.z_ref, s32[16,16]{1,0:T(8,128)S(1)} %copy-done.27, bf16[512,2048]{1,0:T(8,128)(2,1)} %q_ref.11, bf16[512,2048]{1,0:T(8,128)(2,1)} %k_ref.12, bf16[512,2048]{1,0:T(8,128)(2,1)} %u_ref.7, bf16[512,1024]{1,0:T(8,128)(2,1)S(1)} %collective-permute-done.13.key_all), custom_call_target="tpu_custom_call" | custom-call | flops 2147483648 | bytes 8388608 | tf_op jit(solution)/shard_map/near/pallas_call | solution.py:428
  80.7 2.9 far.3
  84.5 14.3 %collective-permute-done.3.key_d = bf16[512,384]{1,0:T(8,128)(2,1)S(1)} collective-permute-done((bf16[512,384]{1,0:T(8,128)(2,1)S(1)}, bf16[512,384]{1,0:T(8,128)(2,1)S(1)}, u32[]{:S(2)}, u32[]{:S(2)}) %collective-permute-start.3) | collective-permute-done | bytes 393248 | tf_op jit(solution)/shard_map/ppermute | solution.py:257
  103.8 4.1 %far.2 = (bf16[512,384]{1,0:T(8,128)(2,1)}, bf16[512,384]{1,0:T(8,128)(2,1)}, bf16[512,384]{1,0:T(8,128)(2,1)}, bf16[512,256]{1,0:T(8,128)(2,1)S(1)}, bf16[512,2...) custom-call(s32[1]{0:T(128)} %bitcast.z_ref, s32[16,16]{1,0:T(8,128)S(1)} %copy-done.27, ...), custom_call_target="tpu_custom_call" | custom-call | flops 4294967296 | bytes 16777216 | tf_op jit(solution)/shard_map/far/pallas_call | solution.py:540
  109.4 9.0 %near.2 = (bf16[512,1024]{1,0:T(8,128)(2,1)}, f32[512,1024]{1,0:T(8,128)S(1)}) custom-call(s32[1]{0:T(128)} %bitcast.z_ref, s32[16,16]{1,0:T(8,128)S(1)} %copy-done.27, bf16[512,2048]{1,0:T(8,128)(2,1)} %q_ref.11, bf16[512,2048]{1,0:T(8,128)(2,1)} %k_ref.12, bf16[512,2048]{1,0:T(8,128)(2,1)} %u_ref.7, bf16[512,1024]{1,0:T(8,128)(2,1)S(1)} %collective-permute-done.key_all), custom_call_target="tpu_custom_call" | custom-call | flops 2147483648 | bytes 8388608 | tf_op jit(solution)/shard_map/near/pallas_call | solution.py:428
  118.4 1.3 copy-done.5
  121.8 11.0 %collective-permute-done.25.two_c = bf16[512,256]{1,0:T(8,128)(2,1)S(1)} collective-permute-done((bf16[512,256]{1,0:T(8,128)(2,1)S(1)}, bf16[512,256]{1,0:T(8,128)(2,1)S(1)}, u32[]{:S(2)}, u32[]{:S(2)}) %collective-permute-start.25) | collective-permute-done | bytes 262176 | tf_op jit(solution)/shard_map/ppermute | solution.py:257
  138.2 9.9 %collective-permute-done.20.three_d = bf16[512,384]{1,0:T(8,128)(2,1)S(1)} collective-permute-done((bf16[512,384]{1,0:T(8,128)(2,1)S(1)}, bf16[512,384]{1,0:T(8,128)(2,1)S(1)}, u32[]{:S(2)}, u32[]{:S(2)}) %collective-permute-start.20) | collective-permute-done | bytes 393248 | tf_op jit(solution)/shard_map/ppermute | solution.py:257
  149.4 33.0 %collective-permute-done.21.three_e = bf16[512,384]{1,0:T(8,128)(2,1)S(1)} collective-permute-done((bf16[512,384]{1,0:T(8,128)(2,1)S(1)}, bf16[512,384]{1,0:T(8,128)(2,1)S(1)}, u32[]{:S(2)}, u32[]{:S(2)}) %collective-permute-start.21) | collective-permute-done | bytes 393248 | tf_op jit(solution)/shard_map/ppermute | solution.py:257
  184.5 1.4 collective-permute-start.9
  188.0 14.7 %state.1 = (bf16[16,64,128]{2,1,0:T(8,128)(2,1)}, bf16[16,8,128]{2,1,0:T(8,128)(2,1)}, bf16[512,2048]{1,0:T(8,128)(2,1)}) custom-call(bf16[512,2048]{1,0:T(8,128)(2,1)} %q_ref.15, bf16[512,2048]{1,0:T(8,128)(2,1)} %k_ref.17, bf16[512,2048]{1,0:T(8,128)(2,1)} %v_ref.9, bf16[512,32]{1,0:T(8,128)(2,1)} %copy.43.d_ref), custom_call_target="tpu_custom_call" | custom-call | flops 1073741824 | bytes 8388608 | tf_op jit(solution)/shard_map/state/pallas_call | solution.py:666
  204.6 1.6 copy-done.4
  212.6 1.5 copy-done.1
  214.7 1.5 collective-permute-done.12.two_c
  216.3 1.8 merge.2.refs_0_
  219.3 39.3 %all_to_all.10 = bf16[32,72,128]{2,1,0:T(8,128)(2,1)S(1)} all-to-all(bf16[32,72,128]{2,1,0:T(8,128)(2,1)S(1)} %maximum_maximum_fusion), channel_id=1, replica_groups=mesh['ctx'=8,'head'=4] {'ctx','head'}, dimensions={0} | all-to-all | bytes 1179648 | tf_op jit(solution)/shard_map/all_to_all | solution.py:967
  259.8 4.3 %all-to-all-start.1 = ((bf16[32,64,128]{2,1,0:T(8,128)(2,1)}), bf16[32,64,128]{2,1,0:T(8,128)(2,1)S(1)}, u32[]{:S(2)}, u32[]{:S(2)}) async-start(bf16[32,64,128]{2,1,0:T(8,128)(2,1)} %chain.1), calls=%async_computation.1 | async-start | bytes 1048576 | tf_op jit(solution)/shard_map/all_to_all | solution.py:967
  264.1 17.7 %local.3 = (f32[512,2048]{1,0:T(8,128)}, f32[512,2048]{1,0:T(8,128)}, f32[512,2048]{1,0:T(8,128)}, bf16[512,2048]{1,0:T(8,128)(2,1)}) custom-call(s32[1]{0:T(128)} %bitcast.z_ref, bf16[512,2048]{1,0:T(8,128)(2,1)} %q_ref.15, bf16[512,2048]{1,0:T(8,128)(2,1)} %k_ref.17, bf16[512,2048]{1,0:T(8,128)(2,1)} %v_ref.9, bf16[512,32]{1,0:T(8,128)(2,1)} %copy.43.d_ref, ...), custom_call_target="tpu_custom_call" | custom-call | flops 2684354560 | bytes 11534336 | tf_op jit(solution)/shard_map/local/pallas_call | solution.py:837
  281.8 10.1 %local.4 = (f32[512,2048]{1,0:T(8,128)}, f32[512,2048]{1,0:T(8,128)}, f32[512,2048]{1,0:T(8,128)}, bf16[512,2048]{1,0:T(8,128)(2,1)}) custom-call(s32[1]{0:T(128)} %bitcast.z_ref, bf16[512,2048]{1,0:T(8,128)(2,1)} %q_ref.15, bf16[512,2048]{1,0:T(8,128)(2,1)} %k_ref.17, ...), custom_call_target="tpu_custom_call", output_to_operand_aliasing={{0}: (6, {}), {1}: (7, {}), {2}: (8, {}), {3}: (9, {})} | custom-call | flops 1342177280 | bytes 5767168 | tf_op jit(solution)/shard_map/local/pallas_call | solution.py:837
  291.9 10.1 %local.5 = (f32[512,2048]{1,0:T(8,128)}, f32[512,2048]{1,0:T(8,128)}, f32[512,2048]{1,0:T(8,128)}, bf16[512,2048]{1,0:T(8,128)(2,1)}) custom-call(s32[1]{0:T(128)} %bitcast.z_ref, bf16[512,2048]{1,0:T(8,128)(2,1)} %q_ref.15, bf16[512,2048]{1,0:T(8,128)(2,1)} %k_ref.17, ...), custom_call_target="tpu_custom_call", output_to_operand_aliasing={{0}: (6, {}), {1}: (7, {}), {2}: (8, {}), {3}: (9, {})} | custom-call | flops 1342177280 | bytes 5767168 | tf_op jit(solution)/shard_map/local/pallas_call | solution.py:837
  303.4 13.0 %final.1 = (bf16[512,2048]{1,0:T(8,128)(2,1)}, bf16[512,2048]{1,0:T(8,128)(2,1)}, bf16[512,2048]{1,0:T(8,128)(2,1)}) custom-call(f32[512,2048]{1,0:T(8,128)} %get-tuple-element.82.pq_ref, f32[512,2048]{1,0:T(8,128)} %get-tuple-element.83.pk_ref, f32[512,2048]{1,0:T(8,128)} %get-tuple-element.84.pv_ref, bf16[512,2048]{1,0:T(8,128)(2,1)} %get-tuple-element.85.lit_ref, ...), custom_call_target="tpu_custom_call" | custom-call | flops 805306368 | bytes 25165824 | tf_op jit(solution)/shard_map/final/pallas_call | solution.py:892
  (121 shorter events, 39.0 us)
Async XLA Ops:
  5.1 15.8 %collective-permute-start.15 = (bf16[512,384]{1,0:T(8,128)(2,1)}, bf16[512,384]{1,0:T(8,128)(2,1)S(1)}, u32[]{:S(2)}, u32[]{:S(2)}) collective-permute-start(bf16[512,384]{1,0:T(8,128)(2,1)} %get-tuple-element.63), channel_id=1, source_target_pairs={{0,2},{1,3},{4,6},{5,7},{8,10},{9,11},{12,14},{13,15},{16,18},{17,... | collective-permute-start | bytes 1179656 | tf_op jit(solution)/shard_map/ppermute | solution.py:257
  11.1 18.3 %collective-permute-start.16 = (bf16[512,384]{1,0:T(8,128)(2,1)}, bf16[512,384]{1,0:T(8,128)(2,1)S(1)}, u32[]{:S(2)}, u32[]{:S(2)}) collective-permute-start(bf16[512,384]{1,0:T(8,128)(2,1)} %get-tuple-element.64), channel_id=1, source_target_pairs={{0,3},{1,2},{4,7},{5,6},{8,11},{9,10},{12,15},{13,14},{16,19},{17,... | collective-permute-start | bytes 1179656 | tf_op jit(solution)/shard_map/ppermute | solution.py:257
  13.3 56.1 %collective-permute-start.13 = (bf16[512,1024]{1,0:T(8,128)(2,1)}, bf16[512,1024]{1,0:T(8,128)(2,1)S(1)}, u32[]{:S(2)}, u32[]{:S(2)}) collective-permute-start(bf16[512,1024]{1,0:T(8,128)(2,1)} %get-tuple-element.60), channel_id=1, source_target_pairs={{0,1},{4,5},{8,9},{12,13},{16,17},{20,21},{24,25},{28,29}} | collective-permute-start | bytes 3145736 | tf_op jit(solution)/shard_map/ppermute | solution.py:257
  15.9 44.1 %collective-permute-start.18 = (bf16[3,512,256]{2,1,0:T(8,128)(2,1)}, bf16[3,512,256]{2,1,0:T(8,128)(2,1)S(1)}, u32[]{:S(2)}, u32[]{:S(2)}) collective-permute-start(bf16[3,512,256]{2,1,0:T(8,128)(2,1)} %get-tuple-element.65), channel_id=1, source_target_pairs={{3,1},{7,5},{11,9},{15,13},{19,17},{23,21},{27,25},{31,29}} | collective-permute-start | bytes 2359304 | tf_op jit(solution)/shard_map/ppermute | solution.py:257
  16.6 53.5 %copy-start.27 = (s32[16,16]{1,0:T(8,128)S(1)}, s32[16,16]{1,0:T(8,128)}, u32[]{:S(2)}) copy-start(s32[16,16]{1,0:T(8,128)} %flags.7) | copy-start | bytes 3076
  16.6 62.8 %collective-permute-start.14 = (bf16[3,512,384]{2,1,0:T(8,128)(2,1)}, bf16[3,512,384]{2,1,0:T(8,128)(2,1)}, u32[]{:S(2)}, u32[]{:S(2)}) collective-permute-start(bf16[3,512,384]{2,1,0:T(8,128)(2,1)} %get-tuple-element.62), channel_id=1, source_target_pairs={{3,2},{2,3},{7,6},{6,7},{11,10},{10,11},{15,14},{14,15},{19,18},{1... | collective-permute-start | bytes 3538952 | tf_op jit(solution)/shard_map/ppermute | solution.py:257
  20.9 47.6 %collective-permute-start.17 = (bf16[3,512,256]{2,1,0:T(8,128)(2,1)}, bf16[3,512,256]{2,1,0:T(8,128)(2,1)S(1)}, u32[]{:S(2)}, u32[]{:S(2)}) collective-permute-start(bf16[3,512,256]{2,1,0:T(8,128)(2,1)} %get-tuple-element.65), channel_id=1, source_target_pairs={{2,1},{6,5},{10,9},{14,13},{18,17},{22,21},{26,25},{30,29}} | collective-permute-start | bytes 2359304 | tf_op jit(solution)/shard_map/ppermute | solution.py:257
  29.4 29.9 %collective-permute-start.2 = (bf16[512,384]{1,0:T(8,128)(2,1)}, bf16[512,384]{1,0:T(8,128)(2,1)S(1)}, u32[]{:S(2)}, u32[]{:S(2)}) collective-permute-start(bf16[512,384]{1,0:T(8,128)(2,1)} %get-tuple-element.49), channel_id=1, source_target_pairs={{0,2},{1,3},{4,6},{5,7},{8,10},{9,11},{12,14},{13,15},{16,18},{17,... | collective-permute-start | bytes 1179656 | tf_op jit(solution)/shard_map/ppermute | solution.py:257
  59.3 43.6 %collective-permute-start.1 = (bf16[3,512,384]{2,1,0:T(8,128)(2,1)}, bf16[3,512,384]{2,1,0:T(8,128)(2,1)S(1)}, u32[]{:S(2)}, u32[]{:S(2)}) collective-permute-start(bf16[3,512,384]{2,1,0:T(8,128)(2,1)} %get-tuple-element.48), channel_id=1, source_target_pairs={{3,2},{2,3},{7,6},{6,7},{11,10},{10,11},{15,14},{14,15},{19,18},{1... | collective-permute-start | bytes 3538952 | tf_op jit(solution)/shard_map/ppermute | solution.py:257
  60.0 41.5 %collective-permute-start = (bf16[512,1024]{1,0:T(8,128)(2,1)}, bf16[512,1024]{1,0:T(8,128)(2,1)S(1)}, u32[]{:S(2)}, u32[]{:S(2)}) collective-permute-start(bf16[512,1024]{1,0:T(8,128)(2,1)} %get-tuple-element.46), channel_id=1, source_target_pairs={{0,1},{4,5},{8,9},{12,13},{16,17},{20,21},{24,25},{28,29}} | collective-permute-start | bytes 3145736 | tf_op jit(solution)/shard_map/ppermute | solution.py:257
  68.6 31.6 %collective-permute-start.5 = (bf16[3,512,256]{2,1,0:T(8,128)(2,1)}, bf16[3,512,256]{2,1,0:T(8,128)(2,1)S(1)}, u32[]{:S(2)}, u32[]{:S(2)}) collective-permute-start(bf16[3,512,256]{2,1,0:T(8,128)(2,1)} %get-tuple-element.51), channel_id=1, source_target_pairs={{3,1},{7,5},{11,9},{15,13},{19,17},{23,21},{27,25},{31,29}} | collective-permute-start | bytes 2359304 | tf_op jit(solution)/shard_map/ppermute | solution.py:257
  69.4 31.4 %collective-permute-start.4 = (bf16[3,512,256]{2,1,0:T(8,128)(2,1)}, bf16[3,512,256]{2,1,0:T(8,128)(2,1)S(1)}, u32[]{:S(2)}, u32[]{:S(2)}) collective-permute-start(bf16[3,512,256]{2,1,0:T(8,128)(2,1)} %get-tuple-element.51), channel_id=1, source_target_pairs={{2,1},{6,5},{10,9},{14,13},{18,17},{22,21},{26,25},{30,29}} | collective-permute-start | bytes 2359304 | tf_op jit(solution)/shard_map/ppermute | solution.py:257
  79.4 19.4 %collective-permute-start.3 = (bf16[512,384]{1,0:T(8,128)(2,1)S(1)}, bf16[512,384]{1,0:T(8,128)(2,1)S(1)}, u32[]{:S(2)}, u32[]{:S(2)}) collective-permute-start(bf16[512,384]{1,0:T(8,128)(2,1)S(1)} %copy-done.30), channel_id=1, source_target_pairs={{0,3},{1,2},{4,7},{5,6},{8,11},{9,10},{12,15},{13,14},{16,19},{17,... | collective-permute-start | bytes 1179656 | tf_op jit(solution)/shard_map/ppermute | solution.py:257
  98.8 87.1 %collective-permute-start.19 = (bf16[512,1024]{1,0:T(8,128)(2,1)S(1)}, bf16[512,1024]{1,0:T(8,128)(2,1)S(1)}, u32[]{:S(2)}, u32[]{:S(2)}) collective-permute-start(bf16[512,1024]{1,0:T(8,128)(2,1)S(1)} %get-tuple-element.67), channel_id=1, source_target_pairs={{1,0},{5,4},{9,8},{13,12},{17,16},{21,20},{25,24},{29,28}} | collective-permute-start | bytes 3145736 | tf_op jit(solution)/shard_map/ppermute | solution.py:257
  100.1 8.5 %collective-permute-start.23 = (bf16[512,256]{1,0:T(8,128)(2,1)S(1)}, bf16[512,256]{1,0:T(8,128)(2,1)S(1)}, u32[]{:S(2)}, u32[]{:S(2)}) collective-permute-start(bf16[512,256]{1,0:T(8,128)(2,1)S(1)} %get-tuple-element.71), channel_id=1, source_target_pairs={{1,2},{5,6},{9,10},{13,14},{17,18},{21,22},{25,26},{29,30}} | collective-permute-start | bytes 786440 | tf_op jit(solution)/shard_map/ppermute | solution.py:257
  100.8 18.9 %collective-permute-start.24 = (bf16[512,256]{1,0:T(8,128)(2,1)S(1)}, bf16[512,256]{1,0:T(8,128)(2,1)S(1)}, u32[]{:S(2)}, u32[]{:S(2)}) collective-permute-start(bf16[512,256]{1,0:T(8,128)(2,1)S(1)} %get-tuple-element.72), channel_id=1, source_target_pairs={{1,3},{5,7},{9,11},{13,15},{17,19},{21,23},{25,27},{29,31}} | collective-permute-start | bytes 786440 | tf_op jit(solution)/shard_map/ppermute | solution.py:257
  101.5 31.3 %collective-permute-start.25 = (bf16[512,256]{1,0:T(8,128)(2,1)S(1)}, bf16[512,256]{1,0:T(8,128)(2,1)S(1)}, u32[]{:S(2)}, u32[]{:S(2)}) collective-permute-start(bf16[512,256]{1,0:T(8,128)(2,1)S(1)} %get-tuple-element.73), channel_id=1, source_target_pairs={{1,0},{5,4},{9,8},{13,12},{17,16},{21,20},{25,24},{29,28}} | collective-permute-start | bytes 786440 | tf_op jit(solution)/shard_map/ppermute | solution.py:257
  107.9 26.9 %collective-permute-start.10 = (bf16[512,256]{1,0:T(8,128)(2,1)S(1)}, bf16[512,256]{1,0:T(8,128)(2,1)S(1)}, u32[]{:S(2)}, u32[]{:S(2)}) collective-permute-start(bf16[512,256]{1,0:T(8,128)(2,1)S(1)} %get-tuple-element.57), channel_id=1, source_target_pairs={{1,2},{5,6},{9,10},{13,14},{17,18},{21,22},{25,26},{29,30}} | collective-permute-start | bytes 786440 | tf_op jit(solution)/shard_map/ppermute | solution.py:257
  108.6 78.6 %copy-start.28 = (bf16[512,32]{0,1:T(8,128)(2,1)S(1)}, bf16[512,32]{0,1:T(8,128)(2,1)}, u32[]{:S(2)}) copy-start(bf16[512,32]{0,1:T(8,128)(2,1)} %param.14) | copy-start | bytes 98308
  108.6 28.2 %collective-permute-start.11 = (bf16[512,256]{1,0:T(8,128)(2,1)S(1)}, bf16[512,256]{1,0:T(8,128)(2,1)S(1)}, u32[]{:S(2)}, u32[]{:S(2)}) collective-permute-start(bf16[512,256]{1,0:T(8,128)(2,1)S(1)} %get-tuple-element.58), channel_id=1, source_target_pairs={{1,3},{5,7},{9,11},{13,15},{17,19},{21,23},{25,27},{29,31}} | collective-permute-start | bytes 786440 | tf_op jit(solution)/shard_map/ppermute | solution.py:257
  120.5 95.7 %collective-permute-start.6 = (bf16[512,1024]{1,0:T(8,128)(2,1)}, bf16[512,1024]{1,0:T(8,128)(2,1)S(1)}, u32[]{:S(2)}, u32[]{:S(2)}) collective-permute-start(bf16[512,1024]{1,0:T(8,128)(2,1)} %get-tuple-element.53), channel_id=1, source_target_pairs={{1,0},{5,4},{9,8},{13,12},{17,16},{21,20},{25,24},{29,28}} | collective-permute-start | bytes 3145736 | tf_op jit(solution)/shard_map/ppermute | solution.py:257
  133.5 14.6 %collective-permute-start.20 = (bf16[512,384]{1,0:T(8,128)(2,1)S(1)}, bf16[512,384]{1,0:T(8,128)(2,1)S(1)}, u32[]{:S(2)}, u32[]{:S(2)}) collective-permute-start(bf16[512,384]{1,0:T(8,128)(2,1)S(1)} %get-tuple-element.68), channel_id=1, source_target_pairs={{2,0},{3,1},{6,4},{7,5},{10,8},{11,9},{14,12},{15,13},{18,16},{19,... | collective-permute-start | bytes 1179656 | tf_op jit(solution)/shard_map/ppermute | solution.py:257
  135.5 46.9 %collective-permute-start.21 = (bf16[512,384]{1,0:T(8,128)(2,1)S(1)}, bf16[512,384]{1,0:T(8,128)(2,1)S(1)}, u32[]{:S(2)}, u32[]{:S(2)}) collective-permute-start(bf16[512,384]{1,0:T(8,128)(2,1)S(1)} %get-tuple-element.69), channel_id=1, source_target_pairs={{2,1},{3,0},{6,5},{7,4},{10,9},{11,8},{14,13},{15,12},{18,17},{19,... | collective-permute-start | bytes 1179656 | tf_op jit(solution)/shard_map/ppermute | solution.py:257
  137.5 46.2 %collective-permute-start.22 = (bf16[512,384]{1,0:T(8,128)(2,1)S(1)}, bf16[512,384]{1,0:T(8,128)(2,1)S(1)}, u32[]{:S(2)}, u32[]{:S(2)}) collective-permute-start(bf16[512,384]{1,0:T(8,128)(2,1)S(1)} %get-tuple-element.70), channel_id=1, source_target_pairs={{2,3},{3,2},{6,7},{7,6},{10,11},{11,10},{14,15},{15,14},{18,19},{1... | collective-permute-start | bytes 1179656 | tf_op jit(solution)/shard_map/ppermute | solution.py:257
  148.2 54.6 %copy-start.11 = (bf16[512,384]{1,0:T(8,128)(2,1)}, bf16[512,384]{1,0:T(8,128)(2,1)S(1)}, u32[]{:S(2)}) copy-start(bf16[512,384]{1,0:T(8,128)(2,1)S(1)} %collective-permute-done.20.three_d) | copy-start | bytes 1179652
  148.2 68.0 %collective-permute-start.7 = (bf16[512,384]{1,0:T(8,128)(2,1)}, bf16[512,384]{1,0:T(8,128)(2,1)S(1)}, u32[]{:S(2)}, u32[]{:S(2)}) collective-permute-start(bf16[512,384]{1,0:T(8,128)(2,1)} %get-tuple-element.54), channel_id=1, source_target_pairs={{2,0},{3,1},{6,4},{7,5},{10,8},{11,9},{14,12},{15,13},{18,16},{19,... | collective-permute-start | bytes 1179656 | tf_op jit(solution)/shard_map/ppermute | solution.py:257
  182.4 20.3 %copy-start.13 = (bf16[512,384]{1,0:T(8,128)(2,1)}, bf16[512,384]{1,0:T(8,128)(2,1)S(1)}, u32[]{:S(2)}) copy-start(bf16[512,384]{1,0:T(8,128)(2,1)S(1)} %collective-permute-done.21.three_e) | copy-start | bytes 1179652
  182.4 33.8 %collective-permute-start.8 = (bf16[512,384]{1,0:T(8,128)(2,1)}, bf16[512,384]{1,0:T(8,128)(2,1)}, u32[]{:S(2)}, u32[]{:S(2)}) collective-permute-start(bf16[512,384]{1,0:T(8,128)(2,1)} %get-tuple-element.55), channel_id=1, source_target_pairs={{2,1},{3,0},{6,5},{7,4},{10,9},{11,8},{14,13},{15,12},{18,17},{19,... | collective-permute-start | bytes 1179656 | tf_op jit(solution)/shard_map/ppermute | solution.py:257
  184.5 31.7 %collective-permute-start.9 = (bf16[512,384]{1,0:T(8,128)(2,1)}, bf16[512,384]{1,0:T(8,128)(2,1)}, u32[]{:S(2)}, u32[]{:S(2)}) collective-permute-start(bf16[512,384]{1,0:T(8,128)(2,1)} %get-tuple-element.56), channel_id=1, source_target_pairs={{2,3},{3,2},{6,7},{7,6},{10,11},{11,10},{14,15},{15,14},{18,19},{1... | collective-permute-start | bytes 1179656 | tf_op jit(solution)/shard_map/ppermute | solution.py:257
  185.9 30.3 %collective-permute-start.12 = (bf16[512,256]{1,0:T(8,128)(2,1)}, bf16[512,256]{1,0:T(8,128)(2,1)}, u32[]{:S(2)}, u32[]{:S(2)}) collective-permute-start(bf16[512,256]{1,0:T(8,128)(2,1)} %get-tuple-element.59), channel_id=1, source_target_pairs={{1,0},{5,4},{9,8},{13,12},{17,16},{21,20},{25,24},{29,28}} | collective-permute-start | bytes 786440 | tf_op jit(solution)/shard_map/ppermute | solution.py:257
  188.0 16.6 %copy-start.16 = (bf16[512,384]{1,0:T(8,128)(2,1)S(1)}, bf16[512,384]{1,0:T(8,128)(2,1)}, u32[]{:S(2)}) copy-start(bf16[512,384]{1,0:T(8,128)(2,1)} %copy-done.15) | copy-start | bytes 1179652
  259.8 42.1 %all-to-all-start.1 = ((bf16[32,64,128]{2,1,0:T(8,128)(2,1)}), bf16[32,64,128]{2,1,0:T(8,128)(2,1)S(1)}, u32[]{:S(2)}, u32[]{:S(2)}) async-start(bf16[32,64,128]{2,1,0:T(8,128)(2,1)} %chain.1), calls=%async_computation.1 | async-start | bytes 1048576 | tf_op jit(solution)/shard_map/all_to_all | solution.py:967
  (26 other events, 70.6 us)

commit v3 on v2

--- a/solution.py
+++ b/solution.py
@@ -202,6 +202,8 @@
 
 OWNED = ((), (0, 1), (2, 3, 4), (5, 6, 7))
 SHARE = 8
+IN_ORDER = (0, 1, 4, 5, 2, 3)
+OUT_ORDER = (5, 3, 4, 1, 0, 2)
 UNROLLS = {2: (4, 2, 1), 3: (4, 2, 1), 8: (2, 1)}
 
 
@@ -257,29 +259,37 @@
     return lax.ppermute(x, "head", routes)
 
 
+def in_turn(order, jobs):
+    results = [None] * len(jobs)
+    for n in order:
+        results[n] = send(*jobs[n])
+    return tuple(results)
+
+
 def turn_in(pieces):
     two, three, key_c, key_d, key_all = pieces
-    key_all = send(key_all, (0, 1))
-    return (
-        key_all,
-        send(three, (3, 2), (2, 3)),
-        send(key_c, (0, 2), (1, 3)),
-        send(key_d, (0, 3), (1, 2)),
-        send(two, (2, 1)),
-        send(two, (3, 1)),
+    jobs = (
+        (key_all, (0, 1)),
+        (three, (3, 2), (2, 3)),
+        (key_c, (0, 2), (1, 3)),
+        (key_d, (0, 3), (1, 2)),
+        (two, (2, 1)),
+        (two, (3, 1)),
     )
+    return in_turn(IN_ORDER, jobs)
 
 
 def turn_out(pieces):
     three_d, three_e, three_f, two_a, two_b, two_c = pieces
-    return (
-        send(three_d, (2, 0), (3, 1)),
-        send(three_e, (2, 1), (3, 0)),
-        send(three_f, (2, 3), (3, 2)),
-        send(two_a, (1, 2)),
-        send(two_b, (1, 3)),
-        send(two_c, (1, 0)),
+    jobs = (
+        (three_d, (2, 0), (3, 1)),
+        (three_e, (2, 1), (3, 0)),
+        (three_f, (2, 3), (3, 2)),
+        (two_a, (1, 2)),
+        (two_b, (1, 3)),
+        (two_c, (1, 0)),
     )
+    return in_turn(OUT_ORDER, jobs)
 
 
 def rows_of(j):
@@ -758,7 +768,7 @@
     )(items, totals)
 
 
-def local_kernel(count, first_pair, skip, olds, z_ref, q_ref, k_ref, v_ref, d_ref, *refs):
+def local_kernel(count, first_pair, skip, olds, scale, z_ref, q_ref, k_ref, v_ref, d_ref, *refs):
     lits = refs[:count]
     gq_ref, gk_ref, gv_ref, lit_ref, held = refs[count + olds :]
     take_lit(count, z_ref[0], lits, held)
@@ -803,7 +813,7 @@
         grad_query = mm(back, keys, 1, 0)
         if state is not None:
             grad_query = grad_query + entries * mm(lit, state.astype(BF), 1, 1)
-        gq_ref[at, :] = grad_query
+        gq_ref[at, :] = scale * grad_query
         grad_key = mm(back_turned, queries, 1, 0)
         grad_value = mm(mixed_turned, twice, 1, 0)
         kept.append((grad_key, grad_value, entries, leaving, decay))
@@ -819,15 +829,15 @@
             low = state.astype(BF)
             grad_key = grad_key + leaving * mm(v_ref[at, :], low, 1, 1)
             grad_value = grad_value + leaving * mm(k_ref[at, :], low, 1, 0)
-        gk_ref[at, :] = grad_key
-        gv_ref[at, :] = grad_value
+        gk_ref[at, :] = scale * grad_key
+        gv_ref[at, :] = scale * grad_value
         if b > 0:
             query = (q_ref[at, :].astype(F32) * entries).astype(BF)
             query = on_diagonal(mm(query, held[slot, at, :], 0, 0))
             state = query if state is None else decay * state + query
 
 
-def local(here, light_query, light_key, light_value, decays, lits, first, skip, many, olds):
+def local(here, light_query, light_key, light_value, decays, lits, first, skip, many, olds, scale):
     count = len(lits)
     rows, columns = light_query.shape
     width = lits[0].shape[1]
@@ -835,7 +845,7 @@
     block = pl.BlockSpec((rows, BLOCK), lambda p, z: (0, first + skip + p))
     base = 5 + count
     return pl.pallas_call(
-        functools.partial(local_kernel, count, first, skip, len(olds)),
+        functools.partial(local_kernel, count, first, skip, len(olds), scale),
         out_shape=[jax.ShapeDtypeStruct((rows, columns), F32)] * 3 + [jax.ShapeDtypeStruct((rows, columns), BF)],
         grid_spec=pltpu.PrefetchScalarGridSpec(
             num_scalar_prefetch=1,
@@ -878,9 +888,9 @@
     entries = scale * jnp.exp(-level)
     leaving = scale * jnp.exp(level - last)
     state, reach = wide_state(s_ref[...]), wide_state(r_ref[...])
-    gq_ref[...] = (scale * pq_ref[...] + entries * mm(lit_ref[...], state, 1, 1)).astype(BF)
-    gk_ref[...] = (scale * pk_ref[...] + leaving * mm(v_ref[...], reach, 1, 1)).astype(BF)
-    gv_ref[...] = (scale * pv_ref[...] + leaving * mm(k_ref[...], reach, 1, 0)).astype(BF)
+    gq_ref[...] = (pq_ref[...] + entries * mm(lit_ref[...], state, 1, 1)).astype(BF)
+    gk_ref[...] = (pk_ref[...] + leaving * mm(v_ref[...], reach, 1, 1)).astype(BF)
+    gv_ref[...] = (pv_ref[...] + leaving * mm(k_ref[...], reach, 1, 0)).astype(BF)
 
 
 def final(parts, light_key, light_value, decays, state_in, reach_in, scale):
@@ -960,7 +970,7 @@
         for n in range(len(cuts) - 1):
             parts = local(
                 here, light_query, light_key, light_value, decays, lits, first,
-                cuts[n], cuts[n + 1] - cuts[n], tuple(parts),
+                cuts[n], cuts[n + 1] - cuts[n], tuple(parts), scale,
             )
 
     def exchange(x):

time: 318 us -> 318 us (level)
  no operation moved by 1% of the time
where the time goes in v3:
time: 318 us; the launch traced here: 317 us
  Pallas kernels  103 us (32%)
  waiting for transfers between devices  84.8 us (27%)
  starting transfers between devices  66.3 us (21%)
  blocking collectives  39.3 us (12%)
  local copies, waits for them, and re-layouts  21.9 us (7%)
    ppermute x26, waiting for transfers between devices, send(): return lax.ppermute(x, 'head', routes)  84.8 us
    ppermute x26, starting transfers between devices, send(): return lax.ppermute(x, 'head', routes)  62.1 us
    all_to_all x1, blocking collectives, exchange(): return lax.all_to_all(x, AXES, split_axis=0, concat_axis=0, tiled=True)  39.3 us
    pallas_call x3, Pallas kernels, local(): pl.pallas_call(functools.partial(local_kernel, count, first, skip, len(ol...  37.9 us
    unnamed x63, local copies, waits for them, and re-layouts  18.4 us
    pallas_call x2, Pallas kernels, soft_near(): pl.pallas_call(functools.partial(near_kernel, root), out_shape=[jax.Shape...  16.9 us
    pallas_call x1, Pallas kernels, device_state(): pl.pallas_call(state_kernel, out_shape=[jax.ShapeDtypeStruct((pairs, BLOC...  14.7 us
    pallas_call x1, Pallas kernels, final(): pl.pallas_call(functools.partial(final_kernel, scale), out_shape=[jax.Sha...  13 us
  transfers between devices with their start and end apart: 27, of which 8 were waited for; matrix products, arithmetic and copies ran while one was open for 1% of the time, Pallas kernels for 26%

profile of v3, /device:TPU:0, one launch (start us, length us, event | category | flops | bytes accessed | tf_op | source)
XLA Modules:
  0.0 316.7 jit_solution(3851967909463425541)
XLA Ops:
  0.6 4.5 %pack.3 = (bf16[3,512,256]{2,1,0:T(8,128)(2,1)}, bf16[3,512,384]{2,1,0:T(8,128)(2,1)}, bf16[512,384]{1,0:T(8,128)(2,1)}, bf16[512,384]{1,0:T(8,128)(2,1)}, bf16[512,1024]{1,0:T(8,128)(2,1)}) custom-call(s32[1]{0:T(128)} %bitcast.z_ref, bf16[512,2048]{1,0:T(8,128)(2,1)} %q_ref.11, bf16[512,2048]{1,0:T(8,128)(2,1)} %k_ref.12, bf16[512,2048]{1,0:T(8,128)(2,1)} %u_ref.7, ...), custom_call_target="tpu_custom_call" | custom-call | bytes 7864320 | tf_op jit(solution)/shard_map/pack/pallas_call | solution.py:243
  5.1 6.0 %collective-permute-start.15 = (bf16[512,384]{1,0:T(8,128)(2,1)}, bf16[512,384]{1,0:T(8,128)(2,1)S(1)}, u32[]{:S(2)}, u32[]{:S(2)}) collective-permute-start(bf16[512,384]{1,0:T(8,128)(2,1)} %get-tuple-element.63), channel_id=1, source_target_pairs={{0,2},{1,3},{4,6},{5,7},{8,10},{9,11},{12,14},{13,15},{16,18},{17,... | collective-permute-start | bytes 1179656 | tf_op jit(solution)/shard_map/ppermute | solution.py:259
  11.1 2.2 collective-permute-start.16
  13.3 2.6 collective-permute-start.13
  16.6 1.7 collective-permute-start.14
  18.4 2.6 collective-permute-done.15.key_c
  21.6 4.4 %pack.2 = (bf16[3,512,256]{2,1,0:T(8,128)(2,1)}, bf16[3,512,384]{2,1,0:T(8,128)(2,1)}, bf16[512,384]{1,0:T(8,128)(2,1)}, bf16[512,384]{1,0:T(8,128)(2,1)}, bf16[512,1024]{1,0:T(8,128)(2,1)}) custom-call(s32[1]{0:T(128)} %bitcast.z_ref, bf16[512,2048]{1,0:T(8,128)(2,1)} %q_ref.11, bf16[512,2048]{1,0:T(8,128)(2,1)} %k_ref.12, bf16[512,2048]{1,0:T(8,128)(2,1)} %u_ref.7, ...), custom_call_target="tpu_custom_call" | custom-call | bytes 7864320 | tf_op jit(solution)/shard_map/pack/pallas_call | solution.py:243
  26.0 3.4 %collective-permute-done.16.key_d = bf16[512,384]{1,0:T(8,128)(2,1)S(1)} collective-permute-done((bf16[512,384]{1,0:T(8,128)(2,1)}, bf16[512,384]{1,0:T(8,128)(2,1)S(1)}, u32[]{:S(2)}, u32[]{:S(2)}) %collective-permute-start.16) | collective-permute-done | bytes 393248 | tf_op jit(solution)/shard_map/ppermute | solution.py:259
  29.4 20.9 %collective-permute-start.2 = (bf16[512,384]{1,0:T(8,128)(2,1)}, bf16[512,384]{1,0:T(8,128)(2,1)S(1)}, u32[]{:S(2)}, u32[]{:S(2)}) collective-permute-start(bf16[512,384]{1,0:T(8,128)(2,1)} %get-tuple-element.49), channel_id=1, source_target_pairs={{0,2},{1,3},{4,6},{5,7},{8,10},{9,11},{12,14},{13,15},{16,18},{17,... | collective-permute-start | bytes 1179656 | tf_op jit(solution)/shard_map/ppermute | solution.py:259
  50.3 9.0 %collective-permute-done.2.key_c = bf16[512,384]{1,0:T(8,128)(2,1)S(1)} collective-permute-done((bf16[512,384]{1,0:T(8,128)(2,1)}, bf16[512,384]{1,0:T(8,128)(2,1)S(1)}, u32[]{:S(2)}, u32[]{:S(2)}) %collective-permute-start.2) | collective-permute-done | bytes 393248 | tf_op jit(solution)/shard_map/ppermute | solution.py:259
  60.0 8.5 %collective-permute-start = (bf16[512,1024]{1,0:T(8,128)(2,1)}, bf16[512,1024]{1,0:T(8,128)(2,1)S(1)}, u32[]{:S(2)}, u32[]{:S(2)}) collective-permute-start(bf16[512,1024]{1,0:T(8,128)(2,1)} %get-tuple-element.46), channel_id=1, source_target_pairs={{0,1},{4,5},{8,9},{12,13},{16,17},{20,21},{24,25},{28,29}} | collective-permute-start | bytes 3145736 | tf_op jit(solution)/shard_map/ppermute | solution.py:259
  70.1 7.9 %near.3 = (bf16[512,1024]{1,0:T(8,128)(2,1)S(1)}, f32[512,1024]{1,0:T(8,128)S(1)}) custom-call(s32[1]{0:T(128)} %bitcast.z_ref, s32[16,16]{1,0:T(8,128)S(1)} %copy-done.27, bf16[512,2048]{1,0:T(8,128)(2,1)} %q_ref.11, bf16[512,2048]{1,0:T(8,128)(2,1)} %k_ref.12, bf16[512,2048]{1,0:T(8,128)(2,1)} %u_ref.7, bf16[512,1024]{1,0:T(8,128)(2,1)S(1)} %collective-permute-done.13.key_all), custom_call_target="tpu_custom_call" | custom-call | flops 2147483648 | bytes 8388608 | tf_op jit(solution)/shard_map/near/pallas_call | solution.py:438
  80.7 2.9 far.3
  84.5 14.3 %collective-permute-done.3.key_d = bf16[512,384]{1,0:T(8,128)(2,1)S(1)} collective-permute-done((bf16[512,384]{1,0:T(8,128)(2,1)S(1)}, bf16[512,384]{1,0:T(8,128)(2,1)S(1)}, u32[]{:S(2)}, u32[]{:S(2)}) %collective-permute-start.3) | collective-permute-done | bytes 393248 | tf_op jit(solution)/shard_map/ppermute | solution.py:259
  103.8 4.1 %far.2 = (bf16[512,384]{1,0:T(8,128)(2,1)}, bf16[512,384]{1,0:T(8,128)(2,1)}, bf16[512,384]{1,0:T(8,128)(2,1)}, bf16[512,256]{1,0:T(8,128)(2,1)S(1)}, bf16[512,2...) custom-call(s32[1]{0:T(128)} %bitcast.z_ref, s32[16,16]{1,0:T(8,128)S(1)} %copy-done.27, ...), custom_call_target="tpu_custom_call" | custom-call | flops 4294967296 | bytes 16777216 | tf_op jit(solution)/shard_map/far/pallas_call | solution.py:550
  109.4 9.0 %near.2 = (bf16[512,1024]{1,0:T(8,128)(2,1)}, f32[512,1024]{1,0:T(8,128)S(1)}) custom-call(s32[1]{0:T(128)} %bitcast.z_ref, s32[16,16]{1,0:T(8,128)S(1)} %copy-done.27, bf16[512,2048]{1,0:T(8,128)(2,1)} %q_ref.11, bf16[512,2048]{1,0:T(8,128)(2,1)} %k_ref.12, bf16[512,2048]{1,0:T(8,128)(2,1)} %u_ref.7, bf16[512,1024]{1,0:T(8,128)(2,1)S(1)} %collective-permute-done.key_all), custom_call_target="tpu_custom_call" | custom-call | flops 2147483648 | bytes 8388608 | tf_op jit(solution)/shard_map/near/pallas_call | solution.py:438
  118.4 1.3 copy-done.5
  121.8 11.0 %collective-permute-done.25.two_c = bf16[512,256]{1,0:T(8,128)(2,1)S(1)} collective-permute-done((bf16[512,256]{1,0:T(8,128)(2,1)S(1)}, bf16[512,256]{1,0:T(8,128)(2,1)S(1)}, u32[]{:S(2)}, u32[]{:S(2)}) %collective-permute-start.25) | collective-permute-done | bytes 262176 | tf_op jit(solution)/shard_map/ppermute | solution.py:259
  138.2 9.9 %collective-permute-done.20.three_d = bf16[512,384]{1,0:T(8,128)(2,1)S(1)} collective-permute-done((bf16[512,384]{1,0:T(8,128)(2,1)S(1)}, bf16[512,384]{1,0:T(8,128)(2,1)S(1)}, u32[]{:S(2)}, u32[]{:S(2)}) %collective-permute-start.20) | collective-permute-done | bytes 393248 | tf_op jit(solution)/shard_map/ppermute | solution.py:259
  149.4 33.0 %collective-permute-done.21.three_e = bf16[512,384]{1,0:T(8,128)(2,1)S(1)} collective-permute-done((bf16[512,384]{1,0:T(8,128)(2,1)S(1)}, bf16[512,384]{1,0:T(8,128)(2,1)S(1)}, u32[]{:S(2)}, u32[]{:S(2)}) %collective-permute-start.21) | collective-permute-done | bytes 393248 | tf_op jit(solution)/shard_map/ppermute | solution.py:259
  184.5 1.4 collective-permute-start.9
  188.0 14.7 %state.1 = (bf16[16,64,128]{2,1,0:T(8,128)(2,1)}, bf16[16,8,128]{2,1,0:T(8,128)(2,1)}, bf16[512,2048]{1,0:T(8,128)(2,1)}) custom-call(bf16[512,2048]{1,0:T(8,128)(2,1)} %q_ref.15, bf16[512,2048]{1,0:T(8,128)(2,1)} %k_ref.17, bf16[512,2048]{1,0:T(8,128)(2,1)} %v_ref.9, bf16[512,32]{1,0:T(8,128)(2,1)} %copy.43.d_ref), custom_call_target="tpu_custom_call" | custom-call | flops 1073741824 | bytes 8388608 | tf_op jit(solution)/shard_map/state/pallas_call | solution.py:676
  204.6 1.6 copy-done.4
  212.6 1.5 copy-done.1
  214.7 1.5 collective-permute-done.12.two_c
  216.3 1.8 merge.2.refs_0_
  219.3 39.3 %all_to_all.10 = bf16[32,72,128]{2,1,0:T(8,128)(2,1)S(1)} all-to-all(bf16[32,72,128]{2,1,0:T(8,128)(2,1)S(1)} %maximum_maximum_fusion), channel_id=1, replica_groups=mesh['ctx'=8,'head'=4] {'ctx','head'}, dimensions={0} | all-to-all | bytes 1179648 | tf_op jit(solution)/shard_map/all_to_all | solution.py:977
  259.8 4.3 %all-to-all-start.1 = ((bf16[32,64,128]{2,1,0:T(8,128)(2,1)}), bf16[32,64,128]{2,1,0:T(8,128)(2,1)S(1)}, u32[]{:S(2)}, u32[]{:S(2)}) async-start(bf16[32,64,128]{2,1,0:T(8,128)(2,1)} %chain.1), calls=%async_computation.1 | async-start | bytes 1048576 | tf_op jit(solution)/shard_map/all_to_all | solution.py:977
  264.1 17.7 %local.3 = (f32[512,2048]{1,0:T(8,128)}, f32[512,2048]{1,0:T(8,128)}, f32[512,2048]{1,0:T(8,128)}, bf16[512,2048]{1,0:T(8,128)(2,1)}) custom-call(s32[1]{0:T(128)} %bitcast.z_ref, bf16[512,2048]{1,0:T(8,128)(2,1)} %q_ref.15, bf16[512,2048]{1,0:T(8,128)(2,1)} %k_ref.17, bf16[512,2048]{1,0:T(8,128)(2,1)} %v_ref.9, bf16[512,32]{1,0:T(8,128)(2,1)} %copy.43.d_ref, ...), custom_call_target="tpu_custom_call" | custom-call | flops 2684354560 | bytes 11534336 | tf_op jit(solution)/shard_map/local/pallas_call | solution.py:847
  281.8 10.1 %local.4 = (f32[512,2048]{1,0:T(8,128)}, f32[512,2048]{1,0:T(8,128)}, f32[512,2048]{1,0:T(8,128)}, bf16[512,2048]{1,0:T(8,128)(2,1)}) custom-call(s32[1]{0:T(128)} %bitcast.z_ref, bf16[512,2048]{1,0:T(8,128)(2,1)} %q_ref.15, bf16[512,2048]{1,0:T(8,128)(2,1)} %k_ref.17, ...), custom_call_target="tpu_custom_call", output_to_operand_aliasing={{0}: (6, {}), {1}: (7, {}), {2}: (8, {}), {3}: (9, {})} | custom-call | flops 1342177280 | bytes 5767168 | tf_op jit(solution)/shard_map/local/pallas_call | solution.py:847
  291.9 10.1 %local.5 = (f32[512,2048]{1,0:T(8,128)}, f32[512,2048]{1,0:T(8,128)}, f32[512,2048]{1,0:T(8,128)}, bf16[512,2048]{1,0:T(8,128)(2,1)}) custom-call(s32[1]{0:T(128)} %bitcast.z_ref, bf16[512,2048]{1,0:T(8,128)(2,1)} %q_ref.15, bf16[512,2048]{1,0:T(8,128)(2,1)} %k_ref.17, ...), custom_call_target="tpu_custom_call", output_to_operand_aliasing={{0}: (6, {}), {1}: (7, {}), {2}: (8, {}), {3}: (9, {})} | custom-call | flops 1342177280 | bytes 5767168 | tf_op jit(solution)/shard_map/local/pallas_call | solution.py:847
  303.5 13.0 %final.1 = (bf16[512,2048]{1,0:T(8,128)(2,1)}, bf16[512,2048]{1,0:T(8,128)(2,1)}, bf16[512,2048]{1,0:T(8,128)(2,1)}) custom-call(f32[512,2048]{1,0:T(8,128)} %get-tuple-element.82.pq_ref, f32[512,2048]{1,0:T(8,128)} %get-tuple-element.83.pk_ref, f32[512,2048]{1,0:T(8,128)} %get-tuple-element.84.pv_ref, bf16[512,2048]{1,0:T(8,128)(2,1)} %get-tuple-element.85.lit_ref, ...), custom_call_target="tpu_custom_call" | custom-call | flops 805306368 | bytes 25165824 | tf_op jit(solution)/shard_map/final/pallas_call | solution.py:902
  (121 shorter events, 39.0 us)
Async XLA Ops:
  5.1 15.8 %collective-permute-start.15 = (bf16[512,384]{1,0:T(8,128)(2,1)}, bf16[512,384]{1,0:T(8,128)(2,1)S(1)}, u32[]{:S(2)}, u32[]{:S(2)}) collective-permute-start(bf16[512,384]{1,0:T(8,128)(2,1)} %get-tuple-element.63), channel_id=1, source_target_pairs={{0,2},{1,3},{4,6},{5,7},{8,10},{9,11},{12,14},{13,15},{16,18},{17,... | collective-permute-start | bytes 1179656 | tf_op jit(solution)/shard_map/ppermute | solution.py:259
  11.1 18.3 %collective-permute-start.16 = (bf16[512,384]{1,0:T(8,128)(2,1)}, bf16[512,384]{1,0:T(8,128)(2,1)S(1)}, u32[]{:S(2)}, u32[]{:S(2)}) collective-permute-start(bf16[512,384]{1,0:T(8,128)(2,1)} %get-tuple-element.64), channel_id=1, source_target_pairs={{0,3},{1,2},{4,7},{5,6},{8,11},{9,10},{12,15},{13,14},{16,19},{17,... | collective-permute-start | bytes 1179656 | tf_op jit(solution)/shard_map/ppermute | solution.py:259
  13.3 56.1 %collective-permute-start.13 = (bf16[512,1024]{1,0:T(8,128)(2,1)}, bf16[512,1024]{1,0:T(8,128)(2,1)S(1)}, u32[]{:S(2)}, u32[]{:S(2)}) collective-permute-start(bf16[512,1024]{1,0:T(8,128)(2,1)} %get-tuple-element.60), channel_id=1, source_target_pairs={{0,1},{4,5},{8,9},{12,13},{16,17},{20,21},{24,25},{28,29}} | collective-permute-start | bytes 3145736 | tf_op jit(solution)/shard_map/ppermute | solution.py:259
  15.9 44.1 %collective-permute-start.18 = (bf16[3,512,256]{2,1,0:T(8,128)(2,1)}, bf16[3,512,256]{2,1,0:T(8,128)(2,1)S(1)}, u32[]{:S(2)}, u32[]{:S(2)}) collective-permute-start(bf16[3,512,256]{2,1,0:T(8,128)(2,1)} %get-tuple-element.65), channel_id=1, source_target_pairs={{3,1},{7,5},{11,9},{15,13},{19,17},{23,21},{27,25},{31,29}} | collective-permute-start | bytes 2359304 | tf_op jit(solution)/shard_map/ppermute | solution.py:259
  16.6 53.5 %copy-start.27 = (s32[16,16]{1,0:T(8,128)S(1)}, s32[16,16]{1,0:T(8,128)}, u32[]{:S(2)}) copy-start(s32[16,16]{1,0:T(8,128)} %flags.7) | copy-start | bytes 3076
  16.6 62.8 %collective-permute-start.14 = (bf16[3,512,384]{2,1,0:T(8,128)(2,1)}, bf16[3,512,384]{2,1,0:T(8,128)(2,1)}, u32[]{:S(2)}, u32[]{:S(2)}) collective-permute-start(bf16[3,512,384]{2,1,0:T(8,128)(2,1)} %get-tuple-element.62), channel_id=1, source_target_pairs={{3,2},{2,3},{7,6},{6,7},{11,10},{10,11},{15,14},{14,15},{19,18},{1... | collective-permute-start | bytes 3538952 | tf_op jit(solution)/shard_map/ppermute | solution.py:259
  20.9 47.6 %collective-permute-start.17 = (bf16[3,512,256]{2,1,0:T(8,128)(2,1)}, bf16[3,512,256]{2,1,0:T(8,128)(2,1)S(1)}, u32[]{:S(2)}, u32[]{:S(2)}) collective-permute-start(bf16[3,512,256]{2,1,0:T(8,128)(2,1)} %get-tuple-element.65), channel_id=1, source_target_pairs={{2,1},{6,5},{10,9},{14,13},{18,17},{22,21},{26,25},{30,29}} | collective-permute-start | bytes 2359304 | tf_op jit(solution)/shard_map/ppermute | solution.py:259
  29.4 29.9 %collective-permute-start.2 = (bf16[512,384]{1,0:T(8,128)(2,1)}, bf16[512,384]{1,0:T(8,128)(2,1)S(1)}, u32[]{:S(2)}, u32[]{:S(2)}) collective-permute-start(bf16[512,384]{1,0:T(8,128)(2,1)} %get-tuple-element.49), channel_id=1, source_target_pairs={{0,2},{1,3},{4,6},{5,7},{8,10},{9,11},{12,14},{13,15},{16,18},{17,... | collective-permute-start | bytes 1179656 | tf_op jit(solution)/shard_map/ppermute | solution.py:259
  59.3 43.6 %collective-permute-start.1 = (bf16[3,512,384]{2,1,0:T(8,128)(2,1)}, bf16[3,512,384]{2,1,0:T(8,128)(2,1)S(1)}, u32[]{:S(2)}, u32[]{:S(2)}) collective-permute-start(bf16[3,512,384]{2,1,0:T(8,128)(2,1)} %get-tuple-element.48), channel_id=1, source_target_pairs={{3,2},{2,3},{7,6},{6,7},{11,10},{10,11},{15,14},{14,15},{19,18},{1... | collective-permute-start | bytes 3538952 | tf_op jit(solution)/shard_map/ppermute | solution.py:259
  60.0 41.5 %collective-permute-start = (bf16[512,1024]{1,0:T(8,128)(2,1)}, bf16[512,1024]{1,0:T(8,128)(2,1)S(1)}, u32[]{:S(2)}, u32[]{:S(2)}) collective-permute-start(bf16[512,1024]{1,0:T(8,128)(2,1)} %get-tuple-element.46), channel_id=1, source_target_pairs={{0,1},{4,5},{8,9},{12,13},{16,17},{20,21},{24,25},{28,29}} | collective-permute-start | bytes 3145736 | tf_op jit(solution)/shard_map/ppermute | solution.py:259
  68.6 31.6 %collective-permute-start.5 = (bf16[3,512,256]{2,1,0:T(8,128)(2,1)}, bf16[3,512,256]{2,1,0:T(8,128)(2,1)S(1)}, u32[]{:S(2)}, u32[]{:S(2)}) collective-permute-start(bf16[3,512,256]{2,1,0:T(8,128)(2,1)} %get-tuple-element.51), channel_id=1, source_target_pairs={{3,1},{7,5},{11,9},{15,13},{19,17},{23,21},{27,25},{31,29}} | collective-permute-start | bytes 2359304 | tf_op jit(solution)/shard_map/ppermute | solution.py:259
  69.4 31.4 %collective-permute-start.4 = (bf16[3,512,256]{2,1,0:T(8,128)(2,1)}, bf16[3,512,256]{2,1,0:T(8,128)(2,1)S(1)}, u32[]{:S(2)}, u32[]{:S(2)}) collective-permute-start(bf16[3,512,256]{2,1,0:T(8,128)(2,1)} %get-tuple-element.51), channel_id=1, source_target_pairs={{2,1},{6,5},{10,9},{14,13},{18,17},{22,21},{26,25},{30,29}} | collective-permute-start | bytes 2359304 | tf_op jit(solution)/shard_map/ppermute | solution.py:259
  79.4 19.4 %collective-permute-start.3 = (bf16[512,384]{1,0:T(8,128)(2,1)S(1)}, bf16[512,384]{1,0:T(8,128)(2,1)S(1)}, u32[]{:S(2)}, u32[]{:S(2)}) collective-permute-start(bf16[512,384]{1,0:T(8,128)(2,1)S(1)} %copy-done.30), channel_id=1, source_target_pairs={{0,3},{1,2},{4,7},{5,6},{8,11},{9,10},{12,15},{13,14},{16,19},{17,... | collective-permute-start | bytes 1179656 | tf_op jit(solution)/shard_map/ppermute | solution.py:259
  98.8 87.1 %collective-permute-start.19 = (bf16[512,1024]{1,0:T(8,128)(2,1)S(1)}, bf16[512,1024]{1,0:T(8,128)(2,1)S(1)}, u32[]{:S(2)}, u32[]{:S(2)}) collective-permute-start(bf16[512,1024]{1,0:T(8,128)(2,1)S(1)} %get-tuple-element.67), channel_id=1, source_target_pairs={{1,0},{5,4},{9,8},{13,12},{17,16},{21,20},{25,24},{29,28}} | collective-permute-start | bytes 3145736 | tf_op jit(solution)/shard_map/ppermute | solution.py:259
  100.1 8.5 %collective-permute-start.23 = (bf16[512,256]{1,0:T(8,128)(2,1)S(1)}, bf16[512,256]{1,0:T(8,128)(2,1)S(1)}, u32[]{:S(2)}, u32[]{:S(2)}) collective-permute-start(bf16[512,256]{1,0:T(8,128)(2,1)S(1)} %get-tuple-element.71), channel_id=1, source_target_pairs={{1,2},{5,6},{9,10},{13,14},{17,18},{21,22},{25,26},{29,30}} | collective-permute-start | bytes 786440 | tf_op jit(solution)/shard_map/ppermute | solution.py:259
  100.8 18.9 %collective-permute-start.24 = (bf16[512,256]{1,0:T(8,128)(2,1)S(1)}, bf16[512,256]{1,0:T(8,128)(2,1)S(1)}, u32[]{:S(2)}, u32[]{:S(2)}) collective-permute-start(bf16[512,256]{1,0:T(8,128)(2,1)S(1)} %get-tuple-element.72), channel_id=1, source_target_pairs={{1,3},{5,7},{9,11},{13,15},{17,19},{21,23},{25,27},{29,31}} | collective-permute-start | bytes 786440 | tf_op jit(solution)/shard_map/ppermute | solution.py:259
  101.5 31.3 %collective-permute-start.25 = (bf16[512,256]{1,0:T(8,128)(2,1)S(1)}, bf16[512,256]{1,0:T(8,128)(2,1)S(1)}, u32[]{:S(2)}, u32[]{:S(2)}) collective-permute-start(bf16[512,256]{1,0:T(8,128)(2,1)S(1)} %get-tuple-element.73), channel_id=1, source_target_pairs={{1,0},{5,4},{9,8},{13,12},{17,16},{21,20},{25,24},{29,28}} | collective-permute-start | bytes 786440 | tf_op jit(solution)/shard_map/ppermute | solution.py:259
  107.9 26.9 %collective-permute-start.10 = (bf16[512,256]{1,0:T(8,128)(2,1)S(1)}, bf16[512,256]{1,0:T(8,128)(2,1)S(1)}, u32[]{:S(2)}, u32[]{:S(2)}) collective-permute-start(bf16[512,256]{1,0:T(8,128)(2,1)S(1)} %get-tuple-element.57), channel_id=1, source_target_pairs={{1,2},{5,6},{9,10},{13,14},{17,18},{21,22},{25,26},{29,30}} | collective-permute-start | bytes 786440 | tf_op jit(solution)/shard_map/ppermute | solution.py:259
  108.6 78.6 %copy-start.28 = (bf16[512,32]{0,1:T(8,128)(2,1)S(1)}, bf16[512,32]{0,1:T(8,128)(2,1)}, u32[]{:S(2)}) copy-start(bf16[512,32]{0,1:T(8,128)(2,1)} %param.14) | copy-start | bytes 98308
  108.6 28.2 %collective-permute-start.11 = (bf16[512,256]{1,0:T(8,128)(2,1)S(1)}, bf16[512,256]{1,0:T(8,128)(2,1)S(1)}, u32[]{:S(2)}, u32[]{:S(2)}) collective-permute-start(bf16[512,256]{1,0:T(8,128)(2,1)S(1)} %get-tuple-element.58), channel_id=1, source_target_pairs={{1,3},{5,7},{9,11},{13,15},{17,19},{21,23},{25,27},{29,31}} | collective-permute-start | bytes 786440 | tf_op jit(solution)/shard_map/ppermute | solution.py:259
  120.5 95.7 %collective-permute-start.6 = (bf16[512,1024]{1,0:T(8,128)(2,1)}, bf16[512,1024]{1,0:T(8,128)(2,1)S(1)}, u32[]{:S(2)}, u32[]{:S(2)}) collective-permute-start(bf16[512,1024]{1,0:T(8,128)(2,1)} %get-tuple-element.53), channel_id=1, source_target_pairs={{1,0},{5,4},{9,8},{13,12},{17,16},{21,20},{25,24},{29,28}} | collective-permute-start | bytes 3145736 | tf_op jit(solution)/shard_map/ppermute | solution.py:259
  133.5 14.6 %collective-permute-start.20 = (bf16[512,384]{1,0:T(8,128)(2,1)S(1)}, bf16[512,384]{1,0:T(8,128)(2,1)S(1)}, u32[]{:S(2)}, u32[]{:S(2)}) collective-permute-start(bf16[512,384]{1,0:T(8,128)(2,1)S(1)} %get-tuple-element.68), channel_id=1, source_target_pairs={{2,0},{3,1},{6,4},{7,5},{10,8},{11,9},{14,12},{15,13},{18,16},{19,... | collective-permute-start | bytes 1179656 | tf_op jit(solution)/shard_map/ppermute | solution.py:259
  135.5 46.9 %collective-permute-start.21 = (bf16[512,384]{1,0:T(8,128)(2,1)S(1)}, bf16[512,384]{1,0:T(8,128)(2,1)S(1)}, u32[]{:S(2)}, u32[]{:S(2)}) collective-permute-start(bf16[512,384]{1,0:T(8,128)(2,1)S(1)} %get-tuple-element.69), channel_id=1, source_target_pairs={{2,1},{3,0},{6,5},{7,4},{10,9},{11,8},{14,13},{15,12},{18,17},{19,... | collective-permute-start | bytes 1179656 | tf_op jit(solution)/shard_map/ppermute | solution.py:259
  137.5 46.2 %collective-permute-start.22 = (bf16[512,384]{1,0:T(8,128)(2,1)S(1)}, bf16[512,384]{1,0:T(8,128)(2,1)S(1)}, u32[]{:S(2)}, u32[]{:S(2)}) collective-permute-start(bf16[512,384]{1,0:T(8,128)(2,1)S(1)} %get-tuple-element.70), channel_id=1, source_target_pairs={{2,3},{3,2},{6,7},{7,6},{10,11},{11,10},{14,15},{15,14},{18,19},{1... | collective-permute-start | bytes 1179656 | tf_op jit(solution)/shard_map/ppermute | solution.py:259
  148.2 54.6 %copy-start.11 = (bf16[512,384]{1,0:T(8,128)(2,1)}, bf16[512,384]{1,0:T(8,128)(2,1)S(1)}, u32[]{:S(2)}) copy-start(bf16[512,384]{1,0:T(8,128)(2,1)S(1)} %collective-permute-done.20.three_d) | copy-start | bytes 1179652
  148.2 68.0 %collective-permute-start.7 = (bf16[512,384]{1,0:T(8,128)(2,1)}, bf16[512,384]{1,0:T(8,128)(2,1)S(1)}, u32[]{:S(2)}, u32[]{:S(2)}) collective-permute-start(bf16[512,384]{1,0:T(8,128)(2,1)} %get-tuple-element.54), channel_id=1, source_target_pairs={{2,0},{3,1},{6,4},{7,5},{10,8},{11,9},{14,12},{15,13},{18,16},{19,... | collective-permute-start | bytes 1179656 | tf_op jit(solution)/shard_map/ppermute | solution.py:259
  182.4 20.3 %copy-start.13 = (bf16[512,384]{1,0:T(8,128)(2,1)}, bf16[512,384]{1,0:T(8,128)(2,1)S(1)}, u32[]{:S(2)}) copy-start(bf16[512,384]{1,0:T(8,128)(2,1)S(1)} %collective-permute-done.21.three_e) | copy-start | bytes 1179652
  182.4 33.8 %collective-permute-start.8 = (bf16[512,384]{1,0:T(8,128)(2,1)}, bf16[512,384]{1,0:T(8,128)(2,1)}, u32[]{:S(2)}, u32[]{:S(2)}) collective-permute-start(bf16[512,384]{1,0:T(8,128)(2,1)} %get-tuple-element.55), channel_id=1, source_target_pairs={{2,1},{3,0},{6,5},{7,4},{10,9},{11,8},{14,13},{15,12},{18,17},{19,... | collective-permute-start | bytes 1179656 | tf_op jit(solution)/shard_map/ppermute | solution.py:259
  184.5 31.7 %collective-permute-start.9 = (bf16[512,384]{1,0:T(8,128)(2,1)}, bf16[512,384]{1,0:T(8,128)(2,1)}, u32[]{:S(2)}, u32[]{:S(2)}) collective-permute-start(bf16[512,384]{1,0:T(8,128)(2,1)} %get-tuple-element.56), channel_id=1, source_target_pairs={{2,3},{3,2},{6,7},{7,6},{10,11},{11,10},{14,15},{15,14},{18,19},{1... | collective-permute-start | bytes 1179656 | tf_op jit(solution)/shard_map/ppermute | solution.py:259
  185.9 30.3 %collective-permute-start.12 = (bf16[512,256]{1,0:T(8,128)(2,1)}, bf16[512,256]{1,0:T(8,128)(2,1)}, u32[]{:S(2)}, u32[]{:S(2)}) collective-permute-start(bf16[512,256]{1,0:T(8,128)(2,1)} %get-tuple-element.59), channel_id=1, source_target_pairs={{1,0},{5,4},{9,8},{13,12},{17,16},{21,20},{25,24},{29,28}} | collective-permute-start | bytes 786440 | tf_op jit(solution)/shard_map/ppermute | solution.py:259
  188.0 16.6 %copy-start.16 = (bf16[512,384]{1,0:T(8,128)(2,1)S(1)}, bf16[512,384]{1,0:T(8,128)(2,1)}, u32[]{:S(2)}) copy-start(bf16[512,384]{1,0:T(8,128)(2,1)} %copy-done.15) | copy-start | bytes 1179652
  259.8 42.2 %all-to-all-start.1 = ((bf16[32,64,128]{2,1,0:T(8,128)(2,1)}), bf16[32,64,128]{2,1,0:T(8,128)(2,1)S(1)}, u32[]{:S(2)}, u32[]{:S(2)}) async-start(bf16[32,64,128]{2,1,0:T(8,128)(2,1)} %chain.1), calls=%async_computation.1 | async-start | bytes 1048576 | tf_op jit(solution)/shard_map/all_to_all | solution.py:977
  (26 other events, 70.6 us)
